TPU v7x, 32 devices: a whole 2x2x4 slice. The times are simulated.
32 devices in a mesh: vocab: 8 (over z, x), tok: 4 (over y, core).
Axes of the slice: x: 2, y: 2, z: 4, core: 2. Of those that a mesh axis runs over, the one named last changes fastest.
Arguments:
- src_embed: bfloat16 [8192, 8192], P('vocab', 'tok'), may hold values from -6 to 6
- src_head: bfloat16 [8192, 8192], P('vocab', 'tok'), may hold values from -0.25 to 0.25
- block_ids: int32 [64, 3], P('vocab'), may hold values from 0 to 63, as said below
- slot_counts: int32 [64], P('vocab'), may hold values from 1 to 3
- slot_weights: bfloat16 [64, 3, 128, 128], P('vocab'), may hold values from -0.375 to 0.375
- hidden: bfloat16 [2048, 8192], P('tok', 'vocab'), may hold values from -48 to 48
- targets: int32 [2048], P('tok'), may hold values from 0 to 8191
- byte_counts: int32 [2048], P('tok'), may hold values from 1 to 8
Outputs:
- new_embed: bfloat16 [8192, 8192], P('vocab', 'tok')
- token_bpb: float32 [2048], P('tok')
Inputs may be any that keep to these rules, and one draw needn't show every extreme that they name: `block_ids`: slot k of new block b names a source block between b - 2 and b + 2.
All inputs are finite; a program needn't handle non-finite values.
Results may differ from a plain program's by a relative error of at most 0.005.
Values may be sent and summed in bfloat16 or wider, within the bound.
No kernel may reach another device: no remote copies, remote signals or barrier semaphores. Data moves between devices by JAX's collectives and lax.ppermute only.
A program may use at most 128 MiB of HBM per device.

v0:
```python
import math

import jax
import jax.numpy as jnp
from jax import lax
from jax.sharding import PartitionSpec as P

REACH = 2


def with_halo(value, sides, width):
    for axis, dim in sides:
        count, length = (lax.axis_size(axis), value.shape[dim])
        up = [(i, (i + 1) % count) for i in range(count - 1)]
        down = [(j, i) for i, j in up]
        last = lax.slice_in_dim(value, length - width, length, axis=dim)
        leading = lax.slice_in_dim(value, 0, width, axis=dim)
        before = lax.ppermute(last, axis, up)
        after = lax.ppermute(leading, axis, down)
        value = jnp.concatenate([before, value, after], axis=dim)
    return value


def blend_rows(padded, local_ids, masked_weights, block_rows):
    columns = padded.shape[1]
    blocks = padded.reshape(-1, block_rows, columns)
    chosen = blocks[local_ids]
    summed = lax.dot_general(
        masked_weights, chosen, (((1, 3), (1, 2)), ((0,), (0,))), preferred_element_type=jnp.float32
    )
    return summed.astype(jnp.bfloat16).reshape(-1, columns)


def body(src_embed, src_head, block_ids, slot_counts, slot_weights, hidden, targets, byte_counts):
    block_rows = slot_weights.shape[2]
    slot_total = slot_weights.shape[1]
    src_rows = src_embed.shape[0]
    new_rows = slot_weights.shape[0] * block_rows
    quarter_width = src_embed.shape[1]
    vocab_index = lax.axis_index("vocab")
    both_tables = jnp.concatenate((src_embed, src_head), 1)
    padded = with_halo(both_tables, (("vocab", 0),), REACH * block_rows)
    first_block = vocab_index * (src_rows // block_rows) - REACH
    local_ids = block_ids - first_block
    live_slots = jnp.arange(slot_total, dtype=jnp.int32)[None, :] < slot_counts[:, None]
    masked_weights = jnp.where(
        live_slots[:, :, None, None], slot_weights, jnp.zeros_like(slot_weights)
    )
    blended = blend_rows(padded, local_ids, masked_weights, block_rows)
    new_embed = blended[:, :quarter_width]
    new_head = blended[:, quarter_width:]
    whole_rows = lax.all_gather(hidden, "vocab", axis=1, tiled=True)
    logits = lax.dot_general(
        whole_rows,
        lax.all_gather(new_head, "tok", axis=1, tiled=True),
        (((1,), (1,)), ((), ())),
        preferred_element_type=jnp.float32,
    )
    local_max = jnp.max(logits, axis=1)
    target_local = targets - vocab_index * new_rows
    target_mask = jnp.arange(new_rows, dtype=jnp.int32)[None, :] == target_local[:, None]
    picked = jnp.sum(jnp.where(target_mask, logits, jnp.zeros_like(logits)), axis=1)
    global_max = lax.pmax(local_max, "vocab")
    exp_sum = jnp.sum(jnp.exp(logits - global_max[:, None]), axis=1)
    total_sum, target_logit = lax.psum((exp_sum, picked), "vocab")
    log_total = global_max + jnp.log(total_sum)
    token_bpb = (log_total - target_logit) / (
        jnp.float32(math.log(2.0)) * byte_counts.astype(jnp.float32)
    )
    return (new_embed, token_bpb)


def solution(mesh):
    in_specs = (
        P("vocab", "tok"),
        P("vocab", "tok"),
        P("vocab", None),
        P("vocab"),
        P("vocab", None, None, None),
        P("tok", "vocab"),
        P("tok"),
        P("tok"),
    )
    out_specs = (P("vocab", "tok"), P("tok"))
    return jax.shard_map(body, mesh=mesh, in_specs=in_specs, out_specs=out_specs, check_vma=False)
```

profile of v0, /device:TPU:0, one launch (start us, length us, event | category | flops | bytes accessed | tf_op | source)
XLA Modules:
  0.0 363.6 jit_solution(138690657940287788)
XLA Ops:
  7.2 0.0 all-gather.5.cloned.1.call-start
  7.2 0.7 all-gather.5.cloned.1.call-update
  7.9 0.0 all-gather.3.cloned.1.call-start
  8.0 2.7 constant_dynamic-update-slice_fusion.1
  10.6 0.8 copy-done.1
  11.4 0.6 constant_dynamic-update-slice_fusion
  12.0 0.0 copy-start
  12.0 3.2 copy-done
  15.2 2.3 fusion.8
  17.5 5.0 %collective-permute-start = (bf16[256,4096]{1,0:T(8,128)(2,1)}, bf16[256,4096]{1,0:T(8,128)(2,1)S(1)}, u32[]{:S(2)}, u32[]{:S(2)}) collective-permute-start(bf16[256,4096]{1,0:T(8,128)(2,1)} %get-tuple-element.8), channel_id=1, source_target_pairs={{0,4},{4,8},{8,12},{12,16},{16,20},{20,24},{24,28},{1,5},{5,9},{9,... | collective-permute-start | bytes 6291464 | tf_op jit(solution)/shard_map/ppermute | solution.py:18
  22.5 1.3 collective-permute-start.1
  23.8 0.0 copy-done.4
  23.8 0.1 copy.11
  23.9 0.1 reshape.37
  24.0 0.1 iota_compare_fusion.1
  24.1 120.0 %collective-permute-done = bf16[256,4096]{1,0:T(8,128)(2,1)S(1)} collective-permute-done((bf16[256,4096]{1,0:T(8,128)(2,1)}, bf16[256,4096]{1,0:T(8,128)(2,1)S(1)}, u32[]{:S(2)}, u32[]{:S(2)}) %collective-permute-start) | collective-permute-done | bytes 2097184 | tf_op jit(solution)/shard_map/ppermute | solution.py:18
  144.1 0.0 collective-permute-done.1
  144.1 15.5 %pad_maximum_fusion = bf16[1536,4096]{1,0:T(8,128)(2,1)} fusion(bf16[256,4096]{1,0:T(8,128)(2,1)} %collective-permute-done.1, bf16[1024,4096]{1,0:T(8,128)(2,1)} %copy-done, bf16[256,4096]{1,0:T(8,128)(2,1)S(1)} %collective-permute-done), kind=kLoop, calls=%fused_computation.2 | loop fusion | flops 37748736 | bytes 25165824 | tf_op jit(solution)/shard_map/concatenate | solution.py:20
  159.6 14.7 %gather_fusion = bf16[24,128,4096]{2,1,0:T(8,128)(2,1)} fusion(bf16[12,128,4096]{2,1,0:T(8,128)(2,1)} %bitcast.18, s32[1024]{0:T(1024)S(1)} %pad_clamp_fusion), kind=kCustom, calls=%fused_computation | custom fusion | bytes 50331744 | tf_op jit(solution)/shard_map/gather | solution.py:27
  174.3 0.0 copy-done.2
  174.3 10.6 %bitcast_convert_fusion = bf16[8,128,4096]{2,1,0:T(8,128)(2,1)S(1)} fusion(bf16[8,3,128,4096]{3,2,1,0:T(8,128)(2,1)} %bitcast.19, bf16[8,3,128,128]{3,2,1,0:T(8,128)(2,1)S(1)} %copy-done.2, pred[8,3]{1,0:T(8,128)(4,1)S(1)} %iota_compare_fusion.1), kind=kOutput, calls=%fused_computation.1 | convolution fusion | flops 3225812992 | bytes 34340888 | tf_op jit(solution)/shard_map/dot_general | solution.py:28
  184.9 0.0 copy-start.5
  184.9 3.9 %fusion.7 = (bf16[1024,2048]{1,0:T(8,128)(2,1)}, bf16[1024,2048]{1,0:T(8,128)(2,1)}) fusion(bf16[1024,4096]{1,0:T(8,128)(2,1)S(1)} %bitcast.20), kind=kLoop, calls=%fused_computation.20 | loop fusion | bytes 16777216 | tf_op jit(solution)/shard_map/slice | solution.py:51
  188.8 0.0 all-gather.3.cloned.1.call-update
  188.9 0.0 copy-start.3
  188.9 8.0 %all-gather.5.cloned.1.call-done = bf16[512,8192]{1,0:T(8,128)(2,1)} async-done(((bf16[512,1024]{1,0:T(8,128)(2,1)}), bf16[512,8192]{1,0:T(8,128)(2,1)}) %all-gather.5.cloned.1.call-update) | async-done | bytes 8388624 | tf_op jit(solution)/shard_map/all_gather | solution.py:52
  196.9 105.7 %all-gather.3.cloned.1.call-done = bf16[1024,8192]{1,0:T(8,128)(2,1)} async-done(((bf16[1024,2048]{1,0:T(8,128)(2,1)}), bf16[1024,8192]{1,0:T(8,128)(2,1)}) %all-gather.3.cloned.1.call-update) | async-done | bytes 16777232 | tf_op jit(solution)/shard_map/all_gather | solution.py:55
  302.6 14.5 %fusion.9 = (f32[512]{0:T(512)S(1)}, f32[1024,512]{1,0:T(8,128)S(1)}) fusion(bf16[1024,8192]{1,0:T(8,128)(2,1)} %all-gather.3.cloned.1.call-done, bf16[512,8192]{1,0:T(8,128)(2,1)} %all-gather.5.cloned.1.call-done), kind=kOutput, calls=%fused_computation.22 | convolution fusion | flops 8590458880 | bytes 27265024 | tf_op jit(solution)/shard_map/dot_general | solution.py:53
  317.1 21.4 %pmax.7 = f32[512]{0:T(512)S(1)} all-reduce(f32[512]{0:T(512)S(1)} %get-tuple-element.10), channel_id=1, replica_groups=mesh['vocab'=8,'tok'=4] {'vocab'}, use_global_device_ids=true, to_apply=%region_1.2 | all-reduce | flops 512 | bytes 4096 | tf_op jit(solution)/shard_map/pmax | solution.py:63
  338.5 0.6 fusion.1
  339.1 17.1 %all-reduce = (f32[512]{0:T(512)S(1)}, f32[512]{0:T(512)S(1)}) all-reduce(f32[512]{0:T(512)S(1)} %get-tuple-element.3, f32[512]{0:T(512)S(1)} %get-tuple-element.2), channel_id=1, replica_groups=mesh['vocab'=8,'tok'=4] {'vocab'}, use_global_device_ids=true, to_apply=%region_5.6 | all-reduce | flops 1024 | bytes 8192 | tf_op jit(solution)/shard_map/psum | solution.py:65
  356.2 0.6 multiply_divide_fusion
  (10 shorter events, 0.0 us)
Async XLA Ops:
  7.2 189.8 %all-gather.5.cloned.1.call-start = ((), (), s32[]{:S(2)}) async-start(), calls=%async_computation.1 | async-start | bytes 9437184 | tf_op jit(solution)/shard_map/all_gather | solution.py:52
  7.9 294.7 %all-gather.3.cloned.1.call-start = ((), (), s32[]{:S(2)}) async-start(), calls=%async_computation | async-start | bytes 20971520 | tf_op jit(solution)/shard_map/all_gather | solution.py:55
  7.9 3.5 copy-start.1
  11.4 12.4 %copy-start.4 = (s32[8,3]{0,1:T(4,128)S(1)}, s32[8,3]{0,1:T(4,128)}, u32[]{:S(2)}) copy-start(s32[8,3]{0,1:T(4,128)} %param.10) | copy-start | bytes 292
  11.4 12.6 %copy-start.6 = (s32[8]{0:T(128)S(1)}, s32[8]{0:T(128)}, u32[]{:S(2)}) copy-start(s32[8]{0:T(128)} %param.11) | copy-start | bytes 100
  12.0 3.2 copy-start
  17.5 126.6 %collective-permute-start = (bf16[256,4096]{1,0:T(8,128)(2,1)}, bf16[256,4096]{1,0:T(8,128)(2,1)S(1)}, u32[]{:S(2)}, u32[]{:S(2)}) collective-permute-start(bf16[256,4096]{1,0:T(8,128)(2,1)} %get-tuple-element.8), channel_id=1, source_target_pairs={{0,4},{4,8},{8,12},{12,16},{16,20},{20,24},{24,28},{1,5},{5,9},{9,... | collective-permute-start | bytes 6291464 | tf_op jit(solution)/shard_map/ppermute | solution.py:18
  22.5 121.6 %collective-permute-start.1 = (bf16[256,4096]{1,0:T(8,128)(2,1)}, bf16[256,4096]{1,0:T(8,128)(2,1)}, u32[]{:S(2)}, u32[]{:S(2)}) collective-permute-start(bf16[256,4096]{1,0:T(8,128)(2,1)} %get-tuple-element.9), channel_id=1, source_target_pairs={{4,0},{8,4},{12,8},{16,12},{20,16},{24,20},{28,24},{5,1},{9,5},{13... | collective-permute-start | bytes 6291464 | tf_op jit(solution)/shard_map/ppermute | solution.py:19
  159.6 14.7 %copy-start.2 = (bf16[8,3,128,128]{3,2,1,0:T(8,128)(2,1)S(1)}, bf16[8,3,128,128]{3,2,1,0:T(8,128)(2,1)}, u32[]{:S(2)}) copy-start(bf16[8,3,128,128]{3,2,1,0:T(8,128)(2,1)} %param.12) | copy-start | bytes 2359300
  184.9 3.9 %copy-start.5 = (s32[512]{0:T(512)S(1)}, s32[512]{0:T(512)}, u32[]{:S(2)}) copy-start(s32[512]{0:T(512)} %param.14) | copy-start | bytes 6148
  188.9 167.3 %copy-start.3 = (s32[512]{0:T(512)S(1)}, s32[512]{0:T(512)}, u32[]{:S(2)}) copy-start(s32[512]{0:T(512)} %param.15) | copy-start | bytes 6148
Sparse Core Ops, SparseCore 0:
  10.2 186.6 all-gather.4
  198.5 104.1 all-gather.2
where the time goes:
time: 364 us
  waiting for transfers between devices  234 us (64%)
  blocking collectives  38.5 us (11%)
  local copies, waits for them, and re-layouts  28.3 us (8%)
  matrix products  25 us (7%)
  other arithmetic  16.8 us (5%)
  between operations  14.2 us (4%)
  starting transfers between devices  6.33 us (2%)
    ppermute x1, waiting for transfers between devices, with_halo(): before = lax.ppermute(last, axis, up)  120 us
    all_gather x1, waiting for transfers between devices, body(): lax.all_gather(new_head, 'tok', axis=1, tiled=True)  106 us
    pmax x1, blocking collectives, body(): global_max = lax.pmax(local_max, 'vocab')  21.4 us
    psum x1, blocking collectives, body(): total_sum, target_logit = lax.psum((exp_sum, picked), 'vocab')  17.1 us
    concatenate x1, other arithmetic, with_halo(): value = jnp.concatenate([before, value, after], axis=dim)  15.5 us
    gather x1, local copies, waits for them, and re-layouts, blend_rows(): chosen = blocks[local_ids]  14.7 us
    dot_general x1, matrix products, body(): lax.dot_general(whole_rows, lax.all_gather(new_head, 'tok', axis=1, tiled...  14.5 us
    dot_general x1, matrix products, blend_rows(): lax.dot_general(masked_weights, chosen, (((1, 3), (1, 2)), ((0,), (0,))),...  10.6 us
  transfers between devices with their start and end apart: 4, of which 3 were waited for; matrix products, arithmetic and copies ran while one was open for 14% of the time, Pallas kernels for 0%

commit v1 on v0

v1 whole, which is shorter than its diff:
```python
import functools
import math

import jax
import jax.numpy as jnp
from jax import lax
from jax.experimental import pallas as pl
from jax.experimental.pallas import tpu as pltpu
from jax.sharding import PartitionSpec as P

REACH = 2


def xor_perm(count, mask):
    return [(i, i ^ mask) for i in range(count)]


def masked(weights, slot, amount):
    return jnp.where(slot < amount, weights, jnp.zeros_like(weights))


def fill_padded(padded, before_ref, own_ref, after_ref):
    edge, rows = before_ref.shape[0], own_ref.shape[0]
    padded[pl.ds(0, edge), :] = before_ref[...]
    padded[pl.ds(edge, rows), :] = own_ref[...]
    padded[pl.ds(edge + rows, edge), :] = after_ref[...]


def blend_block(ids_ref, counts_ref, weights_ref, padded, block):
    slots, rows = weights_ref.shape[1], weights_ref.shape[2]
    total = None
    for slot in range(slots):
        start = pl.multiple_of(ids_ref[block, slot] * rows, rows)
        part = jnp.dot(
            masked(weights_ref[block, slot], slot, counts_ref[block]),
            padded[pl.ds(start, rows), :],
            preferred_element_type=jnp.float32,
        )
        total = part if total is None else total + part
    return total


def table_kernel(ids_ref, counts_ref, weights_ref, before_ref, own_ref, after_ref, out_ref, padded):
    fill_padded(padded, before_ref, own_ref, after_ref)
    blocks, rows = weights_ref.shape[0], weights_ref.shape[2]
    for block in range(blocks):
        summed = blend_block(ids_ref, counts_ref, weights_ref, padded, block)
        out_ref[pl.ds(block * rows, rows), :] = summed.astype(out_ref.dtype)


def blend_table(ids, counts, weights, before, own, after, tile=512):
    rows, columns = own.shape
    edge = before.shape[0]
    tile = math.gcd(tile, columns)
    smem = pl.BlockSpec(memory_space=pltpu.SMEM)
    return pl.pallas_call(
        table_kernel,
        grid=(columns // tile,),
        out_shape=jax.ShapeDtypeStruct((weights.shape[0] * weights.shape[2], columns), own.dtype),
        in_specs=[
            smem,
            smem,
            pl.BlockSpec(weights.shape, lambda i: (0, 0, 0, 0)),
            pl.BlockSpec((edge, tile), lambda i: (0, i)),
            pl.BlockSpec((rows, tile), lambda i: (0, i)),
            pl.BlockSpec((edge, tile), lambda i: (0, i)),
        ],
        out_specs=pl.BlockSpec((weights.shape[0] * weights.shape[2], tile), lambda i: (0, i)),
        scratch_shapes=[pltpu.VMEM((rows + 2 * edge, tile), own.dtype)],
        compiler_params=pltpu.CompilerParams(vmem_limit_bytes=32 << 20),
        cost_estimate=pl.CostEstimate(
            flops=2 * weights.size * columns,
            bytes_accessed=2 * (2 * rows + 2 * edge) * columns + 2 * weights.size,
            transcendentals=0,
        ),
        name="blend_table",
    )(ids, counts, weights, before, own, after)


def stats_kernel(ids_ref, counts_ref, weights_ref, before_ref, own_ref, after_ref, goals_ref, out_ref, padded, logits):
    fill_padded(padded, before_ref, own_ref, after_ref)
    blocks, rows = weights_ref.shape[0], weights_ref.shape[2]
    tokens = own_ref.shape[1]
    goals = goals_ref[...]
    peak = jnp.full((1, tokens), -jnp.inf, jnp.float32)
    picked = jnp.zeros((1, tokens), jnp.float32)
    for block in range(blocks):
        summed = blend_block(ids_ref, counts_ref, weights_ref, padded, block)
        logits[pl.ds(block * rows, rows), :] = summed
        peak = jnp.maximum(peak, jnp.max(summed, axis=0, keepdims=True))
        row_ids = lax.broadcasted_iota(jnp.int32, summed.shape, 0) + block * rows
        picked = picked + jnp.sum(jnp.where(row_ids == goals, summed, 0.0), axis=0, keepdims=True)
    total = jnp.zeros((1, tokens), jnp.float32)
    for block in range(blocks):
        values = jnp.exp(logits[pl.ds(block * rows, rows), :] - peak)
        total = total + jnp.sum(values, axis=0, keepdims=True)
    out_ref[0:1, :] = peak
    out_ref[1:2, :] = total
    out_ref[2:3, :] = picked


def local_stats(ids, counts, weights, before, own, after, goals):
    rows, tokens = own.shape
    edge = before.shape[0]
    smem = pl.BlockSpec(memory_space=pltpu.SMEM)
    vmem = pl.BlockSpec(memory_space=pltpu.VMEM)
    new_rows = weights.shape[0] * weights.shape[2]
    return pl.pallas_call(
        stats_kernel,
        out_shape=jax.ShapeDtypeStruct((3, tokens), jnp.float32),
        in_specs=[smem, smem, vmem, vmem, vmem, vmem, vmem],
        out_specs=vmem,
        scratch_shapes=[
            pltpu.VMEM((rows + 2 * edge, tokens), own.dtype),
            pltpu.VMEM((new_rows, tokens), jnp.float32),
        ],
        compiler_params=pltpu.CompilerParams(vmem_limit_bytes=32 << 20),
        cost_estimate=pl.CostEstimate(
            flops=2 * weights.size * tokens, bytes_accessed=4 * rows * tokens, transcendentals=new_rows * tokens
        ),
        name="blend_stats",
    )(ids, counts, weights, before, own, after, goals)


def edges(value, axis, width):
    count, length = lax.axis_size(axis), value.shape[0]
    up = [(i, i + 1) for i in range(count - 1)]
    down = [(j, i) for i, j in up]
    before = lax.ppermute(lax.slice_in_dim(value, length - width, length, axis=0), axis, up)
    after = lax.ppermute(lax.slice_in_dim(value, 0, width, axis=0), axis, down)
    return before, after


def merge_stats(stats, axis):
    count = lax.axis_size(axis)
    index = lax.axis_index(axis)
    mask = 1
    while mask < count:
        other = lax.ppermute(stats, axis, xor_perm(count, mask))
        upper = (index & mask) != 0
        first = jnp.where(upper, other, stats)
        second = jnp.where(upper, stats, other)
        peak = jnp.maximum(first[0], second[0])
        total = first[1] * jnp.exp(first[0] - peak) + second[1] * jnp.exp(second[0] - peak)
        stats = jnp.stack([peak, total, first[2] + second[2]])
        mask *= 2
    return stats


def body(src_embed, src_head, block_ids, slot_counts, slot_weights, hidden, targets, byte_counts):
    block_rows = slot_weights.shape[2]
    rows, quarter = src_embed.shape
    new_rows = slot_weights.shape[0] * block_rows
    vocab_index = lax.axis_index("vocab")
    tok_index = lax.axis_index("tok")
    tok_count = lax.axis_size("tok")
    halo = REACH * block_rows
    last_local = rows // block_rows + 2 * REACH - 1
    local_ids = jnp.clip(block_ids - (vocab_index * (rows // block_rows) - REACH), 0, last_local)

    whole_rows = lax.all_gather(hidden, "vocab", axis=1, tiled=True)
    pieces = {0: src_head}
    mask = tok_count // 2
    while mask >= 1:
        for held in list(pieces):
            pieces[held | mask] = lax.ppermute(pieces[held], "tok", xor_perm(tok_count, mask))
        mask //= 2

    source_logits = None
    for held, piece in pieces.items():
        columns = lax.dynamic_slice_in_dim(whole_rows, (tok_index ^ held) * quarter, quarter, axis=1)
        part = lax.dot_general(piece, columns, (((1,), (1,)), ((), ())), preferred_element_type=jnp.float32)
        source_logits = part if source_logits is None else source_logits + part
    source_logits = source_logits.astype(jnp.bfloat16)
    before, after = edges(source_logits, "vocab", halo)
    goals = (targets - vocab_index * new_rows)[None, :]
    stats = local_stats(local_ids, slot_counts, slot_weights, before, source_logits, after, goals)
    stats = merge_stats(stats, "vocab")
    log_total = stats[0] + jnp.log(stats[1])
    token_bpb = (log_total - stats[2]) / (jnp.float32(math.log(2.0)) * byte_counts.astype(jnp.float32))

    before, after = edges(src_embed, "vocab", halo)
    new_embed = blend_table(local_ids, slot_counts, slot_weights, before, src_embed, after)
    return (new_embed, token_bpb)


def solution(mesh):
    in_specs = (
        P("vocab", "tok"),
        P("vocab", "tok"),
        P("vocab", None),
        P("vocab"),
        P("vocab", None, None, None),
        P("tok", "vocab"),
        P("tok"),
        P("tok"),
    )
    out_specs = (P("vocab", "tok"), P("tok"))
    return jax.shard_map(body, mesh=mesh, in_specs=in_specs, out_specs=out_specs, check_vma=False)
```

time: 364 us -> 242 us (0.66)
  waiting for transfers between devices: 234 us -> 173 us
  blocking collectives: 38.5 us -> 0 us
  local copies, waits for them, and re-layouts: 28.3 us -> 6.56 us
  other arithmetic: 16.8 us -> 0.73 us
  starting transfers between devices: 6.33 us -> 19.3 us
  Pallas kernels: 0 us -> 8.32 us
  matrix products: 25 us -> 17 us
    all_gather x1 -> x0, waiting for transfers between devices: 106 us -> none  [body(): lax.all_gather(new_head, 'tok', axis=1, tiled=True)]
    all_gather x1, waiting for transfers between devices: 8.04 us -> 36 us  [body(): whole_rows = lax.all_gather(hidden, 'vocab', axis=1, tiled=True)]
    pmax x1 -> x0, blocking collectives: 21.4 us -> none  [body(): global_max = lax.pmax(local_max, 'vocab')]
    psum x1 -> x0, blocking collectives: 17.1 us -> none  [body(): total_sum, target_logit = lax.psum((exp_sum, picked), 'vocab')]
    ppermute x2 -> x10, waiting for transfers between devices: 120 us -> 136 us  [the longest x3 90.9 us: body(): lax.ppermute(pieces[held], 'tok', xor_perm(tok_count, mask))]
    concatenate x1 -> x0, other arithmetic: 15.5 us -> none  [with_halo(): value = jnp.concatenate([before, value, after], axis=dim)]
    gather x1 -> x0, local copies, waits for them, and re-layouts: 14.7 us -> none  [blend_rows(): chosen = blocks[local_ids]]
    ppermute x2 -> x10, starting transfers between devices: 6.26 us -> 19.2 us  [the longest x3 9.17 us: merge_stats(): other = lax.ppermute(stats, axis, xor_perm(count, mask))]
  transfers between devices with their start and end apart: 4 -> 11, of which waited for: 3 -> 5; matrix products, arithmetic and copies ran while one was open for 14% -> 7% of each run, Pallas kernels for 0% -> 3%
where the time goes in v1:
time: 242 us; the launch traced here: 239 us
  waiting for transfers between devices  173 us (71%)
  starting transfers between devices  19.3 us (8%)
  matrix products  17 us (7%)
  between operations  14.3 us (6%)
  Pallas kernels  8.32 us (3%)
  local copies, waits for them, and re-layouts  6.56 us (3%)
    ppermute x3, waiting for transfers between devices, body(): lax.ppermute(pieces[held], 'tok', xor_perm(tok_count, mask))  90.9 us
    all_gather x1, waiting for transfers between devices, body(): whole_rows = lax.all_gather(hidden, 'vocab', axis=1, tiled=True)  36 us
    ppermute x3, waiting for transfers between devices, merge_stats(): other = lax.ppermute(stats, axis, xor_perm(count, mask))  23 us
    ppermute x2, waiting for transfers between devices, edges(): lax.ppermute(lax.slice_in_dim(value, length - width, length, axis=0), axi...  22 us
    dot_general x4, matrix products, body(): lax.dot_general(piece, columns, (((1,), (1,)), ((), ())), preferred_eleme...  17 us
    ppermute x3, starting transfers between devices, merge_stats(): other = lax.ppermute(stats, axis, xor_perm(count, mask))  9.17 us
    pallas_call x1, Pallas kernels, blend_table(): pl.pallas_call(table_kernel, grid=(columns // tile,), out_shape=jax.Shape...  6.29 us
  transfers between devices with their start and end apart: 11, of which 5 were waited for; matrix products, arithmetic and copies ran while one was open for 7% of the time, Pallas kernels for 3%

profile of v1, /device:TPU:0, one launch (start us, length us, event | category | flops | bytes accessed | tf_op | source)
XLA Modules:
  0.0 238.8 jit_solution(6312558596128261255)
XLA Ops:
  7.2 0.0 all-gather.2.cloned.1.call-start
  7.2 0.7 all-gather.2.cloned.1.call-update
  7.9 3.0 %collective-permute-start.2 = (bf16[1024,2048]{1,0:T(8,128)(2,1)}, bf16[1024,2048]{1,0:T(8,128)(2,1)}, u32[]{:S(2)}, u32[]{:S(2)}) collective-permute-start(bf16[1024,2048]{1,0:T(8,128)(2,1)} %param.9), channel_id=1, source_target_pairs={{0,2},{1,3},{2,0},{3,1},{4,6},{5,7},{6,4},{7,5},{8,10},{9,11},{10,... | collective-permute-start | bytes 12582920 | tf_op jit(solution)/shard_map/ppermute | solution.py:166
  10.9 0.0 collective-permute-start.3
  10.9 90.9 %collective-permute-done.2 = bf16[1024,2048]{1,0:T(8,128)(2,1)} collective-permute-done((bf16[1024,2048]{1,0:T(8,128)(2,1)}, bf16[1024,2048]{1,0:T(8,128)(2,1)}, u32[]{:S(2)}, u32[]{:S(2)}) %collective-permute-start.2) | collective-permute-done | bytes 4194336 | tf_op jit(solution)/shard_map/ppermute | solution.py:166
  101.8 36.0 %all-gather.2.cloned.1.call-done = bf16[512,8192]{1,0:T(8,128)(2,1)} async-done(((bf16[512,1024]{1,0:T(8,128)(2,1)}), bf16[512,8192]{1,0:T(8,128)(2,1)}) %all-gather.2.cloned.1.call-update) | async-done | bytes 8388624 | tf_op jit(solution)/shard_map/all_gather | solution.py:161
  137.8 5.3 %fusion.4 = f32[512,1024]{0,1:T(8,128)S(1)} fusion(bf16[1024,2048]{1,0:T(8,128)(2,1)} %collective-permute-done.2, bf16[512,8192]{1,0:T(8,128)(2,1)} %all-gather.2.cloned.1.call-done, s32[]{:T(128)S(6)} %select_n.48), kind=kOutput, calls=%fused_computation.5 | convolution fusion | flops 2147483648 | bytes 8388612 | tf_op jit(solution)/shard_map/dot_general | solution.py:172
  143.2 1.1 copy-done.7
  144.2 2.4 fusion.6
  146.6 4.6 %fusion.2 = f32[512,1024]{0,1:T(8,128)S(1)} fusion(bf16[1024,2048]{1,0:T(8,128)(2,1)} %collective-permute-done.3, bf16[512,8192]{1,0:T(8,128)(2,1)S(1)} %copy-done.6, s32[]{:T(128)S(6)} %select_n.49), kind=kOutput, calls=%fused_computation.3 | convolution fusion | flops 2147483648 | bytes 8388612 | tf_op jit(solution)/shard_map/dot_general | solution.py:172
  151.2 0.0 copy-start.5
  151.2 0.0 copy-start.3
  151.2 0.0 copy-start.1
  151.3 0.0 copy-start.2
  151.3 4.7 %fusion.10.own_ref = bf16[1024,512]{1,0:T(8,128)(2,1)S(1)} fusion(bf16[1024,2048]{1,0:T(8,128)(2,1)} %collective-permute-done.4, bf16[512,8192]{1,0:T(8,128)(2,1)S(1)} %copy-done.6, s32[]{:T(128)S(6)} %select_n.50, f32[512,1024]{0,1:T(8,128)S(1)} %fusion.2, f32[512,1024]{0,1:T(8,128)S(1)} %fusion.6, f32[512,1024]{0,1:T(8,128)S(1)} %fusion.4), kind=kOutput, calls=%fused_computation.9 | convolution fusion | flops 2149580800 | bytes 13631492 | tf_op jit(solution)/shard_map/dot_general | solution.py:172
  156.1 2.5 %collective-permute-start.5 = (bf16[256,512]{1,0:T(8,128)(2,1)S(1)}, bf16[256,512]{1,0:T(8,128)(2,1)S(1)}, u32[]{:S(2)}, u32[]{:S(2)}) collective-permute-start(bf16[256,512]{1,0:T(8,128)(2,1)S(1)} %get-tuple-element.9), channel_id=1, source_target_pairs={{0,4},{4,8},{8,12},{12,16},{16,20},{20,24},{24,28},{1,5},{5,9},{9,... | collective-permute-start | bytes 786440 | tf_op jit(solution)/shard_map/ppermute | solution.py:129
  158.5 1.3 collective-permute-start.6
  159.9 0.1 copy.10
  160.0 9.3 %collective-permute-done.5.before_ref = bf16[256,512]{1,0:T(8,128)(2,1)S(1)} collective-permute-done((bf16[256,512]{1,0:T(8,128)(2,1)S(1)}, bf16[256,512]{1,0:T(8,128)(2,1)S(1)}, u32[]{:S(2)}, u32[]{:S(2)}) %collective-permute-start.5) | collective-permute-done | bytes 262176 | tf_op jit(solution)/shard_map/ppermute | solution.py:129
  169.3 2.0 blend_stats.1
  171.3 2.6 %collective-permute-start.7 = (f32[3,512]{1,0:T(4,128)S(1)}, f32[3,512]{1,0:T(4,128)S(1)}, u32[]{:S(2)}, u32[]{:S(2)}) collective-permute-start(f32[3,512]{1,0:T(4,128)S(1)} %blend_stats.1), channel_id=1, source_target_pairs={{0,4},{4,0},{8,12},{12,8},{16,20},{20,16},{24,28},{28,24},{1,5},{5... | collective-permute-start | bytes 18440 | tf_op jit(solution)/shard_map/ppermute | solution.py:139
  173.9 3.1 %fusion.21 = (bf16[256,2048]{1,0:T(8,128)(2,1)}, bf16[256,2048]{1,0:T(8,128)(2,1)}) fusion(bf16[1024,2048]{1,0:T(8,128)(2,1)} %own_ref.1), kind=kLoop, calls=%fused_computation.39 | loop fusion | bytes 4194304 | tf_op jit(solution)/shard_map/slice | solution.py:130
  177.0 2.0 collective-permute-start
  179.0 1.3 collective-permute-start.1
  180.4 3.5 %collective-permute-start.8 = (f32[3,512]{1,0:T(4,128)S(1)}, f32[3,512]{1,0:T(4,128)S(1)}, u32[]{:S(2)}, u32[]{:S(2)}) collective-permute-start(f32[3,512]{1,0:T(4,128)S(1)} %pad_maximum_fusion), channel_id=1, source_target_pairs={{0,8},{4,12},{8,0},{12,4},{16,24},{20,28},{24,16},{28,20},{1,9},{5... | collective-permute-start | bytes 18440 | tf_op jit(solution)/shard_map/ppermute | solution.py:139
  183.9 23.0 %collective-permute-done.8 = f32[3,512]{1,0:T(4,128)S(1)} collective-permute-done((f32[3,512]{1,0:T(4,128)S(1)}, f32[3,512]{1,0:T(4,128)S(1)}, u32[]{:S(2)}, u32[]{:S(2)}) %collective-permute-start.8) | collective-permute-done | bytes 6176 | tf_op jit(solution)/shard_map/ppermute | solution.py:139
  207.0 0.0 copy-start.4
  207.0 3.1 %collective-permute-start.9 = (f32[3,512]{1,0:T(4,128)S(1)}, f32[3,512]{1,0:T(4,128)S(1)}, u32[]{:S(2)}, u32[]{:S(2)}) collective-permute-start(f32[3,512]{1,0:T(4,128)S(1)} %pad_maximum_fusion.1), channel_id=1, source_target_pairs={{0,16},{4,20},{8,24},{12,28},{16,0},{20,4},{24,8},{28,12},{1,17},{... | collective-permute-start | bytes 18440 | tf_op jit(solution)/shard_map/ppermute | solution.py:139
  210.1 12.7 %collective-permute-done.before_ref = bf16[256,2048]{1,0:T(8,128)(2,1)S(1)} collective-permute-done((bf16[256,2048]{1,0:T(8,128)(2,1)}, bf16[256,2048]{1,0:T(8,128)(2,1)S(1)}, u32[]{:S(2)}, u32[]{:S(2)}) %collective-permute-start) | collective-permute-done | bytes 1048608 | tf_op jit(solution)/shard_map/ppermute | solution.py:129
  222.8 2.2 copy-done
  225.0 6.3 %blend_table.1 = bf16[1024,2048]{1,0:T(8,128)(2,1)} custom-call(s32[8,3]{1,0:T(8,128)S(1)} %subtract_clamp_fusion.ids_ref, s32[8]{0:T(128)S(1)} %copy-done.2, bf16[8,3,128,128]{3,2,1,0:T(8,128)(2,1)S(1)} %copy-done.1, bf16[256,2048]{1,0:T(8,128)(2,1)S(1)} %collective-permute-done.before_ref, bf16[1024,2048]{1,0:T(8,128)(2,1)S(1)} %copy-done, ...), custom_call_target="tpu_custom_call" | custom-call | flops 1610612736 | bytes 11272192 | tf_op jit(solution)/shard_map/blend_table/pallas_call | solution.py:56
  231.3 0.6 multiply_divide_fusion
  (27 shorter events, 0.2 us)
Async XLA Ops:
  7.2 130.7 %all-gather.2.cloned.1.call-start = ((), (), s32[]{:S(2)}) async-start(), calls=%async_computation | async-start | bytes 9437184 | tf_op jit(solution)/shard_map/all_gather | solution.py:161
  7.9 93.9 %collective-permute-start.2 = (bf16[1024,2048]{1,0:T(8,128)(2,1)}, bf16[1024,2048]{1,0:T(8,128)(2,1)}, u32[]{:S(2)}, u32[]{:S(2)}) collective-permute-start(bf16[1024,2048]{1,0:T(8,128)(2,1)} %param.9), channel_id=1, source_target_pairs={{0,2},{1,3},{2,0},{3,1},{4,6},{5,7},{6,4},{7,5},{8,10},{9,11},{10,... | collective-permute-start | bytes 12582920 | tf_op jit(solution)/shard_map/ppermute | solution.py:166
  10.9 135.7 %collective-permute-start.3 = (bf16[1024,2048]{1,0:T(8,128)(2,1)}, bf16[1024,2048]{1,0:T(8,128)(2,1)}, u32[]{:S(2)}, u32[]{:S(2)}) collective-permute-start(bf16[1024,2048]{1,0:T(8,128)(2,1)} %param.9), channel_id=1, source_target_pairs={{0,1},{1,0},{2,3},{3,2},{4,5},{5,4},{6,7},{7,6},{8,9},{9,8},{10,11... | collective-permute-start | bytes 12582920 | tf_op jit(solution)/shard_map/ppermute | solution.py:166
  101.8 49.5 %collective-permute-start.4 = (bf16[1024,2048]{1,0:T(8,128)(2,1)}, bf16[1024,2048]{1,0:T(8,128)(2,1)}, u32[]{:S(2)}, u32[]{:S(2)}) collective-permute-start(bf16[1024,2048]{1,0:T(8,128)(2,1)} %collective-permute-done.2), channel_id=1, source_target_pairs={{0,1},{1,0},{2,3},{3,2},{4,5},{5,4},{6,7},{7,6},{8,9},{9,8},{10,11... | collective-permute-start | bytes 12582920 | tf_op jit(solution)/shard_map/ppermute | solution.py:166
  137.8 5.3 %copy-start.6 = (bf16[512,8192]{1,0:T(8,128)(2,1)S(1)}, bf16[512,8192]{1,0:T(8,128)(2,1)}, u32[]{:S(2)}) copy-start(bf16[512,8192]{1,0:T(8,128)(2,1)} %all-gather.2.cloned.1.call-done) | copy-start | bytes 25165828
  137.8 6.4 %copy-start.7 = (bf16[1024,2048]{1,0:T(8,128)(2,1)S(1)}, bf16[1024,2048]{1,0:T(8,128)(2,1)}, u32[]{:S(2)}) copy-start(bf16[1024,2048]{1,0:T(8,128)(2,1)} %param.9) | copy-start | bytes 12582916
  151.2 8.6 %copy-start.5 = (s32[512]{0:T(512)S(1)}, s32[512]{0:T(512)}, u32[]{:S(2)}) copy-start(s32[512]{0:T(512)} %param.14) | copy-start | bytes 6148
  151.2 8.6 %copy-start.3 = (s32[8,3]{0,1:T(4,128)S(1)}, s32[8,3]{0,1:T(4,128)}, u32[]{:S(2)}) copy-start(s32[8,3]{0,1:T(4,128)} %param.10) | copy-start | bytes 292
  151.2 18.0 %copy-start.1 = (bf16[8,3,128,128]{3,2,1,0:T(8,128)(2,1)S(1)}, bf16[8,3,128,128]{3,2,1,0:T(8,128)(2,1)}, u32[]{:S(2)}) copy-start(bf16[8,3,128,128]{3,2,1,0:T(8,128)(2,1)} %weights_ref.3) | copy-start | bytes 2359300
  151.3 18.0 %copy-start.2 = (s32[8]{0:T(128)S(1)}, s32[8]{0:T(128)}, u32[]{:S(2)}) copy-start(s32[8]{0:T(128)} %counts_ref.3) | copy-start | bytes 100
  156.1 13.2 %collective-permute-start.5 = (bf16[256,512]{1,0:T(8,128)(2,1)S(1)}, bf16[256,512]{1,0:T(8,128)(2,1)S(1)}, u32[]{:S(2)}, u32[]{:S(2)}) collective-permute-start(bf16[256,512]{1,0:T(8,128)(2,1)S(1)} %get-tuple-element.9), channel_id=1, source_target_pairs={{0,4},{4,8},{8,12},{12,16},{16,20},{20,24},{24,28},{1,5},{5,9},{9,... | collective-permute-start | bytes 786440 | tf_op jit(solution)/shard_map/ppermute | solution.py:129
  158.5 10.7 %collective-permute-start.6 = (bf16[256,512]{1,0:T(8,128)(2,1)S(1)}, bf16[256,512]{1,0:T(8,128)(2,1)S(1)}, u32[]{:S(2)}, u32[]{:S(2)}) collective-permute-start(bf16[256,512]{1,0:T(8,128)(2,1)S(1)} %get-tuple-element.8), channel_id=1, source_target_pairs={{4,0},{8,4},{12,8},{16,12},{20,16},{24,20},{28,24},{5,1},{9,5},{13... | collective-permute-start | bytes 786440 | tf_op jit(solution)/shard_map/ppermute | solution.py:130
  171.3 9.0 %collective-permute-start.7 = (f32[3,512]{1,0:T(4,128)S(1)}, f32[3,512]{1,0:T(4,128)S(1)}, u32[]{:S(2)}, u32[]{:S(2)}) collective-permute-start(f32[3,512]{1,0:T(4,128)S(1)} %blend_stats.1), channel_id=1, source_target_pairs={{0,4},{4,0},{8,12},{12,8},{16,20},{20,16},{24,28},{28,24},{1,5},{5... | collective-permute-start | bytes 18440 | tf_op jit(solution)/shard_map/ppermute | solution.py:139
  177.0 45.8 %collective-permute-start = (bf16[256,2048]{1,0:T(8,128)(2,1)}, bf16[256,2048]{1,0:T(8,128)(2,1)S(1)}, u32[]{:S(2)}, u32[]{:S(2)}) collective-permute-start(bf16[256,2048]{1,0:T(8,128)(2,1)} %get-tuple-element.7), channel_id=1, source_target_pairs={{0,4},{4,8},{8,12},{12,16},{16,20},{20,24},{24,28},{1,5},{5,9},{9,... | collective-permute-start | bytes 3145736 | tf_op jit(solution)/shard_map/ppermute | solution.py:129
  179.0 43.8 %collective-permute-start.1 = (bf16[256,2048]{1,0:T(8,128)(2,1)}, bf16[256,2048]{1,0:T(8,128)(2,1)S(1)}, u32[]{:S(2)}, u32[]{:S(2)}) collective-permute-start(bf16[256,2048]{1,0:T(8,128)(2,1)} %get-tuple-element.6), channel_id=1, source_target_pairs={{4,0},{8,4},{12,8},{16,12},{20,16},{24,20},{28,24},{5,1},{9,5},{13... | collective-permute-start | bytes 3145736 | tf_op jit(solution)/shard_map/ppermute | solution.py:130
  180.4 26.6 %collective-permute-start.8 = (f32[3,512]{1,0:T(4,128)S(1)}, f32[3,512]{1,0:T(4,128)S(1)}, u32[]{:S(2)}, u32[]{:S(2)}) collective-permute-start(f32[3,512]{1,0:T(4,128)S(1)} %pad_maximum_fusion), channel_id=1, source_target_pairs={{0,8},{4,12},{8,0},{12,4},{16,24},{20,28},{24,16},{28,20},{1,9},{5... | collective-permute-start | bytes 18440 | tf_op jit(solution)/shard_map/ppermute | solution.py:139
  207.0 24.3 %copy-start.4 = (s32[512]{0:T(512)S(1)}, s32[512]{0:T(512)}, u32[]{:S(2)}) copy-start(s32[512]{0:T(512)} %param.15) | copy-start | bytes 6148
  207.0 24.3 %collective-permute-start.9 = (f32[3,512]{1,0:T(4,128)S(1)}, f32[3,512]{1,0:T(4,128)S(1)}, u32[]{:S(2)}, u32[]{:S(2)}) collective-permute-start(f32[3,512]{1,0:T(4,128)S(1)} %pad_maximum_fusion.1), channel_id=1, source_target_pairs={{0,16},{4,20},{8,24},{12,28},{16,0},{20,4},{24,8},{28,12},{1,17},{... | collective-permute-start | bytes 18440 | tf_op jit(solution)/shard_map/ppermute | solution.py:139
  222.8 2.2 copy-start
Sparse Core Ops, SparseCore 0:
  10.2 127.5 all-gather.1

commit v2 on v1

v2 whole, which is shorter than its diff:
```python
import functools
import math

import jax
import jax.numpy as jnp
from jax import lax
from jax.experimental import pallas as pl
from jax.experimental.pallas import tpu as pltpu
from jax.sharding import PartitionSpec as P

REACH = 2
CONTRACT_LAST = (((1,), (1,)), ((), ()))


def xor_perm(count, mask):
    return [(i, i ^ mask) for i in range(count)]


def masked(weights, slot, amount):
    return jnp.where(slot < amount, weights, jnp.zeros_like(weights))


def blend_block(ids_ref, counts_ref, weights_ref, padded, block):
    slots, rows = weights_ref.shape[1], weights_ref.shape[2]
    total = None
    for slot in range(slots):
        start = pl.multiple_of(ids_ref[block, slot] * rows, rows)
        part = jnp.dot(
            masked(weights_ref[block, slot], slot, counts_ref[block]),
            padded[pl.ds(start, rows), :],
            preferred_element_type=jnp.float32,
        )
        total = part if total is None else total + part
    return total


def table_kernel(ids_ref, counts_ref, side_ref, weights_ref, own_ref, before_ref, after_ref, relayed_ref, out_ref, padded):
    edge, own_rows = before_ref.shape[0], own_ref.shape[0]
    padded[pl.ds(0, edge), :] = before_ref[...]
    padded[pl.ds(edge, own_rows), :] = own_ref[...]
    padded[pl.ds(edge + own_rows, edge), :] = after_ref[...]

    @pl.when(side_ref[0] == 1)
    def _():
        padded[pl.ds(0, edge), :] = relayed_ref[...]

    @pl.when(side_ref[0] == 2)
    def _():
        padded[pl.ds(edge + own_rows, edge), :] = relayed_ref[...]

    blocks, rows = weights_ref.shape[0], weights_ref.shape[2]
    for block in range(blocks):
        summed = blend_block(ids_ref, counts_ref, weights_ref, padded, block)
        out_ref[pl.ds(block * rows, rows), :] = summed.astype(out_ref.dtype)


def blend_table(ids, counts, weights, own, before, after, relayed, side, tile=512):
    rows, columns = own.shape
    edge = before.shape[0]
    tile = math.gcd(tile, columns)
    smem = pl.BlockSpec(memory_space=pltpu.SMEM)
    strip = lambda count: pl.BlockSpec((count, tile), lambda i: (0, i))
    new_rows = weights.shape[0] * weights.shape[2]
    return pl.pallas_call(
        table_kernel,
        grid=(columns // tile,),
        out_shape=jax.ShapeDtypeStruct((new_rows, columns), own.dtype),
        in_specs=[smem, smem, smem, pl.BlockSpec(weights.shape, lambda i: (0, 0, 0, 0)), strip(rows)] + [strip(edge)] * 3,
        out_specs=strip(new_rows),
        scratch_shapes=[pltpu.VMEM((rows + 2 * edge, tile), own.dtype)],
        compiler_params=pltpu.CompilerParams(vmem_limit_bytes=32 << 20),
        cost_estimate=pl.CostEstimate(
            flops=0, bytes_accessed=0, transcendentals=0
        ),
        name="blend_table",
    )(ids, counts, side, weights, own, before, after, relayed)


def stats_kernel(ids_ref, counts_ref, weights_ref, *refs):
    *source_refs, goals_ref, out_ref, padded, logits = refs
    start = 0
    for source_ref in source_refs:
        padded[pl.ds(start, source_ref.shape[0]), :] = source_ref[...]
        start += source_ref.shape[0]
    blocks, rows = weights_ref.shape[0], weights_ref.shape[2]
    tokens = padded.shape[1]
    goals = goals_ref[...]
    peak = jnp.full((1, tokens), -jnp.inf, jnp.float32)
    picked = jnp.zeros((1, tokens), jnp.float32)
    for block in range(blocks):
        summed = blend_block(ids_ref, counts_ref, weights_ref, padded, block)
        logits[pl.ds(block * rows, rows), :] = summed
        peak = jnp.maximum(peak, jnp.max(summed, axis=0, keepdims=True))
        row_ids = lax.broadcasted_iota(jnp.int32, summed.shape, 0) + block * rows
        picked = picked + jnp.sum(jnp.where(row_ids == goals, summed, 0.0), axis=0, keepdims=True)
    total = jnp.zeros((1, tokens), jnp.float32)
    for block in range(blocks):
        values = jnp.exp(logits[pl.ds(block * rows, rows), :] - peak)
        total = total + jnp.sum(values, axis=0, keepdims=True)
    out_ref[0:1, :] = peak
    out_ref[1:2, :] = total
    out_ref[2:3, :] = picked


def local_stats(ids, counts, weights, source, goals):
    tokens = source[0].shape[1]
    source_rows = sum(value.shape[0] for value in source)
    smem = pl.BlockSpec(memory_space=pltpu.SMEM)
    vmem = pl.BlockSpec(memory_space=pltpu.VMEM)
    new_rows = weights.shape[0] * weights.shape[2]
    return pl.pallas_call(
        stats_kernel,
        out_shape=jax.ShapeDtypeStruct((3, tokens), jnp.float32),
        in_specs=[smem, smem, vmem] + [vmem] * (len(source) + 1),
        out_specs=vmem,
        scratch_shapes=[
            pltpu.VMEM((source_rows, tokens), source[0].dtype),
            pltpu.VMEM((new_rows, tokens), jnp.float32),
        ],
        compiler_params=pltpu.CompilerParams(vmem_limit_bytes=32 << 20),
        cost_estimate=pl.CostEstimate(
            flops=2 * weights.size * tokens, bytes_accessed=2 * source_rows * tokens, transcendentals=new_rows * tokens
        ),
        name="blend_stats",
    )(ids, counts, weights, *source, goals)


def product_kernel(where_ref, *refs, pieces, chunks, final):
    piece_refs, refs = refs[:pieces], refs[pieces:]
    chunk_refs, refs = refs[:chunks], refs[chunks:]
    carried_ref, refs = (refs[0], refs[1:]) if final else (None, refs)
    *out_refs, held, block, sems = refs
    width = held.shape[2]

    def column_copy(at, piece_ref):
        start = pl.multiple_of(where_ref[1, at] * width, width)
        return pltpu.make_async_copy(piece_ref.at[:, pl.ds(start, width)], held.at[at], sems.at[0, at])

    def block_copy(at):
        return pltpu.make_async_copy(chunk_refs[at], block.at[at], sems.at[1, at])

    for at in range(chunks):
        block_copy(at).start()
        for piece, piece_ref in enumerate(piece_refs):
            @pl.when(where_ref[0, at] == piece)
            def _(at=at, piece_ref=piece_ref):
                column_copy(at, piece_ref).start()

    for at in range(chunks):
        block_copy(at).wait()
        column_copy(at, piece_refs[0]).wait()
        row = 0
        for out_ref in out_refs:
            size = out_ref.shape[0]
            part = lax.dot_general(
                held[at, row : row + size, :], block[at], CONTRACT_LAST, preferred_element_type=jnp.float32
            )
            if final:
                out_ref[...] = (part + carried_ref[row : row + size, :]).astype(out_ref.dtype)
            elif at == 0:
                out_ref[...] = part
            else:
                out_ref[...] += part
            row += size


def add_products(where, pieces, chunks, carried=None, out_rows=()):
    rows, (tokens, width) = pieces[0].shape[0], chunks[0].shape
    final = carried is not None
    vmem = pl.BlockSpec(memory_space=pltpu.VMEM)
    hbm = pl.BlockSpec(memory_space=pltpu.HBM)
    shapes = [(size, tokens) for size in out_rows] if final else [(rows, tokens)]
    return pl.pallas_call(
        functools.partial(product_kernel, pieces=len(pieces), chunks=len(chunks), final=final),
        out_shape=[jax.ShapeDtypeStruct(shape, jnp.bfloat16 if final else jnp.float32) for shape in shapes],
        in_specs=[pl.BlockSpec(memory_space=pltpu.SMEM)] + [hbm] * (len(pieces) + len(chunks)) + [vmem] * final,
        out_specs=[vmem] * len(shapes),
        scratch_shapes=[
            pltpu.VMEM((len(chunks), rows, width), jnp.bfloat16),
            pltpu.VMEM((len(chunks), tokens, width), jnp.bfloat16),
            pltpu.SemaphoreType.DMA((2, len(chunks))),
        ],
        compiler_params=pltpu.CompilerParams(vmem_limit_bytes=58 << 20),
        cost_estimate=pl.CostEstimate(flops=0, bytes_accessed=0, transcendentals=0),
        name="last_product" if final else "early_product",
    )(where, *pieces, *chunks, *([carried] if final else []))


def ring_order(count):
    return list(range(0, count, 2)) + list(range(count - 1, 0, -2))


def nothing(*refs):
    del refs


def fence(*values):
    hbm = pl.BlockSpec(memory_space=pl.ANY)
    return pl.pallas_call(
        nothing,
        out_shape=[jax.ShapeDtypeStruct(value.shape, value.dtype) for value in values],
        in_specs=[hbm] * len(values),
        out_specs=[hbm] * len(values),
        input_output_aliases={i: i for i in range(len(values))},
        name="fence",
    )(*values)


def shifted(value, pairs):
    return lax.ppermute(value, "vocab", pairs)


def merge_stats(stats, axis):
    count = lax.axis_size(axis)
    index = lax.axis_index(axis)
    mask = 1
    while mask < count:
        other = lax.ppermute(stats, axis, xor_perm(count, mask))
        upper = (index & mask) != 0
        first = jnp.where(upper, other, stats)
        second = jnp.where(upper, stats, other)
        peak = jnp.maximum(first[0], second[0])
        total = first[1] * jnp.exp(first[0] - peak) + second[1] * jnp.exp(second[0] - peak)
        stats = jnp.stack([peak, total, first[2] + second[2]])
        mask *= 2
    return stats


def body(src_embed, src_head, block_ids, slot_counts, slot_weights, hidden, targets, byte_counts):
    block_rows = slot_weights.shape[2]
    rows, quarter = src_embed.shape
    new_rows = slot_weights.shape[0] * block_rows
    vocab_index = lax.axis_index("vocab")
    halo = REACH * block_rows
    last_local = rows // block_rows + 2 * REACH - 1
    local_ids = jnp.clip(block_ids - (vocab_index * (rows // block_rows) - REACH), 0, last_local)

    count = lax.axis_size("vocab")
    tok_index, tok_count = lax.axis_index("tok"), lax.axis_size("tok")
    up = [(i, i + 1) for i in range(count - 1)]
    down = [(j, i) for i, j in up]
    bottom_edge, top_edge = src_embed[rows - halo :], src_embed[:halo]
    far = tok_count // 2
    near_masks = [1 << bit for bit in reversed(range(far.bit_length() - 1))]
    width = hidden.shape[1]

    def to_far(value):
        return lax.ppermute(value, "tok", xor_perm(tok_count, far))

    def spread(held_pieces):
        for mask in near_masks:
            for held in list(held_pieces):
                held_pieces[held | mask] = lax.ppermute(held_pieces[held], "tok", xor_perm(tok_count, mask))
        return held_pieces

    def assembled(held_pieces, start, size):
        whole = jnp.zeros((size, tok_count * quarter), src_head.dtype)
        for held, entries in held_pieces.items():
            for offset, entry in entries:
                whole = lax.dynamic_update_slice(whole, entry, (offset - start, (tok_index ^ held) * quarter))
        return whole

    def product(head, arrivals):
        total = None
        for origin, value in arrivals:
            columns = lax.dynamic_slice_in_dim(head, origin * width, value.shape[1], axis=1)
            part = lax.dot_general(columns, value, CONTRACT_LAST, preferred_element_type=jnp.float32)
            total = part if total is None else total + part
        return total

    if count == 8 and tok_count == 4:
        order = ring_order(count)
        at = jnp.where(vocab_index % 2 == 0, vocab_index // 2, count - 1 - vocab_index // 2)
        ahead = [(order[i], order[(i + 1) % count]) for i in range(count)]
        behind = [(j, i) for i, j in ahead]

        def origin(offset):
            place = (at + offset) % count
            return jnp.where(place < count // 2, 2 * place, 2 * (count - 1 - place) + 1)

        aside_pairs = [(2, 3), (3, 2), (4, 5), (5, 4)]
        up_pairs = [(0, 1), (1, 2), (2, 3), (3, 4), (4, 6), (6, 7)]
        down_pairs = [(1, 0), (3, 1), (4, 3), (5, 4), (6, 5), (7, 6)]
        side = jnp.where(vocab_index == 5, 1, jnp.where(vocab_index == 2, 2, 0))
        a1, b1 = lax.ppermute(hidden, "vocab", ahead), lax.ppermute(hidden, "vocab", behind)
        far_head = to_far(src_head)
        aside = shifted(jnp.where(vocab_index < 4, top_edge, bottom_edge), aside_pairs)
        near_head = spread({0: src_head})[1]
        a1, b1, aside, near_head = fence(a1, b1, aside, near_head)
        a2, b2 = lax.ppermute(a1, "vocab", ahead), lax.ppermute(b1, "vocab", behind)
        table_before = shifted(jnp.where(vocab_index == 4, aside, bottom_edge), up_pairs)
        table_after = shifted(jnp.where(vocab_index == 3, aside, top_edge), down_pairs)
        a2, b2, table_before, table_after = fence(a2, b2, table_before, table_after)
        a3, b3 = lax.ppermute(a2, "vocab", ahead), lax.ppermute(b2, "vocab", behind)
        new_embed = blend_table(
            local_ids, slot_counts, slot_weights, src_embed, table_before, table_after, aside, side.reshape(1)
        )
        a3, b3, new_embed, far_head = fence(a3, b3, new_embed, far_head)
        even = tok_index % 2 == 0
        last_pairs = [
            (i * tok_count + t, j * tok_count + t) for t in range(tok_count) for i, j in (behind if t % 2 else ahead)
        ]
        c4 = lax.ppermute(jnp.where(even, a3, b3), ("vocab", "tok"), last_pairs)
        far_near_head = spread({far: far_head})[far | 1]
        pieces = [src_head, near_head, far_head, far_near_head]
        per = count // tok_count
        where = lambda offsets: jnp.stack(
            [jnp.stack([(origin(o) // per) ^ tok_index for o in offsets]), jnp.stack([origin(o) % per for o in offsets])]
        ).astype(jnp.int32)
        (early,) = add_products(where([0, -1, 1, -2, 2, -3, 3]), pieces, [hidden, a1, b1, a2, b2, a3, b3])
        source_logits = add_products(where([4]), pieces, [c4], early, (halo, rows - 2 * halo, halo))
    else:
        pieces = spread({0: src_head, far: to_far(src_head)})
        whole_head = assembled({held: [(0, piece)] for held, piece in pieces.items()}, 0, rows)
        whole_rows = lax.all_gather(hidden, "vocab", axis=1, tiled=True)
        total = product(whole_head, [(0, whole_rows)]).astype(jnp.bfloat16)
        source_logits = [total[:halo], total[halo : rows - halo], total[rows - halo :]]
        table_before, table_after = shifted(bottom_edge, up), shifted(top_edge, down)
        new_embed = blend_table(
            local_ids, slot_counts, slot_weights, src_embed, table_before, table_after, table_before, jnp.zeros((1,), jnp.int32)
        )
    after_rows = shifted(source_logits[0], down)
    before_rows = shifted(source_logits[-1], up)
    goals = (targets - vocab_index * new_rows)[None, :]
    stats = local_stats(local_ids, slot_counts, slot_weights, [before_rows] + list(source_logits) + [after_rows], goals)
    stats = merge_stats(stats, "vocab")
    log_total = stats[0] + jnp.log(stats[1])
    token_bpb = (log_total - stats[2]) / (jnp.float32(math.log(2.0)) * byte_counts.astype(jnp.float32))

    return (new_embed, token_bpb)


def solution(mesh):
    in_specs = (
        P("vocab", "tok"),
        P("vocab", "tok"),
        P("vocab", None),
        P("vocab"),
        P("vocab", None, None, None),
        P("tok", "vocab"),
        P("tok"),
        P("tok"),
    )
    out_specs = (P("vocab", "tok"), P("tok"))
    return jax.shard_map(body, mesh=mesh, in_specs=in_specs, out_specs=out_specs, check_vma=False)
```

time: 242 us -> 176 us (0.73); the launches traced: 239 us -> 176 us
  waiting for transfers between devices: 173 us -> 87.7 us
  starting transfers between devices: 19.3 us -> 39.6 us
  Pallas kernels: 8.32 us -> 26.3 us
  matrix products: 17 us -> 0 us
  between operations: 14.3 us -> 0.88 us
  other arithmetic: 0.73 us -> 7.89 us
  local copies, waits for them, and re-layouts: 6.56 us -> 13.2 us
    all_gather x1 -> x0, waiting for transfers between devices: 36 us -> none  [body(): whole_rows = lax.all_gather(hidden, 'vocab', axis=1, tiled=True)]
    ppermute x7 -> x15, waiting for transfers between devices: 113 us -> 82.5 us  [the longest x5 30.3 us: shifted(): return lax.ppermute(value, 'vocab', pairs)]
    ppermute x7 -> x15, starting transfers between devices: 10.1 us -> 29.6 us  [the longest x5 8.8 us: shifted(): return lax.ppermute(value, 'vocab', pairs)]
    ppermute x3, waiting for transfers between devices: 23 us -> 5.2 us  [merge_stats(): other = lax.ppermute(stats, axis, xor_perm(count, mask))]
    pallas_call x0 -> x5, Pallas kernels: none -> 17.8 us  [the longest x2 17.8 us: add_products(): pl.pallas_call(functools.partial(product_kernel, pieces=len(pieces), chun...]
    dot_general x4 -> x0, matrix products: 17 us -> none  [body(): lax.dot_general(piece, columns, (((1,), (1,)), ((), ())), preferred_eleme...]
    unnamed x17 -> x45, local copies, waits for them, and re-layouts: 3.37 us -> 13.1 us
    select_n x0 -> x3, other arithmetic: none -> 6.08 us  [the longest x1 2.62 us: body(): jnp.where(vocab_index < 4, top_edge, bottom_edge)]
  transfers between devices with their start and end apart: 11 -> 18, of which waited for: 5 -> 13; matrix products, arithmetic and copies ran while one was open for 7% -> 4% of each run, Pallas kernels for 3% -> 11%
where the time goes in v2:
time: 176 us
  waiting for transfers between devices  87.7 us (50%)
  starting transfers between devices  39.6 us (22%)
  Pallas kernels  26.3 us (15%)
  local copies, waits for them, and re-layouts  13.2 us (8%)
  other arithmetic  7.89 us (4%)
    ppermute x5, waiting for transfers between devices, shifted(): return lax.ppermute(value, 'vocab', pairs)  30.3 us
    ppermute x1, waiting for transfers between devices, body(): lax.ppermute(hidden, 'vocab', ahead)  18.6 us
    pallas_call x2, Pallas kernels, add_products(): pl.pallas_call(functools.partial(product_kernel, pieces=len(pieces), chun...  17.8 us
    ppermute x1, waiting for transfers between devices, body(): lax.ppermute(a1, 'vocab', ahead)  14.8 us
    unnamed x45, local copies, waits for them, and re-layouts  13.1 us
    ppermute x3, starting transfers between devices, merge_stats(): other = lax.ppermute(stats, axis, xor_perm(count, mask))  9.98 us
    ppermute x5, starting transfers between devices, shifted(): return lax.ppermute(value, 'vocab', pairs)  8.8 us
    ppermute x1, waiting for transfers between devices, body(): lax.ppermute(a2, 'vocab', ahead)  7.92 us
  transfers between devices with their start and end apart: 18, of which 13 were waited for; matrix products, arithmetic and copies ran while one was open for 4% of the time, Pallas kernels for 11%

profile of v2, /device:TPU:0, one launch (start us, length us, event | category | flops | bytes accessed | tf_op | source)
XLA Modules:
  0.0 175.6 jit_solution(5964798252678618875)
XLA Ops:
  1.1 2.6 %collective-permute-start = (bf16[512,1024]{1,0:T(8,128)(2,1)}, bf16[512,1024]{1,0:T(8,128)(2,1)S(1)}, u32[]{:S(2)}, u32[]{:S(2)}) collective-permute-start(bf16[512,1024]{1,0:T(8,128)(2,1)} %refs_4_.1), channel_id=1, source_target_pairs={{0,8},{8,16},{16,24},{24,28},{28,20},{20,12},{12,4},{4,0},{1,9},{9... | collective-permute-start | bytes 3145736 | tf_op jit(solution)/shard_map/ppermute | solution.py:285
  3.8 2.0 %collective-permute-start.10 = (bf16[1024,2048]{1,0:T(8,128)(2,1)}, bf16[1024,2048]{1,0:T(8,128)(2,1)}, u32[]{:S(2)}, u32[]{:S(2)}) collective-permute-start(bf16[1024,2048]{1,0:T(8,128)(2,1)} %refs_0_.3), channel_id=1, source_target_pairs={{0,2},{1,3},{2,0},{3,1},{4,6},{5,7},{6,4},{7,5},{8,10},{9,11},{10,... | collective-permute-start | bytes 12582920 | tf_op jit(solution)/shard_map/ppermute | solution.py:248
  5.8 2.6 %broadcast_select_fusion.3 = bf16[256,2048]{1,0:T(8,128)(2,1)} fusion(pred[]{:T(512)S(6)} %lt.125, bf16[1024,2048]{1,0:T(8,128)(2,1)} %own_ref.1), kind=kLoop, calls=%fused_computation.3 | loop fusion | flops 524288 | bytes 3145729 | tf_op jit(solution)/shard_map/jit(_where)/select_n | solution.py:287
  9.1 18.6 %collective-permute-done.refs_0_ = bf16[512,1024]{1,0:T(8,128)(2,1)S(1)} collective-permute-done((bf16[512,1024]{1,0:T(8,128)(2,1)}, bf16[512,1024]{1,0:T(8,128)(2,1)S(1)}, u32[]{:S(2)}, u32[]{:S(2)}) %collective-permute-start) | collective-permute-done | bytes 1048608 | tf_op jit(solution)/shard_map/ppermute | solution.py:285
  27.7 1.5 collective-permute-done.1.refs_1_
  30.5 7.1 %collective-permute-start.4 = (bf16[512,1024]{1,0:T(8,128)(2,1)}, bf16[512,1024]{1,0:T(8,128)(2,1)S(1)}, u32[]{:S(2)}, u32[]{:S(2)}) collective-permute-start(bf16[512,1024]{1,0:T(8,128)(2,1)} %get-tuple-element.17.refs_5_), channel_id=1, source_target_pairs={{0,8},{8,16},{16,24},{24,28},{28,20},{20,12},{12,4},{4,0},{1,9},{9... | collective-permute-start | bytes 3145736 | tf_op jit(solution)/shard_map/ppermute | solution.py:290
  37.7 2.1 %broadcast_select_fusion.1 = (bf16[256,2048]{1,0:T(8,128)(2,1)S(1)}, bf16[256,2048]{1,0:T(8,128)(2,1)S(1)}) fusion(bf16[256,2048]{1,0:T(8,128)(2,1)} %get-tuple-element.19.relayed_ref, pred[]{:T(512)S(6)} %eq.46, bf16[1024,2048]{1,0:T(8,128)(2,1)} %own_ref.1, pred[]{:T(512)S(6)} %eq.45), kind=kLoop, calls=%fused_computation.1 | loop fusion | flops 1048576 | bytes 5242882 | tf_op jit(solution)/shard_map/jit(_where)/select_n | solution.py:292
  39.8 3.5 %collective-permute-start.6 = (bf16[256,2048]{1,0:T(8,128)(2,1)S(1)}, bf16[256,2048]{1,0:T(8,128)(2,1)S(1)}, u32[]{:S(2)}, u32[]{:S(2)}) collective-permute-start(bf16[256,2048]{1,0:T(8,128)(2,1)S(1)} %get-tuple-element.37), channel_id=1, source_target_pairs={{0,4},{4,8},{8,12},{12,16},{16,24},{24,28},{1,5},{5,9},{9,13},{13,... | collective-permute-start | bytes 3145736 | tf_op jit(solution)/shard_map/ppermute | solution.py:210
  43.3 1.3 collective-permute-start.7
  44.6 14.8 %collective-permute-done.4.refs_0_ = bf16[512,1024]{1,0:T(8,128)(2,1)S(1)} collective-permute-done((bf16[512,1024]{1,0:T(8,128)(2,1)}, bf16[512,1024]{1,0:T(8,128)(2,1)S(1)}, u32[]{:S(2)}, u32[]{:S(2)}) %collective-permute-start.4) | collective-permute-done | bytes 1048608 | tf_op jit(solution)/shard_map/ppermute | solution.py:290
  59.4 2.2 %collective-permute-done.5.refs_1_ = bf16[512,1024]{1,0:T(8,128)(2,1)S(1)} collective-permute-done((bf16[512,1024]{1,0:T(8,128)(2,1)}, bf16[512,1024]{1,0:T(8,128)(2,1)S(1)}, u32[]{:S(2)}, u32[]{:S(2)}) %collective-permute-start.5) | collective-permute-done | bytes 1048608 | tf_op jit(solution)/shard_map/ppermute | solution.py:290
  61.6 20.1 %collective-permute-done.6.refs_2_ = bf16[256,2048]{1,0:T(8,128)(2,1)S(1)} collective-permute-done((bf16[256,2048]{1,0:T(8,128)(2,1)S(1)}, bf16[256,2048]{1,0:T(8,128)(2,1)S(1)}, u32[]{:S(2)}, u32[]{:S(2)}) %collective-permute-start.6) | collective-permute-done | bytes 1048608 | tf_op jit(solution)/shard_map/ppermute | solution.py:210
  83.7 6.8 %collective-permute-start.8 = (bf16[512,1024]{1,0:T(8,128)(2,1)}, bf16[512,1024]{1,0:T(8,128)(2,1)S(1)}, u32[]{:S(2)}, u32[]{:S(2)}) collective-permute-start(bf16[512,1024]{1,0:T(8,128)(2,1)} %get-tuple-element.20.refs_7_), channel_id=1, source_target_pairs={{0,8},{8,16},{16,24},{24,28},{28,20},{20,12},{12,4},{4,0},{1,9},{9... | collective-permute-start | bytes 3145736 | tf_op jit(solution)/shard_map/ppermute | solution.py:294
  90.6 2.2 %copy-done = bf16[1024,2048]{1,0:T(8,128)(2,1)S(1)} copy-done((bf16[1024,2048]{1,0:T(8,128)(2,1)S(1)}, bf16[1024,2048]{1,0:T(8,128)(2,1)}, u32[]{:S(2)}) %copy-start) | copy-done | bytes 4194328
  96.4 6.4 %blend_table.1.refs_2_ = bf16[1024,2048]{1,0:T(8,128)(2,1)} custom-call(s32[8,3]{1,0:T(8,128)S(1)} %subtract_clamp_fusion.ids_ref, s32[8]{0:T(128)S(1)} %copy-done.12, s32[1]{0:T(128)} %bitcast.side_ref, bf16[8,3,128,128]{3,2,1,0:T(8,128)(2,1)S(1)} %copy-done.7, bf16[1024,2048]{1,0:T(8,128)(2,1)S(1)} %copy-done, bf16[256,2048]{1,0:T(8,128)(2,1)S(1)} %copy-done.4, ...), custom_call_target="tpu_custom_call" | custom-call | tf_op jit(solution)/shard_map/blend_table/pallas_call | solution.py:64
  102.8 7.9 %collective-permute-done.8.refs_0_ = bf16[512,1024]{1,0:T(8,128)(2,1)S(1)} collective-permute-done((bf16[512,1024]{1,0:T(8,128)(2,1)}, bf16[512,1024]{1,0:T(8,128)(2,1)S(1)}, u32[]{:S(2)}, u32[]{:S(2)}) %collective-permute-start.8) | collective-permute-done | bytes 1048608 | tf_op jit(solution)/shard_map/ppermute | solution.py:294
  110.7 4.1 %collective-permute-done.9.refs_1_ = bf16[512,1024]{1,0:T(8,128)(2,1)} collective-permute-done((bf16[512,1024]{1,0:T(8,128)(2,1)}, bf16[512,1024]{1,0:T(8,128)(2,1)}, u32[]{:S(2)}, u32[]{:S(2)}) %collective-permute-start.9) | collective-permute-done | bytes 1048608 | tf_op jit(solution)/shard_map/ppermute | solution.py:294
  114.8 1.3 broadcast_select_fusion
  116.1 1.8 %collective-permute-start.12 = (bf16[512,1024]{1,0:T(8,128)(2,1)S(1)}, bf16[512,1024]{1,0:T(8,128)(2,1)S(1)}, u32[]{:S(2)}, u32[]{:S(2)}) collective-permute-start(bf16[512,1024]{1,0:T(8,128)(2,1)S(1)} %broadcast_select_fusion), channel_id=1, source_target_pairs={{0,8},{8,16},{16,24},{24,28},{28,20},{20,12},{12,4},{4,0},{9,1},{1... | collective-permute-start | bytes 3145736 | tf_op jit(solution)/shard_map/ppermute | solution.py:303
  119.2 3.1 %collective-permute-done.11.refs_3_ = bf16[1024,2048]{1,0:T(8,128)(2,1)} collective-permute-done((bf16[1024,2048]{1,0:T(8,128)(2,1)}, bf16[1024,2048]{1,0:T(8,128)(2,1)}, u32[]{:S(2)}, u32[]{:S(2)}) %collective-permute-start.11) | collective-permute-done | bytes 4194336 | tf_op jit(solution)/shard_map/ppermute | solution.py:253
  122.3 12.3 %early_product.1.refs_5_ = f32[1024,512]{1,0:T(8,128)} custom-call(s32[2,7]{1,0:T(2,128)} %pad_add_fusion.1.where_ref, bf16[1024,2048]{1,0:T(8,128)(2,1)} %refs_0_.3, bf16[1024,2048]{1,0:T(8,128)(2,1)} %get-tuple-element.25.refs_1_, bf16[1024,2048]{1,0:T(8,128)(2,1)} %get-tuple-element.26.refs_2_, bf16[1024,2048]{1,0:T(8,128)(2,1)} %collective-permute-done.11.refs_3_, ...), custom_call_target="tpu_custom_call" | custom-call | tf_op jit(solution)/shard_map/early_product/pallas_call | solution.py:173
  135.6 5.5 %last_product.1 = (bf16[256,512]{1,0:T(8,128)(2,1)}, bf16[512,512]{1,0:T(8,128)(2,1)}, bf16[256,512]{1,0:T(8,128)(2,1)}) custom-call(s32[2,1]{1,0:T(2,128)} %pad_add_fusion.where_ref, bf16[1024,2048]{1,0:T(8,128)(2,1)} %refs_0_.3, bf16[1024,2048]{1,0:T(8,128)(2,1)} %get-tuple-element.25.refs_1_, bf16[1024,2048]{1,0:T(8,128)(2,1)} %get-tuple-element.26.refs_2_, ...), custom_call_target="tpu_custom_call" | custom-call | tf_op jit(solution)/shard_map/last_product/pallas_call | solution.py:173
  141.2 2.1 %collective-permute-start.13 = (bf16[256,512]{1,0:T(8,128)(2,1)}, bf16[256,512]{1,0:T(8,128)(2,1)S(1)}, u32[]{:S(2)}, u32[]{:S(2)}) collective-permute-start(bf16[256,512]{1,0:T(8,128)(2,1)} %get-tuple-element.29.refs_3_), channel_id=1, source_target_pairs={{0,4},{4,8},{8,12},{12,16},{16,20},{20,24},{24,28},{1,5},{5,9},{9,... | collective-permute-start | bytes 786440 | tf_op jit(solution)/shard_map/ppermute | solution.py:210
  144.6 5.0 %collective-permute-done.13.refs_0_ = bf16[256,512]{1,0:T(8,128)(2,1)S(1)} collective-permute-done((bf16[256,512]{1,0:T(8,128)(2,1)}, bf16[256,512]{1,0:T(8,128)(2,1)S(1)}, u32[]{:S(2)}, u32[]{:S(2)}) %collective-permute-start.13) | collective-permute-done | bytes 262176 | tf_op jit(solution)/shard_map/ppermute | solution.py:210
  149.6 5.2 %collective-permute-done.14.refs_4_ = bf16[256,512]{1,0:T(8,128)(2,1)S(1)} collective-permute-done((bf16[256,512]{1,0:T(8,128)(2,1)}, bf16[256,512]{1,0:T(8,128)(2,1)S(1)}, u32[]{:S(2)}, u32[]{:S(2)}) %collective-permute-start.14) | collective-permute-done | bytes 262176 | tf_op jit(solution)/shard_map/ppermute | solution.py:210
  157.7 2.0 %blend_stats.1 = f32[3,512]{1,0:T(4,128)S(1)} custom-call(s32[8,3]{1,0:T(8,128)S(1)} %subtract_clamp_fusion.ids_ref, s32[8]{0:T(128)S(1)} %copy-done.12, bf16[8,3,128,128]{3,2,1,0:T(8,128)(2,1)S(1)} %copy-done.8, bf16[256,512]{1,0:T(8,128)(2,1)S(1)} %collective-permute-done.13.refs_0_, bf16[256,512]{1,0:T(8,128)(2,1)S(1)} %copy-done.10, ...), custom_call_target="tpu_custom_call" | custom-call | flops 402653184 | bytes 1572864 | tf_op jit(solution)/shard_map/blend_stats/pallas_call | solution.py:111
  159.7 2.7 %collective-permute-start.15 = (f32[3,512]{1,0:T(4,128)S(1)}, f32[3,512]{1,0:T(4,128)S(1)}, u32[]{:S(2)}, u32[]{:S(2)}) collective-permute-start(f32[3,512]{1,0:T(4,128)S(1)} %blend_stats.1), channel_id=1, source_target_pairs={{0,4},{4,0},{8,12},{12,8},{16,20},{20,16},{24,28},{28,24},{1,5},{5... | collective-permute-start | bytes 18440 | tf_op jit(solution)/shard_map/ppermute | solution.py:218
  162.4 1.6 collective-permute-done.15
  164.1 4.6 %collective-permute-start.16 = (f32[3,512]{1,0:T(4,128)S(1)}, f32[3,512]{1,0:T(4,128)S(1)}, u32[]{:S(2)}, u32[]{:S(2)}) collective-permute-start(f32[3,512]{1,0:T(4,128)S(1)} %pad_maximum_fusion), channel_id=1, source_target_pairs={{0,8},{4,12},{8,0},{12,4},{16,24},{20,28},{24,16},{28,20},{1,9},{5... | collective-permute-start | bytes 18440 | tf_op jit(solution)/shard_map/ppermute | solution.py:218
  168.7 1.6 collective-permute-done.16
  170.4 2.7 %collective-permute-start.17 = (f32[3,512]{1,0:T(4,128)S(1)}, f32[3,512]{1,0:T(4,128)S(1)}, u32[]{:S(2)}, u32[]{:S(2)}) collective-permute-start(f32[3,512]{1,0:T(4,128)S(1)} %pad_maximum_fusion.1), channel_id=1, source_target_pairs={{0,16},{4,20},{8,24},{12,28},{16,0},{20,4},{24,8},{28,12},{1,17},{... | collective-permute-start | bytes 18440 | tf_op jit(solution)/shard_map/ppermute | solution.py:218
  173.1 1.9 %collective-permute-done.17 = f32[3,512]{1,0:T(4,128)S(1)} collective-permute-done((f32[3,512]{1,0:T(4,128)S(1)}, f32[3,512]{1,0:T(4,128)S(1)}, u32[]{:S(2)}, u32[]{:S(2)}) %collective-permute-start.17) | collective-permute-done | bytes 6176 | tf_op jit(solution)/shard_map/ppermute | solution.py:218
  (74 shorter events, 15.4 us)
Async XLA Ops:
  0.6 28.6 %collective-permute-start.3 = (bf16[1024,2048]{1,0:T(8,128)(2,1)}, bf16[1024,2048]{1,0:T(8,128)(2,1)}, u32[]{:S(2)}, u32[]{:S(2)}) collective-permute-start(bf16[1024,2048]{1,0:T(8,128)(2,1)} %refs_0_.3), channel_id=1, source_target_pairs={{0,1},{1,0},{2,3},{3,2},{4,5},{5,4},{6,7},{7,6},{8,9},{9,8},{10,11... | collective-permute-start | bytes 12582920 | tf_op jit(solution)/shard_map/ppermute | solution.py:253
  1.1 26.5 %collective-permute-start = (bf16[512,1024]{1,0:T(8,128)(2,1)}, bf16[512,1024]{1,0:T(8,128)(2,1)S(1)}, u32[]{:S(2)}, u32[]{:S(2)}) collective-permute-start(bf16[512,1024]{1,0:T(8,128)(2,1)} %refs_4_.1), channel_id=1, source_target_pairs={{0,8},{8,16},{16,24},{24,28},{28,20},{20,12},{12,4},{4,0},{1,9},{9... | collective-permute-start | bytes 3145736 | tf_op jit(solution)/shard_map/ppermute | solution.py:285
  3.8 25.4 %collective-permute-start.1 = (bf16[512,1024]{1,0:T(8,128)(2,1)}, bf16[512,1024]{1,0:T(8,128)(2,1)S(1)}, u32[]{:S(2)}, u32[]{:S(2)}) collective-permute-start(bf16[512,1024]{1,0:T(8,128)(2,1)} %refs_4_.1), channel_id=1, source_target_pairs={{8,0},{16,8},{24,16},{28,24},{20,28},{12,20},{4,12},{0,4},{9,1},{1... | collective-permute-start | bytes 3145736 | tf_op jit(solution)/shard_map/ppermute | solution.py:285
  3.8 99.0 %collective-permute-start.10 = (bf16[1024,2048]{1,0:T(8,128)(2,1)}, bf16[1024,2048]{1,0:T(8,128)(2,1)}, u32[]{:S(2)}, u32[]{:S(2)}) collective-permute-start(bf16[1024,2048]{1,0:T(8,128)(2,1)} %refs_0_.3), channel_id=1, source_target_pairs={{0,2},{1,3},{2,0},{3,1},{4,6},{5,7},{6,4},{7,5},{8,10},{9,11},{10,... | collective-permute-start | bytes 12582920 | tf_op jit(solution)/shard_map/ppermute | solution.py:248
  8.4 20.9 %collective-permute-start.2 = (bf16[256,2048]{1,0:T(8,128)(2,1)}, bf16[256,2048]{1,0:T(8,128)(2,1)S(1)}, u32[]{:S(2)}, u32[]{:S(2)}) collective-permute-start(bf16[256,2048]{1,0:T(8,128)(2,1)} %broadcast_select_fusion.3), channel_id=1, source_target_pairs={{8,12},{12,8},{16,20},{20,16},{9,13},{13,9},{17,21},{21,17},{10,14... | collective-permute-start | bytes 3145736 | tf_op jit(solution)/shard_map/ppermute | solution.py:210
  27.7 1.6 copy-start.14
  29.2 1.3 copy-start.1
  30.5 28.8 %collective-permute-start.4 = (bf16[512,1024]{1,0:T(8,128)(2,1)}, bf16[512,1024]{1,0:T(8,128)(2,1)S(1)}, u32[]{:S(2)}, u32[]{:S(2)}) collective-permute-start(bf16[512,1024]{1,0:T(8,128)(2,1)} %get-tuple-element.17.refs_5_), channel_id=1, source_target_pairs={{0,8},{8,16},{16,24},{24,28},{28,20},{20,12},{12,4},{4,0},{1,9},{9... | collective-permute-start | bytes 3145736 | tf_op jit(solution)/shard_map/ppermute | solution.py:290
  37.7 23.9 %collective-permute-start.5 = (bf16[512,1024]{1,0:T(8,128)(2,1)}, bf16[512,1024]{1,0:T(8,128)(2,1)S(1)}, u32[]{:S(2)}, u32[]{:S(2)}) collective-permute-start(bf16[512,1024]{1,0:T(8,128)(2,1)} %get-tuple-element.18.refs_6_), channel_id=1, source_target_pairs={{8,0},{16,8},{24,16},{28,24},{20,28},{12,20},{4,12},{0,4},{9,1},{1... | collective-permute-start | bytes 3145736 | tf_op jit(solution)/shard_map/ppermute | solution.py:290
  37.7 52.8 %copy-start.19 = (s32[8,3]{0,1:T(4,128)S(1)}, s32[8,3]{0,1:T(4,128)}, u32[]{:S(2)}) copy-start(s32[8,3]{0,1:T(4,128)} %param.10) | copy-start | bytes 292
  37.7 52.9 %copy-start.2 = (bf16[256,2048]{1,0:T(8,128)(2,1)S(1)}, bf16[256,2048]{1,0:T(8,128)(2,1)}, u32[]{:S(2)}) copy-start(bf16[256,2048]{1,0:T(8,128)(2,1)} %get-tuple-element.19.relayed_ref) | copy-start | bytes 3145732
  37.7 52.9 %copy-start.12 = (s32[8]{0:T(128)S(1)}, s32[8]{0:T(128)}, u32[]{:S(2)}) copy-start(s32[8]{0:T(128)} %counts_ref.3) | copy-start | bytes 100
  39.8 41.9 %collective-permute-start.6 = (bf16[256,2048]{1,0:T(8,128)(2,1)S(1)}, bf16[256,2048]{1,0:T(8,128)(2,1)S(1)}, u32[]{:S(2)}, u32[]{:S(2)}) collective-permute-start(bf16[256,2048]{1,0:T(8,128)(2,1)S(1)} %get-tuple-element.37), channel_id=1, source_target_pairs={{0,4},{4,8},{8,12},{12,16},{16,24},{24,28},{1,5},{5,9},{9,13},{13,... | collective-permute-start | bytes 3145736 | tf_op jit(solution)/shard_map/ppermute | solution.py:210
  43.3 38.5 %collective-permute-start.7 = (bf16[256,2048]{1,0:T(8,128)(2,1)S(1)}, bf16[256,2048]{1,0:T(8,128)(2,1)S(1)}, u32[]{:S(2)}, u32[]{:S(2)}) collective-permute-start(bf16[256,2048]{1,0:T(8,128)(2,1)S(1)} %get-tuple-element.36), channel_id=1, source_target_pairs={{4,0},{12,4},{16,12},{20,16},{24,20},{28,24},{5,1},{13,5},{17,13},... | collective-permute-start | bytes 3145736 | tf_op jit(solution)/shard_map/ppermute | solution.py:210
  59.4 22.4 %copy-start.16 = (bf16[512,1024]{1,0:T(8,128)(2,1)}, bf16[512,1024]{1,0:T(8,128)(2,1)S(1)}, u32[]{:S(2)}) copy-start(bf16[512,1024]{1,0:T(8,128)(2,1)S(1)} %collective-permute-done.4.refs_0_) | copy-start | bytes 3145732
  61.6 20.1 %copy-start.17 = (bf16[512,1024]{1,0:T(8,128)(2,1)}, bf16[512,1024]{1,0:T(8,128)(2,1)S(1)}, u32[]{:S(2)}) copy-start(bf16[512,1024]{1,0:T(8,128)(2,1)S(1)} %collective-permute-done.5.refs_1_) | copy-start | bytes 3145732
  83.7 27.0 %collective-permute-start.8 = (bf16[512,1024]{1,0:T(8,128)(2,1)}, bf16[512,1024]{1,0:T(8,128)(2,1)S(1)}, u32[]{:S(2)}, u32[]{:S(2)}) collective-permute-start(bf16[512,1024]{1,0:T(8,128)(2,1)} %get-tuple-element.20.refs_7_), channel_id=1, source_target_pairs={{0,8},{8,16},{16,24},{24,28},{28,20},{20,12},{12,4},{4,0},{1,9},{9... | collective-permute-start | bytes 3145736 | tf_op jit(solution)/shard_map/ppermute | solution.py:294
  90.5 24.3 %collective-permute-start.9 = (bf16[512,1024]{1,0:T(8,128)(2,1)}, bf16[512,1024]{1,0:T(8,128)(2,1)}, u32[]{:S(2)}, u32[]{:S(2)}) collective-permute-start(bf16[512,1024]{1,0:T(8,128)(2,1)} %get-tuple-element.21.refs_8_), channel_id=1, source_target_pairs={{8,0},{16,8},{24,16},{28,24},{20,28},{12,20},{4,12},{0,4},{9,1},{1... | collective-permute-start | bytes 3145736 | tf_op jit(solution)/shard_map/ppermute | solution.py:294
  90.6 2.2 %copy-start = (bf16[1024,2048]{1,0:T(8,128)(2,1)S(1)}, bf16[1024,2048]{1,0:T(8,128)(2,1)}, u32[]{:S(2)}) copy-start(bf16[1024,2048]{1,0:T(8,128)(2,1)} %own_ref.1) | copy-start | bytes 12582916
  92.8 1.2 copy-start.4
  94.0 1.2 copy-start.6
  110.7 4.1 %copy-start.13 = (bf16[512,1024]{1,0:T(8,128)(2,1)}, bf16[512,1024]{1,0:T(8,128)(2,1)S(1)}, u32[]{:S(2)}) copy-start(bf16[512,1024]{1,0:T(8,128)(2,1)S(1)} %collective-permute-done.8.refs_0_) | copy-start | bytes 3145732
  114.8 7.5 %collective-permute-start.11 = (bf16[1024,2048]{1,0:T(8,128)(2,1)}, bf16[1024,2048]{1,0:T(8,128)(2,1)}, u32[]{:S(2)}, u32[]{:S(2)}) collective-permute-start(bf16[1024,2048]{1,0:T(8,128)(2,1)} %get-tuple-element.26.refs_2_), channel_id=1, source_target_pairs={{0,1},{1,0},{2,3},{3,2},{4,5},{5,4},{6,7},{7,6},{8,9},{9,8},{10,11... | collective-permute-start | bytes 12582920 | tf_op jit(solution)/shard_map/ppermute | solution.py:253
  116.1 18.5 %collective-permute-start.12 = (bf16[512,1024]{1,0:T(8,128)(2,1)S(1)}, bf16[512,1024]{1,0:T(8,128)(2,1)S(1)}, u32[]{:S(2)}, u32[]{:S(2)}) collective-permute-start(bf16[512,1024]{1,0:T(8,128)(2,1)S(1)} %broadcast_select_fusion), channel_id=1, source_target_pairs={{0,8},{8,16},{16,24},{24,28},{28,20},{20,12},{12,4},{4,0},{9,1},{1... | collective-permute-start | bytes 3145736 | tf_op jit(solution)/shard_map/ppermute | solution.py:303
  134.6 9.9 %copy-start.21 = (s32[512]{0:T(512)S(1)}, s32[512]{0:T(512)}, u32[]{:S(2)}) copy-start(s32[512]{0:T(512)} %param.14) | copy-start | bytes 6148
  134.6 20.1 %copy-start.8 = (bf16[8,3,128,128]{3,2,1,0:T(8,128)(2,1)S(1)}, bf16[8,3,128,128]{3,2,1,0:T(8,128)(2,1)}, u32[]{:S(2)}) copy-start(bf16[8,3,128,128]{3,2,1,0:T(8,128)(2,1)} %weights_ref.3) | copy-start | bytes 2359300
  134.6 40.4 %copy-start.20 = (s32[512]{0:T(512)S(1)}, s32[512]{0:T(512)}, u32[]{:S(2)}) copy-start(s32[512]{0:T(512)} %param.15) | copy-start | bytes 6148
  141.2 8.4 %collective-permute-start.13 = (bf16[256,512]{1,0:T(8,128)(2,1)}, bf16[256,512]{1,0:T(8,128)(2,1)S(1)}, u32[]{:S(2)}, u32[]{:S(2)}) collective-permute-start(bf16[256,512]{1,0:T(8,128)(2,1)} %get-tuple-element.29.refs_3_), channel_id=1, source_target_pairs={{0,4},{4,8},{8,12},{12,16},{16,20},{20,24},{24,28},{1,5},{5,9},{9,... | collective-permute-start | bytes 786440 | tf_op jit(solution)/shard_map/ppermute | solution.py:210
  143.2 11.5 %collective-permute-start.14 = (bf16[256,512]{1,0:T(8,128)(2,1)}, bf16[256,512]{1,0:T(8,128)(2,1)S(1)}, u32[]{:S(2)}, u32[]{:S(2)}) collective-permute-start(bf16[256,512]{1,0:T(8,128)(2,1)} %get-tuple-element.30.refs_1_), channel_id=1, source_target_pairs={{4,0},{8,4},{12,8},{16,12},{20,16},{24,20},{28,24},{5,1},{9,5},{13... | collective-permute-start | bytes 786440 | tf_op jit(solution)/shard_map/ppermute | solution.py:210
  159.7 4.3 %collective-permute-start.15 = (f32[3,512]{1,0:T(4,128)S(1)}, f32[3,512]{1,0:T(4,128)S(1)}, u32[]{:S(2)}, u32[]{:S(2)}) collective-permute-start(f32[3,512]{1,0:T(4,128)S(1)} %blend_stats.1), channel_id=1, source_target_pairs={{0,4},{4,0},{8,12},{12,8},{16,20},{20,16},{24,28},{28,24},{1,5},{5... | collective-permute-start | bytes 18440 | tf_op jit(solution)/shard_map/ppermute | solution.py:218
  164.1 6.2 %collective-permute-start.16 = (f32[3,512]{1,0:T(4,128)S(1)}, f32[3,512]{1,0:T(4,128)S(1)}, u32[]{:S(2)}, u32[]{:S(2)}) collective-permute-start(f32[3,512]{1,0:T(4,128)S(1)} %pad_maximum_fusion), channel_id=1, source_target_pairs={{0,8},{4,12},{8,0},{12,4},{16,24},{20,28},{24,16},{28,20},{1,9},{5... | collective-permute-start | bytes 18440 | tf_op jit(solution)/shard_map/ppermute | solution.py:218
  170.4 4.6 %collective-permute-start.17 = (f32[3,512]{1,0:T(4,128)S(1)}, f32[3,512]{1,0:T(4,128)S(1)}, u32[]{:S(2)}, u32[]{:S(2)}) collective-permute-start(f32[3,512]{1,0:T(4,128)S(1)} %pad_maximum_fusion.1), channel_id=1, source_target_pairs={{0,16},{4,20},{8,24},{12,28},{16,0},{20,4},{24,8},{28,12},{1,17},{... | collective-permute-start | bytes 18440 | tf_op jit(solution)/shard_map/ppermute | solution.py:218
  (8 other events, 8.0 us)

commit v3 on v2

--- a/solution.py
+++ b/solution.py
@@ -125,62 +125,88 @@
     )(ids, counts, weights, *source, goals)
 
 
-def product_kernel(where_ref, *refs, pieces, chunks, final):
+def product_kernel(where_ref, *refs, pieces, chunks, bands, skipped, only, final):
     piece_refs, refs = refs[:pieces], refs[pieces:]
     chunk_refs, refs = refs[:chunks], refs[chunks:]
     carried_ref, refs = (refs[0], refs[1:]) if final else (None, refs)
-    *out_refs, held, block, sems = refs
+    out_refs, (total, held, block, sems) = refs[:-4], refs[-4:]
     width = held.shape[2]
 
-    def column_copy(at, piece_ref):
+    def copies(at, piece_ref):
         start = pl.multiple_of(where_ref[1, at] * width, width)
-        return pltpu.make_async_copy(piece_ref.at[:, pl.ds(start, width)], held.at[at], sems.at[0, at])
+        row = 0
+        for band, (first, size) in enumerate(bands):
+            yield pltpu.make_async_copy(
+                piece_ref.at[pl.ds(first, size), pl.ds(start, width)],
+                held.at[at, pl.ds(row, size), :],
+                sems.at[1 + band, at],
+            )
+            row += size
 
     def block_copy(at):
-        return pltpu.make_async_copy(chunk_refs[at], block.at[at], sems.at[1, at])
+        return pltpu.make_async_copy(chunk_refs[at], block.at[at], sems.at[0, at])
+
+    def wanted(at):
+        if only and at == chunks - 1:
+            return where_ref[0, at] >= 0
+        return (where_ref[0, at] == skipped) if only else (where_ref[0, at] != skipped)
 
     for at in range(chunks):
-        block_copy(at).start()
+        @pl.when(wanted(at))
+        def _(at=at):
+            block_copy(at).start()
+
         for piece, piece_ref in enumerate(piece_refs):
-            @pl.when(where_ref[0, at] == piece)
+            @pl.when(wanted(at) & (where_ref[0, at] == piece))
             def _(at=at, piece_ref=piece_ref):
-                column_copy(at, piece_ref).start()
-
+                for copy in copies(at, piece_ref):
+                    copy.start()
+
+    if final:
+        row = 0
+        for first, size in bands:
+            total[pl.ds(row, size), :] = carried_ref[pl.ds(first, size), :]
+            row += size
+    else:
+        total[...] = jnp.zeros_like(total)
     for at in range(chunks):
-        block_copy(at).wait()
-        column_copy(at, piece_refs[0]).wait()
-        row = 0
-        for out_ref in out_refs:
-            size = out_ref.shape[0]
-            part = lax.dot_general(
-                held[at, row : row + size, :], block[at], CONTRACT_LAST, preferred_element_type=jnp.float32
-            )
-            if final:
-                out_ref[...] = (part + carried_ref[row : row + size, :]).astype(out_ref.dtype)
-            elif at == 0:
-                out_ref[...] = part
-            else:
-                out_ref[...] += part
-            row += size
-
-
-def add_products(where, pieces, chunks, carried=None, out_rows=()):
-    rows, (tokens, width) = pieces[0].shape[0], chunks[0].shape
+        @pl.when(wanted(at))
+        def _(at=at):
+            block_copy(at).wait()
+            for copy in copies(at, piece_refs[0]):
+                copy.wait()
+            total[...] += lax.dot_general(held[at], block[at], CONTRACT_LAST, preferred_element_type=jnp.float32)
+
+    row = 0
+    for out_ref in out_refs:
+        out_ref[...] = total[pl.ds(row, out_ref.shape[0]), :].astype(out_ref.dtype)
+        row += out_ref.shape[0]
+
+
+def add_products(where, pieces, chunks, bands, skipped, carried=None):
+    tokens, width = chunks[0].shape
+    rows = sum(size for _, size in bands)
     final = carried is not None
     vmem = pl.BlockSpec(memory_space=pltpu.VMEM)
     hbm = pl.BlockSpec(memory_space=pltpu.HBM)
-    shapes = [(size, tokens) for size in out_rows] if final else [(rows, tokens)]
+    if final:
+        shapes = [jax.ShapeDtypeStruct((size, tokens), jnp.bfloat16) for _, size in bands]
+    else:
+        shapes = [jax.ShapeDtypeStruct((rows, tokens), jnp.float32)]
     return pl.pallas_call(
-        functools.partial(product_kernel, pieces=len(pieces), chunks=len(chunks), final=final),
-        out_shape=[jax.ShapeDtypeStruct(shape, jnp.bfloat16 if final else jnp.float32) for shape in shapes],
+        functools.partial(
+            product_kernel, pieces=len(pieces), chunks=len(chunks), bands=bands, skipped=skipped, only=final, final=final
+        ),
+        out_shape=shapes,
         in_specs=[pl.BlockSpec(memory_space=pltpu.SMEM)] + [hbm] * (len(pieces) + len(chunks)) + [vmem] * final,
         out_specs=[vmem] * len(shapes),
         scratch_shapes=[
+            pltpu.VMEM((rows, tokens), jnp.float32),
             pltpu.VMEM((len(chunks), rows, width), jnp.bfloat16),
             pltpu.VMEM((len(chunks), tokens, width), jnp.bfloat16),
-            pltpu.SemaphoreType.DMA((2, len(chunks))),
+            pltpu.SemaphoreType.DMA((1 + len(bands), len(chunks))),
         ],
-        compiler_params=pltpu.CompilerParams(vmem_limit_bytes=58 << 20),
+        compiler_params=pltpu.CompilerParams(vmem_limit_bytes=(52 if final else 58) << 20),
         cost_estimate=pl.CostEstimate(flops=0, bytes_accessed=0, transcendentals=0),
         name="last_product" if final else "early_product",
     )(where, *pieces, *chunks, *([carried] if final else []))
@@ -286,11 +312,11 @@
         far_head = to_far(src_head)
         aside = shifted(jnp.where(vocab_index < 4, top_edge, bottom_edge), aside_pairs)
         near_head = spread({0: src_head})[1]
-        a1, b1, aside, near_head = fence(a1, b1, aside, near_head)
+        a1, b1, near_head = fence(a1, b1, near_head)
         a2, b2 = lax.ppermute(a1, "vocab", ahead), lax.ppermute(b1, "vocab", behind)
         table_before = shifted(jnp.where(vocab_index == 4, aside, bottom_edge), up_pairs)
         table_after = shifted(jnp.where(vocab_index == 3, aside, top_edge), down_pairs)
-        a2, b2, table_before, table_after = fence(a2, b2, table_before, table_after)
+        a2, b2 = fence(a2, b2)
         a3, b3 = lax.ppermute(a2, "vocab", ahead), lax.ppermute(b2, "vocab", behind)
         new_embed = blend_table(
             local_ids, slot_counts, slot_weights, src_embed, table_before, table_after, aside, side.reshape(1)
@@ -307,8 +333,13 @@
         where = lambda offsets: jnp.stack(
             [jnp.stack([(origin(o) // per) ^ tok_index for o in offsets]), jnp.stack([origin(o) % per for o in offsets])]
         ).astype(jnp.int32)
-        (early,) = add_products(where([0, -1, 1, -2, 2, -3, 3]), pieces, [hidden, a1, b1, a2, b2, a3, b3])
-        source_logits = add_products(where([4]), pieces, [c4], early, (halo, rows - 2 * halo, halo))
+        early_offsets = [0, -1, 1, -2, 2, -3, 3]
+        blocks = [hidden, a1, b1, a2, b2, a3, b3]
+        (early,) = add_products(where(early_offsets), pieces[:3], blocks, [(0, rows)], 3)
+        late = lambda bands: add_products(where(early_offsets + [4]), pieces, blocks + [c4], bands, 3, early)
+        top_logits, bottom_logits = late([(0, halo), (rows - halo, halo)])
+        (middle_logits,) = late([(halo, rows - 2 * halo)])
+        source_logits = [top_logits, middle_logits, bottom_logits]
     else:
         pieces = spread({0: src_head, far: to_far(src_head)})
         whole_head = assembled({held: [(0, piece)] for held, piece in pieces.items()}, 0, rows)

time: 176 us -> 156 us (0.89)
  local copies, waits for them, and re-layouts: 13.2 us -> 3.61 us
  waiting for transfers between devices: 87.7 us -> 79.5 us
  starting transfers between devices: 39.6 us -> 31.8 us
  Pallas kernels: 26.3 us -> 30.6 us
    unnamed x45 -> x19, local copies, waits for them, and re-layouts: 13.1 us -> 3.27 us
    ppermute x1, waiting for transfers between devices: 0.01 us -> 6.76 us  [to_far(): return lax.ppermute(value, 'tok', xor_perm(tok_count, far))]
    ppermute x5, waiting for transfers between devices: 30.3 us -> 24.7 us  [shifted(): return lax.ppermute(value, 'vocab', pairs)]
    ppermute x1, starting transfers between devices: 7.14 us -> 1.63 us  [body(): lax.ppermute(a1, 'vocab', ahead)]
    ppermute x1, waiting for transfers between devices: 4.07 us -> 0.01 us  [body(): lax.ppermute(b2, 'vocab', behind)]
    pallas_call x2 -> x3, Pallas kernels: 17.8 us -> 21.9 us  [add_products(): pl.pallas_call(functools.partial(product_kernel, pieces=len(pieces), chun...]
    ppermute x1, starting transfers between devices: 6.76 us -> 3.15 us  [body(): lax.ppermute(a2, 'vocab', ahead)]
    ppermute x1, waiting for transfers between devices: 7.92 us -> 4.79 us  [body(): lax.ppermute(a2, 'vocab', ahead)]
  transfers between devices with their start and end apart: 18 -> 18, of which waited for: 13 -> 11; matrix products, arithmetic and copies ran while one was open for 4% -> 6% of each run, Pallas kernels for 11% -> 15%
where the time goes in v3:
time: 156 us
  waiting for transfers between devices  79.5 us (51%)
  starting transfers between devices  31.8 us (20%)
  Pallas kernels  30.6 us (20%)
  other arithmetic  9.42 us (6%)
  local copies, waits for them, and re-layouts  3.61 us (2%)
    ppermute x5, waiting for transfers between devices, shifted(): return lax.ppermute(value, 'vocab', pairs)  24.7 us
    pallas_call x3, Pallas kernels, add_products(): pl.pallas_call(functools.partial(product_kernel, pieces=len(pieces), chun...  21.9 us
    ppermute x1, waiting for transfers between devices, body(): lax.ppermute(hidden, 'vocab', ahead)  20.1 us
    ppermute x1, waiting for transfers between devices, body(): lax.ppermute(a1, 'vocab', ahead)  17 us
    ppermute x3, starting transfers between devices, merge_stats(): other = lax.ppermute(stats, axis, xor_perm(count, mask))  9.63 us
    ppermute x5, starting transfers between devices, shifted(): return lax.ppermute(value, 'vocab', pairs)  8.87 us
    ppermute x1, waiting for transfers between devices, to_far(): return lax.ppermute(value, 'tok', xor_perm(tok_count, far))  6.76 us
    pallas_call x1, Pallas kernels, blend_table(): pl.pallas_call(table_kernel, grid=(columns // tile,), out_shape=jax.Shape...  6.71 us
  transfers between devices with their start and end apart: 18, of which 11 were waited for; matrix products, arithmetic and copies ran while one was open for 6% of the time, Pallas kernels for 15%

profile of v3, /device:TPU:0, one launch (start us, length us, event | category | flops | bytes accessed | tf_op | source)
XLA Modules:
  0.0 156.0 jit_solution(16736953066763935031)
XLA Ops:
  1.1 2.6 %collective-permute-start.10 = (bf16[1024,2048]{1,0:T(8,128)(2,1)}, bf16[1024,2048]{1,0:T(8,128)(2,1)}, u32[]{:S(2)}, u32[]{:S(2)}) collective-permute-start(bf16[1024,2048]{1,0:T(8,128)(2,1)} %refs_0_.5), channel_id=1, source_target_pairs={{0,2},{1,3},{2,0},{3,1},{4,6},{5,7},{6,4},{7,5},{8,10},{9,11},{10,... | collective-permute-start | bytes 12582920 | tf_op jit(solution)/shard_map/ppermute | solution.py:274
  3.7 1.6 %collective-permute-start = (bf16[512,1024]{1,0:T(8,128)(2,1)}, bf16[512,1024]{1,0:T(8,128)(2,1)S(1)}, u32[]{:S(2)}, u32[]{:S(2)}) collective-permute-start(bf16[512,1024]{1,0:T(8,128)(2,1)} %refs_4_.3), channel_id=1, source_target_pairs={{0,8},{8,16},{16,24},{24,28},{28,20},{20,12},{12,4},{4,0},{1,9},{9... | collective-permute-start | bytes 3145736 | tf_op jit(solution)/shard_map/ppermute | solution.py:311
  5.8 2.6 %broadcast_select_fusion.2 = bf16[256,2048]{1,0:T(8,128)(2,1)} fusion(pred[]{:T(512)S(6)} %lt.245, bf16[1024,2048]{1,0:T(8,128)(2,1)} %own_ref.1), kind=kLoop, calls=%fused_computation.2 | loop fusion | flops 524288 | bytes 3145729 | tf_op jit(solution)/shard_map/jit(_where)/select_n | solution.py:313
  9.1 20.1 %collective-permute-done.refs_0_ = bf16[512,1024]{1,0:T(8,128)(2,1)S(1)} collective-permute-done((bf16[512,1024]{1,0:T(8,128)(2,1)}, bf16[512,1024]{1,0:T(8,128)(2,1)S(1)}, u32[]{:S(2)}, u32[]{:S(2)}) %collective-permute-start) | collective-permute-done | bytes 1048608 | tf_op jit(solution)/shard_map/ppermute | solution.py:311
  29.2 1.4 collective-permute-done.1.refs_1_
  30.6 1.6 %collective-permute-start.3 = (bf16[512,1024]{1,0:T(8,128)(2,1)}, bf16[512,1024]{1,0:T(8,128)(2,1)}, u32[]{:S(2)}, u32[]{:S(2)}) collective-permute-start(bf16[512,1024]{1,0:T(8,128)(2,1)} %get-tuple-element.13.refs_4_.refs_5_), channel_id=1, source_target_pairs={{0,8},{8,16},{16,24},{24,28},{28,20},{20,12},{12,4},{4,0},{1,9},{9... | collective-permute-start | bytes 3145736 | tf_op jit(solution)/shard_map/ppermute | solution.py:316
  32.7 3.2 %broadcast_select_fusion.1 = (bf16[256,2048]{1,0:T(8,128)(2,1)}, bf16[256,2048]{1,0:T(8,128)(2,1)}) fusion(bf16[256,2048]{1,0:T(8,128)(2,1)S(1)} %collective-permute-done.7.relayed_ref, pred[]{:T(512)S(6)} %eq.93, bf16[1024,2048]{1,0:T(8,128)(2,1)} %own_ref.1, pred[]{:T(512)S(6)} %eq.92), kind=kLoop, calls=%fused_computation.1 | loop fusion | flops 1048576 | bytes 5242882 | tf_op jit(solution)/shard_map/jit(_where)/select_n | solution.py:318
  35.9 2.9 %collective-permute-start.8 = (bf16[256,2048]{1,0:T(8,128)(2,1)}, bf16[256,2048]{1,0:T(8,128)(2,1)S(1)}, u32[]{:S(2)}, u32[]{:S(2)}) collective-permute-start(bf16[256,2048]{1,0:T(8,128)(2,1)} %get-tuple-element.29), channel_id=1, source_target_pairs={{0,4},{4,8},{8,12},{12,16},{16,24},{24,28},{1,5},{5,9},{9,13},{13,... | collective-permute-start | bytes 3145736 | tf_op jit(solution)/shard_map/ppermute | solution.py:236
  38.8 1.3 collective-permute-start.9
  40.1 17.0 %collective-permute-done.3.refs_0_ = bf16[512,1024]{1,0:T(8,128)(2,1)} collective-permute-done((bf16[512,1024]{1,0:T(8,128)(2,1)}, bf16[512,1024]{1,0:T(8,128)(2,1)}, u32[]{:S(2)}, u32[]{:S(2)}) %collective-permute-start.3) | collective-permute-done | bytes 1048608 | tf_op jit(solution)/shard_map/ppermute | solution.py:316
  57.1 3.1 %collective-permute-start.5 = (bf16[512,1024]{1,0:T(8,128)(2,1)}, bf16[512,1024]{1,0:T(8,128)(2,1)}, u32[]{:S(2)}, u32[]{:S(2)}) collective-permute-start(bf16[512,1024]{1,0:T(8,128)(2,1)} %get-tuple-element.15.refs_6_.refs_7_), channel_id=1, source_target_pairs={{0,8},{8,16},{16,24},{24,28},{28,20},{20,12},{12,4},{4,0},{1,9},{9... | collective-permute-start | bytes 3145736 | tf_op jit(solution)/shard_map/ppermute | solution.py:320
  60.3 18.8 %collective-permute-done.8.before_ref = bf16[256,2048]{1,0:T(8,128)(2,1)S(1)} collective-permute-done((bf16[256,2048]{1,0:T(8,128)(2,1)}, bf16[256,2048]{1,0:T(8,128)(2,1)S(1)}, u32[]{:S(2)}, u32[]{:S(2)}) %collective-permute-start.8) | collective-permute-done | bytes 1048608 | tf_op jit(solution)/shard_map/ppermute | solution.py:236
  79.6 2.2 %copy-done = bf16[1024,2048]{1,0:T(8,128)(2,1)S(1)} copy-done((bf16[1024,2048]{1,0:T(8,128)(2,1)S(1)}, bf16[1024,2048]{1,0:T(8,128)(2,1)}, u32[]{:S(2)}) %copy-start) | copy-done | bytes 4194328
  81.8 6.7 %blend_table.1.refs_2_ = bf16[1024,2048]{1,0:T(8,128)(2,1)} custom-call(s32[8,3]{1,0:T(8,128)S(1)} %subtract_clamp_fusion.ids_ref, s32[8]{0:T(128)S(1)} %copy-done.3, s32[1]{0:T(128)} %bitcast.side_ref, bf16[8,3,128,128]{3,2,1,0:T(8,128)(2,1)S(1)} %copy-done.2, bf16[1024,2048]{1,0:T(8,128)(2,1)S(1)} %copy-done, ...), custom_call_target="tpu_custom_call" | custom-call | tf_op jit(solution)/shard_map/blend_table/pallas_call | solution.py:64
  88.5 6.8 %collective-permute-done.10.refs_3_ = bf16[1024,2048]{1,0:T(8,128)(2,1)} collective-permute-done((bf16[1024,2048]{1,0:T(8,128)(2,1)}, bf16[1024,2048]{1,0:T(8,128)(2,1)}, u32[]{:S(2)}, u32[]{:S(2)}) %collective-permute-start.10) | collective-permute-done | bytes 4194336 | tf_op jit(solution)/shard_map/ppermute | solution.py:274
  95.2 4.8 %collective-permute-done.5.refs_0_ = bf16[512,1024]{1,0:T(8,128)(2,1)} collective-permute-done((bf16[512,1024]{1,0:T(8,128)(2,1)}, bf16[512,1024]{1,0:T(8,128)(2,1)}, u32[]{:S(2)}, u32[]{:S(2)}) %collective-permute-start.5) | collective-permute-done | bytes 1048608 | tf_op jit(solution)/shard_map/ppermute | solution.py:320
  100.0 2.3 %broadcast_select_fusion = bf16[512,1024]{1,0:T(8,128)(2,1)} fusion(bf16[512,1024]{1,0:T(8,128)(2,1)} %get-tuple-element.20.refs_8_.refs_9_, bf16[512,1024]{1,0:T(8,128)(2,1)} %get-tuple-element.21.refs_9_.refs_10_, pred[]{:T(512)S(6)} %eq.95), kind=kLoop, calls=%fused_computation | loop fusion | flops 524288 | bytes 3145729 | tf_op jit(solution)/shard_map/jit(_where)/select_n | solution.py:329
  102.3 2.9 %collective-permute-start.12 = (bf16[512,1024]{1,0:T(8,128)(2,1)}, bf16[512,1024]{1,0:T(8,128)(2,1)S(1)}, u32[]{:S(2)}, u32[]{:S(2)}) collective-permute-start(bf16[512,1024]{1,0:T(8,128)(2,1)} %broadcast_select_fusion), channel_id=1, source_target_pairs={{0,8},{8,16},{16,24},{24,28},{28,20},{20,12},{12,4},{4,0},{9,1},{1... | collective-permute-start | bytes 3145736 | tf_op jit(solution)/shard_map/ppermute | solution.py:329
  106.3 12.0 %early_product.1.refs_12_ = f32[1024,512]{1,0:T(8,128)} custom-call(s32[2,7]{1,0:T(2,128)} %pad_add_fusion.1.where_ref, bf16[1024,2048]{1,0:T(8,128)(2,1)} %refs_0_.5, bf16[1024,2048]{1,0:T(8,128)(2,1)} %get-tuple-element.18.refs_1_, bf16[1024,2048]{1,0:T(8,128)(2,1)} %get-tuple-element.19.refs_2_, bf16[512,1024]{1,0:T(8,128)(2,1)} %refs_4_.3, ...), custom_call_target="tpu_custom_call" | custom-call | tf_op jit(solution)/shard_map/early_product/pallas_call | solution.py:196
  118.4 1.0 copy-done.5
  119.4 5.0 %last_product.2 = (bf16[256,512]{1,0:T(8,128)(2,1)S(1)}, bf16[256,512]{1,0:T(8,128)(2,1)S(1)}) custom-call(s32[2,8]{1,0:T(2,128)S(1)} %pad_add_fusion.where_ref, bf16[1024,2048]{1,0:T(8,128)(2,1)} %refs_0_.5, bf16[1024,2048]{1,0:T(8,128)(2,1)} %get-tuple-element.18.refs_1_, bf16[1024,2048]{1,0:T(8,128)(2,1)} %get-tuple-element.19.refs_2_, ...), custom_call_target="tpu_custom_call" | custom-call | tf_op jit(solution)/shard_map/last_product/pallas_call | solution.py:196
  124.3 2.6 %collective-permute-start.13 = (bf16[256,512]{1,0:T(8,128)(2,1)S(1)}, bf16[256,512]{1,0:T(8,128)(2,1)S(1)}, u32[]{:S(2)}, u32[]{:S(2)}) collective-permute-start(bf16[256,512]{1,0:T(8,128)(2,1)S(1)} %get-tuple-element.22.refs_3_), channel_id=1, source_target_pairs={{0,4},{4,8},{8,12},{12,16},{16,20},{20,24},{24,28},{1,5},{5,9},{9,... | collective-permute-start | bytes 786440 | tf_op jit(solution)/shard_map/ppermute | solution.py:236
  127.0 1.3 collective-permute-start.14
  128.3 4.9 %last_product.3.refs_2_ = bf16[512,512]{1,0:T(8,128)(2,1)S(1)} custom-call(s32[2,8]{1,0:T(2,128)S(1)} %pad_add_fusion.where_ref, bf16[1024,2048]{1,0:T(8,128)(2,1)} %refs_0_.5, bf16[1024,2048]{1,0:T(8,128)(2,1)} %get-tuple-element.18.refs_1_, bf16[1024,2048]{1,0:T(8,128)(2,1)} %get-tuple-element.19.refs_2_, ...), custom_call_target="tpu_custom_call" | custom-call | tf_op jit(solution)/shard_map/last_product/pallas_call | solution.py:196
  133.2 5.4 %collective-permute-done.13.refs_0_ = bf16[256,512]{1,0:T(8,128)(2,1)S(1)} collective-permute-done((bf16[256,512]{1,0:T(8,128)(2,1)S(1)}, bf16[256,512]{1,0:T(8,128)(2,1)S(1)}, u32[]{:S(2)}, u32[]{:S(2)}) %collective-permute-start.13) | collective-permute-done | bytes 262176 | tf_op jit(solution)/shard_map/ppermute | solution.py:236
  138.7 2.0 %blend_stats.1 = f32[3,512]{1,0:T(4,128)S(1)} custom-call(s32[8,3]{1,0:T(8,128)S(1)} %subtract_clamp_fusion.ids_ref, s32[8]{0:T(128)S(1)} %copy-done.3, bf16[8,3,128,128]{3,2,1,0:T(8,128)(2,1)S(1)} %copy-done.2, bf16[256,512]{1,0:T(8,128)(2,1)S(1)} %collective-permute-done.13.refs_0_, bf16[256,512]{1,0:T(8,128)(2,1)S(1)} %get-tuple-element.23.refs_1_, ...), custom_call_target="tpu_custom_call" | custom-call | flops 402653184 | bytes 1572864 | tf_op jit(solution)/shard_map/blend_stats/pallas_call | solution.py:111
  140.7 2.5 %collective-permute-start.15 = (f32[3,512]{1,0:T(4,128)S(1)}, f32[3,512]{1,0:T(4,128)S(1)}, u32[]{:S(2)}, u32[]{:S(2)}) collective-permute-start(f32[3,512]{1,0:T(4,128)S(1)} %blend_stats.1), channel_id=1, source_target_pairs={{0,4},{4,0},{8,12},{12,8},{16,20},{20,16},{24,28},{28,24},{1,5},{5... | collective-permute-start | bytes 18440 | tf_op jit(solution)/shard_map/ppermute | solution.py:244
  143.2 1.6 %collective-permute-done.15 = f32[3,512]{1,0:T(4,128)S(1)} collective-permute-done((f32[3,512]{1,0:T(4,128)S(1)}, f32[3,512]{1,0:T(4,128)S(1)}, u32[]{:S(2)}, u32[]{:S(2)}) %collective-permute-start.15) | collective-permute-done | bytes 6176 | tf_op jit(solution)/shard_map/ppermute | solution.py:244
  144.9 3.4 %collective-permute-start.16 = (f32[3,512]{1,0:T(4,128)S(1)}, f32[3,512]{1,0:T(4,128)S(1)}, u32[]{:S(2)}, u32[]{:S(2)}) collective-permute-start(f32[3,512]{1,0:T(4,128)S(1)} %pad_maximum_fusion), channel_id=1, source_target_pairs={{0,8},{4,12},{8,0},{12,4},{16,24},{20,28},{24,16},{28,20},{1,9},{5... | collective-permute-start | bytes 18440 | tf_op jit(solution)/shard_map/ppermute | solution.py:244
  148.3 1.6 %collective-permute-done.16 = f32[3,512]{1,0:T(4,128)S(1)} collective-permute-done((f32[3,512]{1,0:T(4,128)S(1)}, f32[3,512]{1,0:T(4,128)S(1)}, u32[]{:S(2)}, u32[]{:S(2)}) %collective-permute-start.16) | collective-permute-done | bytes 6176 | tf_op jit(solution)/shard_map/ppermute | solution.py:244
  150.0 3.7 %collective-permute-start.17 = (f32[3,512]{1,0:T(4,128)S(1)}, f32[3,512]{1,0:T(4,128)S(1)}, u32[]{:S(2)}, u32[]{:S(2)}) collective-permute-start(f32[3,512]{1,0:T(4,128)S(1)} %pad_maximum_fusion.1), channel_id=1, source_target_pairs={{0,16},{4,20},{8,24},{12,28},{16,0},{20,4},{24,8},{28,12},{1,17},{... | collective-permute-start | bytes 18440 | tf_op jit(solution)/shard_map/ppermute | solution.py:244
  153.7 1.6 %collective-permute-done.17 = f32[3,512]{1,0:T(4,128)S(1)} collective-permute-done((f32[3,512]{1,0:T(4,128)S(1)}, f32[3,512]{1,0:T(4,128)S(1)}, u32[]{:S(2)}, u32[]{:S(2)}) %collective-permute-start.17) | collective-permute-done | bytes 6176 | tf_op jit(solution)/shard_map/ppermute | solution.py:244
  (51 shorter events, 4.4 us)
Async XLA Ops:
  0.6 30.0 %collective-permute-start.2 = (bf16[1024,2048]{1,0:T(8,128)(2,1)}, bf16[1024,2048]{1,0:T(8,128)(2,1)}, u32[]{:S(2)}, u32[]{:S(2)}) collective-permute-start(bf16[1024,2048]{1,0:T(8,128)(2,1)} %refs_0_.5), channel_id=1, source_target_pairs={{0,1},{1,0},{2,3},{3,2},{4,5},{5,4},{6,7},{7,6},{8,9},{9,8},{10,11... | collective-permute-start | bytes 12582920 | tf_op jit(solution)/shard_map/ppermute | solution.py:279
  1.1 94.1 %collective-permute-start.10 = (bf16[1024,2048]{1,0:T(8,128)(2,1)}, bf16[1024,2048]{1,0:T(8,128)(2,1)}, u32[]{:S(2)}, u32[]{:S(2)}) collective-permute-start(bf16[1024,2048]{1,0:T(8,128)(2,1)} %refs_0_.5), channel_id=1, source_target_pairs={{0,2},{1,3},{2,0},{3,1},{4,6},{5,7},{6,4},{7,5},{8,10},{9,11},{10,... | collective-permute-start | bytes 12582920 | tf_op jit(solution)/shard_map/ppermute | solution.py:274
  3.7 25.4 %collective-permute-start = (bf16[512,1024]{1,0:T(8,128)(2,1)}, bf16[512,1024]{1,0:T(8,128)(2,1)S(1)}, u32[]{:S(2)}, u32[]{:S(2)}) collective-permute-start(bf16[512,1024]{1,0:T(8,128)(2,1)} %refs_4_.3), channel_id=1, source_target_pairs={{0,8},{8,16},{16,24},{24,28},{28,20},{20,12},{12,4},{4,0},{1,9},{9... | collective-permute-start | bytes 3145736 | tf_op jit(solution)/shard_map/ppermute | solution.py:311
  5.3 25.3 %collective-permute-start.1 = (bf16[512,1024]{1,0:T(8,128)(2,1)}, bf16[512,1024]{1,0:T(8,128)(2,1)}, u32[]{:S(2)}, u32[]{:S(2)}) collective-permute-start(bf16[512,1024]{1,0:T(8,128)(2,1)} %refs_4_.3), channel_id=1, source_target_pairs={{8,0},{16,8},{24,16},{28,24},{20,28},{12,20},{4,12},{0,4},{9,1},{1... | collective-permute-start | bytes 3145736 | tf_op jit(solution)/shard_map/ppermute | solution.py:311
  8.4 24.3 %collective-permute-start.7 = (bf16[256,2048]{1,0:T(8,128)(2,1)}, bf16[256,2048]{1,0:T(8,128)(2,1)S(1)}, u32[]{:S(2)}, u32[]{:S(2)}) collective-permute-start(bf16[256,2048]{1,0:T(8,128)(2,1)} %broadcast_select_fusion.2), channel_id=1, source_target_pairs={{8,12},{12,8},{16,20},{20,16},{9,13},{13,9},{17,21},{21,17},{10,14... | collective-permute-start | bytes 3145736 | tf_op jit(solution)/shard_map/ppermute | solution.py:236
  29.2 1.4 copy-start.4
  30.6 29.7 %copy-start.6 = (s32[8,3]{0,1:T(4,128)S(1)}, s32[8,3]{0,1:T(4,128)}, u32[]{:S(2)}) copy-start(s32[8,3]{0,1:T(4,128)} %param.10) | copy-start | bytes 292
  30.6 49.0 %copy-start.2 = (bf16[8,3,128,128]{3,2,1,0:T(8,128)(2,1)S(1)}, bf16[8,3,128,128]{3,2,1,0:T(8,128)(2,1)}, u32[]{:S(2)}) copy-start(bf16[8,3,128,128]{3,2,1,0:T(8,128)(2,1)} %weights_ref.3) | copy-start | bytes 2359300
  30.6 49.0 %copy-start.3 = (s32[8]{0:T(128)S(1)}, s32[8]{0:T(128)}, u32[]{:S(2)}) copy-start(s32[8]{0:T(128)} %counts_ref.3) | copy-start | bytes 100
  30.6 26.5 %collective-permute-start.3 = (bf16[512,1024]{1,0:T(8,128)(2,1)}, bf16[512,1024]{1,0:T(8,128)(2,1)}, u32[]{:S(2)}, u32[]{:S(2)}) collective-permute-start(bf16[512,1024]{1,0:T(8,128)(2,1)} %get-tuple-element.13.refs_4_.refs_5_), channel_id=1, source_target_pairs={{0,8},{8,16},{16,24},{24,28},{28,20},{20,12},{12,4},{4,0},{1,9},{9... | collective-permute-start | bytes 3145736 | tf_op jit(solution)/shard_map/ppermute | solution.py:316
  32.3 24.8 %collective-permute-start.4 = (bf16[512,1024]{1,0:T(8,128)(2,1)}, bf16[512,1024]{1,0:T(8,128)(2,1)}, u32[]{:S(2)}, u32[]{:S(2)}) collective-permute-start(bf16[512,1024]{1,0:T(8,128)(2,1)} %get-tuple-element.14.refs_5_.refs_6_), channel_id=1, source_target_pairs={{8,0},{16,8},{24,16},{28,24},{20,28},{12,20},{4,12},{0,4},{9,1},{1... | collective-permute-start | bytes 3145736 | tf_op jit(solution)/shard_map/ppermute | solution.py:316
  35.9 43.2 %collective-permute-start.8 = (bf16[256,2048]{1,0:T(8,128)(2,1)}, bf16[256,2048]{1,0:T(8,128)(2,1)S(1)}, u32[]{:S(2)}, u32[]{:S(2)}) collective-permute-start(bf16[256,2048]{1,0:T(8,128)(2,1)} %get-tuple-element.29), channel_id=1, source_target_pairs={{0,4},{4,8},{8,12},{12,16},{16,24},{24,28},{1,5},{5,9},{9,13},{13,... | collective-permute-start | bytes 3145736 | tf_op jit(solution)/shard_map/ppermute | solution.py:236
  38.8 40.7 %collective-permute-start.9 = (bf16[256,2048]{1,0:T(8,128)(2,1)}, bf16[256,2048]{1,0:T(8,128)(2,1)}, u32[]{:S(2)}, u32[]{:S(2)}) collective-permute-start(bf16[256,2048]{1,0:T(8,128)(2,1)} %get-tuple-element.28), channel_id=1, source_target_pairs={{4,0},{12,4},{16,12},{20,16},{24,20},{28,24},{5,1},{13,5},{17,13},... | collective-permute-start | bytes 3145736 | tf_op jit(solution)/shard_map/ppermute | solution.py:236
  57.1 42.9 %collective-permute-start.5 = (bf16[512,1024]{1,0:T(8,128)(2,1)}, bf16[512,1024]{1,0:T(8,128)(2,1)}, u32[]{:S(2)}, u32[]{:S(2)}) collective-permute-start(bf16[512,1024]{1,0:T(8,128)(2,1)} %get-tuple-element.15.refs_6_.refs_7_), channel_id=1, source_target_pairs={{0,8},{8,16},{16,24},{24,28},{28,20},{20,12},{12,4},{4,0},{1,9},{9... | collective-permute-start | bytes 3145736 | tf_op jit(solution)/shard_map/ppermute | solution.py:320
  60.2 39.8 %collective-permute-start.6 = (bf16[512,1024]{1,0:T(8,128)(2,1)}, bf16[512,1024]{1,0:T(8,128)(2,1)}, u32[]{:S(2)}, u32[]{:S(2)}) collective-permute-start(bf16[512,1024]{1,0:T(8,128)(2,1)} %get-tuple-element.16.refs_7_.refs_8_), channel_id=1, source_target_pairs={{8,0},{16,8},{24,16},{28,24},{20,28},{12,20},{4,12},{0,4},{9,1},{1... | collective-permute-start | bytes 3145736 | tf_op jit(solution)/shard_map/ppermute | solution.py:320
  79.6 2.2 %copy-start = (bf16[1024,2048]{1,0:T(8,128)(2,1)S(1)}, bf16[1024,2048]{1,0:T(8,128)(2,1)}, u32[]{:S(2)}) copy-start(bf16[1024,2048]{1,0:T(8,128)(2,1)} %own_ref.1) | copy-start | bytes 12582916
  100.0 18.4 %collective-permute-start.11 = (bf16[1024,2048]{1,0:T(8,128)(2,1)}, bf16[1024,2048]{1,0:T(8,128)(2,1)}, u32[]{:S(2)}, u32[]{:S(2)}) collective-permute-start(bf16[1024,2048]{1,0:T(8,128)(2,1)} %get-tuple-element.19.refs_2_), channel_id=1, source_target_pairs={{0,1},{1,0},{2,3},{3,2},{4,5},{5,4},{6,7},{7,6},{8,9},{9,8},{10,11... | collective-permute-start | bytes 12582920 | tf_op jit(solution)/shard_map/ppermute | solution.py:279
  102.3 16.0 %collective-permute-start.12 = (bf16[512,1024]{1,0:T(8,128)(2,1)}, bf16[512,1024]{1,0:T(8,128)(2,1)S(1)}, u32[]{:S(2)}, u32[]{:S(2)}) collective-permute-start(bf16[512,1024]{1,0:T(8,128)(2,1)} %broadcast_select_fusion), channel_id=1, source_target_pairs={{0,8},{8,16},{16,24},{24,28},{28,20},{20,12},{12,4},{4,0},{9,1},{1... | collective-permute-start | bytes 3145736 | tf_op jit(solution)/shard_map/ppermute | solution.py:329
  106.3 13.1 %copy-start.1 = (bf16[512,1024]{1,0:T(8,128)(2,1)S(1)}, bf16[512,1024]{1,0:T(8,128)(2,1)}, u32[]{:S(2)}) copy-start(bf16[512,1024]{1,0:T(8,128)(2,1)} %refs_4_.3) | copy-start | bytes 3145732
  118.4 9.9 %copy-start.8 = (s32[512]{0:T(512)S(1)}, s32[512]{0:T(512)}, u32[]{:S(2)}) copy-start(s32[512]{0:T(512)} %param.14) | copy-start | bytes 6148
  118.4 1.0 copy-start.5
  124.3 14.3 %collective-permute-start.13 = (bf16[256,512]{1,0:T(8,128)(2,1)S(1)}, bf16[256,512]{1,0:T(8,128)(2,1)S(1)}, u32[]{:S(2)}, u32[]{:S(2)}) collective-permute-start(bf16[256,512]{1,0:T(8,128)(2,1)S(1)} %get-tuple-element.22.refs_3_), channel_id=1, source_target_pairs={{0,4},{4,8},{8,12},{12,16},{16,20},{20,24},{24,28},{1,5},{5,9},{9,... | collective-permute-start | bytes 786440 | tf_op jit(solution)/shard_map/ppermute | solution.py:236
  127.0 11.7 %collective-permute-start.14 = (bf16[256,512]{1,0:T(8,128)(2,1)S(1)}, bf16[256,512]{1,0:T(8,128)(2,1)S(1)}, u32[]{:S(2)}, u32[]{:S(2)}) collective-permute-start(bf16[256,512]{1,0:T(8,128)(2,1)S(1)} %get-tuple-element.23.refs_1_), channel_id=1, source_target_pairs={{4,0},{8,4},{12,8},{16,12},{20,16},{24,20},{28,24},{5,1},{9,5},{13... | collective-permute-start | bytes 786440 | tf_op jit(solution)/shard_map/ppermute | solution.py:236
  128.3 27.1 %copy-start.7 = (s32[512]{0:T(512)S(1)}, s32[512]{0:T(512)}, u32[]{:S(2)}) copy-start(s32[512]{0:T(512)} %param.15) | copy-start | bytes 6148
  140.7 4.2 %collective-permute-start.15 = (f32[3,512]{1,0:T(4,128)S(1)}, f32[3,512]{1,0:T(4,128)S(1)}, u32[]{:S(2)}, u32[]{:S(2)}) collective-permute-start(f32[3,512]{1,0:T(4,128)S(1)} %blend_stats.1), channel_id=1, source_target_pairs={{0,4},{4,0},{8,12},{12,8},{16,20},{20,16},{24,28},{28,24},{1,5},{5... | collective-permute-start | bytes 18440 | tf_op jit(solution)/shard_map/ppermute | solution.py:244
  144.9 5.0 %collective-permute-start.16 = (f32[3,512]{1,0:T(4,128)S(1)}, f32[3,512]{1,0:T(4,128)S(1)}, u32[]{:S(2)}, u32[]{:S(2)}) collective-permute-start(f32[3,512]{1,0:T(4,128)S(1)} %pad_maximum_fusion), channel_id=1, source_target_pairs={{0,8},{4,12},{8,0},{12,4},{16,24},{20,28},{24,16},{28,20},{1,9},{5... | collective-permute-start | bytes 18440 | tf_op jit(solution)/shard_map/ppermute | solution.py:244
  150.0 5.3 %collective-permute-start.17 = (f32[3,512]{1,0:T(4,128)S(1)}, f32[3,512]{1,0:T(4,128)S(1)}, u32[]{:S(2)}, u32[]{:S(2)}) collective-permute-start(f32[3,512]{1,0:T(4,128)S(1)} %pad_maximum_fusion.1), channel_id=1, source_target_pairs={{0,16},{4,20},{8,24},{12,28},{16,0},{20,4},{24,8},{28,12},{1,17},{... | collective-permute-start | bytes 18440 | tf_op jit(solution)/shard_map/ppermute | solution.py:244

commit v4 on v3

--- a/solution.py
+++ b/solution.py
@@ -125,65 +125,64 @@
     )(ids, counts, weights, *source, goals)
 
 
-def product_kernel(where_ref, *refs, pieces, chunks, bands, skipped, only, final):
+def product_kernel(where_ref, *refs, pieces, chunks, bands, final):
     piece_refs, refs = refs[:pieces], refs[pieces:]
     chunk_refs, refs = refs[:chunks], refs[chunks:]
     carried_ref, refs = (refs[0], refs[1:]) if final else (None, refs)
     out_refs, (total, held, block, sems) = refs[:-4], refs[-4:]
     width = held.shape[2]
+    rows_at = [sum(size for _, size in bands[:band]) for band in range(len(bands))]
 
     def copies(at, piece_ref):
         start = pl.multiple_of(where_ref[1, at] * width, width)
-        row = 0
         for band, (first, size) in enumerate(bands):
             yield pltpu.make_async_copy(
                 piece_ref.at[pl.ds(first, size), pl.ds(start, width)],
-                held.at[at, pl.ds(row, size), :],
+                held.at[at, pl.ds(rows_at[band], size), :],
                 sems.at[1 + band, at],
             )
-            row += size
 
     def block_copy(at):
         return pltpu.make_async_copy(chunk_refs[at], block.at[at], sems.at[0, at])
 
-    def wanted(at):
-        if only and at == chunks - 1:
-            return where_ref[0, at] >= 0
-        return (where_ref[0, at] == skipped) if only else (where_ref[0, at] != skipped)
-
+    def carried_copies():
+        for band, (first, size) in enumerate(bands):
+            yield pltpu.make_async_copy(
+                carried_ref.at[pl.ds(first, size), :], total.at[pl.ds(rows_at[band], size), :], sems.at[1 + band, chunks]
+            )
+
+    if final:
+        for copy in carried_copies():
+            copy.start()
+    else:
+        total[...] = jnp.zeros_like(total)
     for at in range(chunks):
-        @pl.when(wanted(at))
+        @pl.when(where_ref[2, at] == 1)
         def _(at=at):
             block_copy(at).start()
 
         for piece, piece_ref in enumerate(piece_refs):
-            @pl.when(wanted(at) & (where_ref[0, at] == piece))
+            @pl.when((where_ref[2, at] == 1) & (where_ref[0, at] == piece))
             def _(at=at, piece_ref=piece_ref):
                 for copy in copies(at, piece_ref):
                     copy.start()
 
     if final:
-        row = 0
-        for first, size in bands:
-            total[pl.ds(row, size), :] = carried_ref[pl.ds(first, size), :]
-            row += size
-    else:
-        total[...] = jnp.zeros_like(total)
+        for copy in carried_copies():
+            copy.wait()
     for at in range(chunks):
-        @pl.when(wanted(at))
+        @pl.when(where_ref[2, at] == 1)
         def _(at=at):
             block_copy(at).wait()
             for copy in copies(at, piece_refs[0]):
                 copy.wait()
             total[...] += lax.dot_general(held[at], block[at], CONTRACT_LAST, preferred_element_type=jnp.float32)
 
-    row = 0
-    for out_ref in out_refs:
+    for out_ref, row in zip(out_refs, rows_at):
         out_ref[...] = total[pl.ds(row, out_ref.shape[0]), :].astype(out_ref.dtype)
-        row += out_ref.shape[0]
-
-
-def add_products(where, pieces, chunks, bands, skipped, carried=None):
+
+
+def add_products(where, pieces, chunks, bands, carried=None):
     tokens, width = chunks[0].shape
     rows = sum(size for _, size in bands)
     final = carried is not None
@@ -194,17 +193,15 @@
     else:
         shapes = [jax.ShapeDtypeStruct((rows, tokens), jnp.float32)]
     return pl.pallas_call(
-        functools.partial(
-            product_kernel, pieces=len(pieces), chunks=len(chunks), bands=bands, skipped=skipped, only=final, final=final
-        ),
+        functools.partial(product_kernel, pieces=len(pieces), chunks=len(chunks), bands=bands, final=final),
         out_shape=shapes,
-        in_specs=[pl.BlockSpec(memory_space=pltpu.SMEM)] + [hbm] * (len(pieces) + len(chunks)) + [vmem] * final,
+        in_specs=[pl.BlockSpec(memory_space=pltpu.SMEM)] + [hbm] * (len(pieces) + len(chunks) + final),
         out_specs=[vmem] * len(shapes),
         scratch_shapes=[
             pltpu.VMEM((rows, tokens), jnp.float32),
             pltpu.VMEM((len(chunks), rows, width), jnp.bfloat16),
             pltpu.VMEM((len(chunks), tokens, width), jnp.bfloat16),
-            pltpu.SemaphoreType.DMA((1 + len(bands), len(chunks))),
+            pltpu.SemaphoreType.DMA((1 + len(bands), len(chunks) + 1)),
         ],
         compiler_params=pltpu.CompilerParams(vmem_limit_bytes=(52 if final else 58) << 20),
         cost_estimate=pl.CostEstimate(flops=0, bytes_accessed=0, transcendentals=0),
@@ -239,16 +236,21 @@
 def merge_stats(stats, axis):
     count = lax.axis_size(axis)
     index = lax.axis_index(axis)
-    mask = 1
-    while mask < count:
-        other = lax.ppermute(stats, axis, xor_perm(count, mask))
-        upper = (index & mask) != 0
-        first = jnp.where(upper, other, stats)
-        second = jnp.where(upper, stats, other)
-        peak = jnp.maximum(first[0], second[0])
-        total = first[1] * jnp.exp(first[0] - peak) + second[1] * jnp.exp(second[0] - peak)
-        stats = jnp.stack([peak, total, first[2] + second[2]])
-        mask *= 2
+    low = 1
+    while low < count:
+        group = min(4, count // low)
+        place = (index // low) % group
+        got = [stats] + [lax.ppermute(stats, axis, xor_perm(count, low * mask)) for mask in range(1, group)]
+        ordered = []
+        for at in range(group):
+            value = got[0]
+            for mask in range(1, group):
+                value = jnp.where((place ^ mask) == at, got[mask], value)
+            ordered.append(value)
+        peak = functools.reduce(jnp.maximum, [value[0] for value in ordered])
+        total = sum(value[1] * jnp.exp(value[0] - peak) for value in ordered)
+        stats = jnp.stack([peak, total, sum(value[2] for value in ordered)])
+        low *= group
     return stats
 
 
@@ -322,21 +324,25 @@
             local_ids, slot_counts, slot_weights, src_embed, table_before, table_after, aside, side.reshape(1)
         )
         a3, b3, new_embed, far_head = fence(a3, b3, new_embed, far_head)
-        even = tok_index % 2 == 0
-        last_pairs = [
-            (i * tok_count + t, j * tok_count + t) for t in range(tok_count) for i, j in (behind if t % 2 else ahead)
-        ]
-        c4 = lax.ppermute(jnp.where(even, a3, b3), ("vocab", "tok"), last_pairs)
+        def some(pairs, parity):
+            return [(i * tok_count + t, j * tok_count + t) for t in range(parity, tok_count, 2) for i, j in pairs]
+
+        even = (tok_index % 2 == 0).astype(jnp.int32)
+        a4 = lax.ppermute(a3, ("vocab", "tok"), some(ahead, 0))
+        b4 = lax.ppermute(b3, ("vocab", "tok"), some(behind, 1))
         far_near_head = spread({far: far_head})[far | 1]
         pieces = [src_head, near_head, far_head, far_near_head]
         per = count // tok_count
-        where = lambda offsets: jnp.stack(
-            [jnp.stack([(origin(o) // per) ^ tok_index for o in offsets]), jnp.stack([origin(o) % per for o in offsets])]
-        ).astype(jnp.int32)
-        early_offsets = [0, -1, 1, -2, 2, -3, 3]
+        offsets = [0, -1, 1, -2, 2, -3, 3, 4, 4]
+        origins = jnp.stack([origin(offset) for offset in offsets]).astype(jnp.int32)
+        piece_of = (origins // per) ^ tok_index
+        late_piece = (piece_of == 3).astype(jnp.int32)
+        wanted = jnp.concatenate([late_piece[:7], jnp.stack([even, 1 - even])])
+        early_where = jnp.stack([piece_of, origins % per, 1 - late_piece])[:, :7]
+        late_where = jnp.stack([piece_of, origins % per, wanted])
         blocks = [hidden, a1, b1, a2, b2, a3, b3]
-        (early,) = add_products(where(early_offsets), pieces[:3], blocks, [(0, rows)], 3)
-        late = lambda bands: add_products(where(early_offsets + [4]), pieces, blocks + [c4], bands, 3, early)
+        (early,) = add_products(early_where, pieces[:3], blocks, [(0, rows)])
+        late = lambda bands: add_products(late_where, pieces, blocks + [a4, b4], bands, early)
         top_logits, bottom_logits = late([(0, halo), (rows - halo, halo)])
         (middle_logits,) = late([(halo, rows - 2 * halo)])
         source_logits = [top_logits, middle_logits, bottom_logits]

time: 156 us -> 153 us (0.981)
  other arithmetic: 9.42 us -> 7.19 us
    ppermute x4 -> x6, starting transfers between devices: 12.5 us -> 14.9 us  [the longest x4 8.45 us: merge_stats(): lax.ppermute(stats, axis, xor_perm(count, low * mask))]
    select_n x4 -> x2, other arithmetic: 2.35 us -> 0.03 us  [merge_stats(): value = jnp.where(place ^ mask == at, got[mask], value)]
    ppermute x4 -> x6, waiting for transfers between devices: 4.89 us -> 4.16 us  [the longest x4 4.15 us: merge_stats(): lax.ppermute(stats, axis, xor_perm(count, low * mask))]
  transfers between devices with their start and end apart: 18 -> 20, of which waited for: 11 -> 11; matrix products, arithmetic and copies ran while one was open for 6% -> 4% of each run, Pallas kernels for 15% -> 15%
where the time goes in v4:
time: 153 us
  waiting for transfers between devices  79 us (52%)
  starting transfers between devices  32.8 us (21%)
  Pallas kernels  29.2 us (19%)
  other arithmetic  7.19 us (5%)
  local copies, waits for them, and re-layouts  3.43 us (2%)
    ppermute x5, waiting for transfers between devices, shifted(): return lax.ppermute(value, 'vocab', pairs)  24.9 us
    pallas_call x3, Pallas kernels, add_products(): pl.pallas_call(functools.partial(product_kernel, pieces=len(pieces), chun...  20.5 us
    ppermute x1, waiting for transfers between devices, body(): lax.ppermute(hidden, 'vocab', ahead)  20.1 us
    ppermute x1, waiting for transfers between devices, body(): lax.ppermute(a1, 'vocab', ahead)  17 us
    ppermute x4, starting transfers between devices, merge_stats(): lax.ppermute(stats, axis, xor_perm(count, low * mask))  8.45 us
    ppermute x5, starting transfers between devices, shifted(): return lax.ppermute(value, 'vocab', pairs)  7.55 us
    ppermute x1, waiting for transfers between devices, to_far(): return lax.ppermute(value, 'tok', xor_perm(tok_count, far))  6.76 us
    pallas_call x1, Pallas kernels, blend_table(): pl.pallas_call(table_kernel, grid=(columns // tile,), out_shape=jax.Shape...  6.71 us
  transfers between devices with their start and end apart: 20, of which 11 were waited for; matrix products, arithmetic and copies ran while one was open for 4% of the time, Pallas kernels for 15%

profile of v4, /device:TPU:0, one launch (start us, length us, event | category | flops | bytes accessed | tf_op | source)
XLA Modules:
  0.0 152.5 jit_solution(13452674514295953701)
XLA Ops:
  1.1 2.6 %collective-permute-start.10 = (bf16[1024,2048]{1,0:T(8,128)(2,1)}, bf16[1024,2048]{1,0:T(8,128)(2,1)}, u32[]{:S(2)}, u32[]{:S(2)}) collective-permute-start(bf16[1024,2048]{1,0:T(8,128)(2,1)} %refs_0_.5), channel_id=1, source_target_pairs={{0,2},{1,3},{2,0},{3,1},{4,6},{5,7},{6,4},{7,5},{8,10},{9,11},{10,... | collective-permute-start | bytes 12582920 | tf_op jit(solution)/shard_map/ppermute | solution.py:276
  3.7 1.6 %collective-permute-start = (bf16[512,1024]{1,0:T(8,128)(2,1)}, bf16[512,1024]{1,0:T(8,128)(2,1)S(1)}, u32[]{:S(2)}, u32[]{:S(2)}) collective-permute-start(bf16[512,1024]{1,0:T(8,128)(2,1)} %refs_4_.3), channel_id=1, source_target_pairs={{0,8},{8,16},{16,24},{24,28},{28,20},{20,12},{12,4},{4,0},{1,9},{9... | collective-permute-start | bytes 3145736 | tf_op jit(solution)/shard_map/ppermute | solution.py:313
  5.8 2.6 %broadcast_select_fusion.1 = bf16[256,2048]{1,0:T(8,128)(2,1)} fusion(pred[]{:T(512)S(6)} %lt.88, bf16[1024,2048]{1,0:T(8,128)(2,1)} %own_ref.1), kind=kLoop, calls=%fused_computation.1 | loop fusion | flops 524288 | bytes 3145729 | tf_op jit(solution)/shard_map/jit(_where)/select_n | solution.py:315
  8.4 0.7 collective-permute-start.7
  9.1 20.1 %collective-permute-done.refs_0_ = bf16[512,1024]{1,0:T(8,128)(2,1)S(1)} collective-permute-done((bf16[512,1024]{1,0:T(8,128)(2,1)}, bf16[512,1024]{1,0:T(8,128)(2,1)S(1)}, u32[]{:S(2)}, u32[]{:S(2)}) %collective-permute-start) | collective-permute-done | bytes 1048608 | tf_op jit(solution)/shard_map/ppermute | solution.py:313
  29.2 1.4 collective-permute-done.1.refs_1_
  30.6 1.6 %collective-permute-start.3 = (bf16[512,1024]{1,0:T(8,128)(2,1)}, bf16[512,1024]{1,0:T(8,128)(2,1)}, u32[]{:S(2)}, u32[]{:S(2)}) collective-permute-start(bf16[512,1024]{1,0:T(8,128)(2,1)} %get-tuple-element.13.refs_4_.refs_5_), channel_id=1, source_target_pairs={{0,8},{8,16},{16,24},{24,28},{28,20},{20,12},{12,4},{4,0},{1,9},{9... | collective-permute-start | bytes 3145736 | tf_op jit(solution)/shard_map/ppermute | solution.py:318
  32.7 3.2 %broadcast_select_fusion = (bf16[256,2048]{1,0:T(8,128)(2,1)}, bf16[256,2048]{1,0:T(8,128)(2,1)}) fusion(bf16[256,2048]{1,0:T(8,128)(2,1)S(1)} %collective-permute-done.7.relayed_ref, pred[]{:T(512)S(6)} %eq.92, bf16[1024,2048]{1,0:T(8,128)(2,1)} %own_ref.1, pred[]{:T(512)S(6)} %eq.91), kind=kLoop, calls=%fused_computation | loop fusion | flops 1048576 | bytes 5242882 | tf_op jit(solution)/shard_map/jit(_where)/select_n | solution.py:320
  35.9 2.9 %collective-permute-start.8 = (bf16[256,2048]{1,0:T(8,128)(2,1)}, bf16[256,2048]{1,0:T(8,128)(2,1)S(1)}, u32[]{:S(2)}, u32[]{:S(2)}) collective-permute-start(bf16[256,2048]{1,0:T(8,128)(2,1)} %get-tuple-element.29), channel_id=1, source_target_pairs={{0,4},{4,8},{8,12},{12,16},{16,24},{24,28},{1,5},{5,9},{9,13},{13,... | collective-permute-start | bytes 3145736 | tf_op jit(solution)/shard_map/ppermute | solution.py:233
  38.8 1.3 collective-permute-start.9
  40.1 17.0 %collective-permute-done.3.refs_0_ = bf16[512,1024]{1,0:T(8,128)(2,1)} collective-permute-done((bf16[512,1024]{1,0:T(8,128)(2,1)}, bf16[512,1024]{1,0:T(8,128)(2,1)}, u32[]{:S(2)}, u32[]{:S(2)}) %collective-permute-start.3) | collective-permute-done | bytes 1048608 | tf_op jit(solution)/shard_map/ppermute | solution.py:318
  57.1 3.1 %collective-permute-start.5 = (bf16[512,1024]{1,0:T(8,128)(2,1)}, bf16[512,1024]{1,0:T(8,128)(2,1)}, u32[]{:S(2)}, u32[]{:S(2)}) collective-permute-start(bf16[512,1024]{1,0:T(8,128)(2,1)} %get-tuple-element.15.refs_6_.refs_7_), channel_id=1, source_target_pairs={{0,8},{8,16},{16,24},{24,28},{28,20},{20,12},{12,4},{4,0},{1,9},{9... | collective-permute-start | bytes 3145736 | tf_op jit(solution)/shard_map/ppermute | solution.py:322
  60.3 18.8 %collective-permute-done.8.before_ref = bf16[256,2048]{1,0:T(8,128)(2,1)S(1)} collective-permute-done((bf16[256,2048]{1,0:T(8,128)(2,1)}, bf16[256,2048]{1,0:T(8,128)(2,1)S(1)}, u32[]{:S(2)}, u32[]{:S(2)}) %collective-permute-start.8) | collective-permute-done | bytes 1048608 | tf_op jit(solution)/shard_map/ppermute | solution.py:233
  79.6 2.2 %copy-done = bf16[1024,2048]{1,0:T(8,128)(2,1)S(1)} copy-done((bf16[1024,2048]{1,0:T(8,128)(2,1)S(1)}, bf16[1024,2048]{1,0:T(8,128)(2,1)}, u32[]{:S(2)}) %copy-start) | copy-done | bytes 4194328
  81.8 6.7 %blend_table.1.refs_2_ = bf16[1024,2048]{1,0:T(8,128)(2,1)} custom-call(s32[8,3]{1,0:T(8,128)S(1)} %subtract_clamp_fusion.ids_ref, s32[8]{0:T(128)S(1)} %copy-done.3, s32[1]{0:T(128)} %bitcast.side_ref, bf16[8,3,128,128]{3,2,1,0:T(8,128)(2,1)S(1)} %copy-done.2, bf16[1024,2048]{1,0:T(8,128)(2,1)S(1)} %copy-done, ...), custom_call_target="tpu_custom_call" | custom-call | tf_op jit(solution)/shard_map/blend_table/pallas_call | solution.py:64
  88.5 6.8 %collective-permute-done.10.refs_3_ = bf16[1024,2048]{1,0:T(8,128)(2,1)} collective-permute-done((bf16[1024,2048]{1,0:T(8,128)(2,1)}, bf16[1024,2048]{1,0:T(8,128)(2,1)}, u32[]{:S(2)}, u32[]{:S(2)}) %collective-permute-start.10) | collective-permute-done | bytes 4194336 | tf_op jit(solution)/shard_map/ppermute | solution.py:276
  95.2 4.8 %collective-permute-done.5.refs_0_ = bf16[512,1024]{1,0:T(8,128)(2,1)} collective-permute-done((bf16[512,1024]{1,0:T(8,128)(2,1)}, bf16[512,1024]{1,0:T(8,128)(2,1)}, u32[]{:S(2)}, u32[]{:S(2)}) %collective-permute-start.5) | collective-permute-done | bytes 1048608 | tf_op jit(solution)/shard_map/ppermute | solution.py:322
  100.0 4.8 %collective-permute-start.12 = (bf16[512,1024]{1,0:T(8,128)(2,1)}, bf16[512,1024]{1,0:T(8,128)(2,1)S(1)}, u32[]{:S(2)}, u32[]{:S(2)}) collective-permute-start(bf16[512,1024]{1,0:T(8,128)(2,1)} %get-tuple-element.20.refs_8_.refs_9_), channel_id=1, source_target_pairs={{0,8},{8,16},{16,24},{24,28},{28,20},{20,12},{12,4},{4,0},{2,10},{... | collective-permute-start | bytes 3145736 | tf_op jit(solution)/shard_map/ppermute | solution.py:331
  104.8 1.6 %collective-permute-start.13 = (bf16[512,1024]{1,0:T(8,128)(2,1)}, bf16[512,1024]{1,0:T(8,128)(2,1)}, u32[]{:S(2)}, u32[]{:S(2)}) collective-permute-start(bf16[512,1024]{1,0:T(8,128)(2,1)} %get-tuple-element.21.refs_9_.refs_10_), channel_id=1, source_target_pairs={{9,1},{17,9},{25,17},{29,25},{21,29},{13,21},{5,13},{1,5},{11,3},{... | collective-permute-start | bytes 3145736 | tf_op jit(solution)/shard_map/ppermute | solution.py:332
  107.4 12.1 %early_product.1.refs_13_ = f32[1024,512]{1,0:T(8,128)} custom-call(s32[3,7]{1,0:T(4,128)} %bitcast.29, bf16[1024,2048]{1,0:T(8,128)(2,1)} %refs_0_.5, bf16[1024,2048]{1,0:T(8,128)(2,1)} %get-tuple-element.18.refs_1_, bf16[1024,2048]{1,0:T(8,128)(2,1)} %get-tuple-element.19.refs_2_, bf16[512,1024]{1,0:T(8,128)(2,1)} %refs_4_.3, ...), custom_call_target="tpu_custom_call" | custom-call | tf_op jit(solution)/shard_map/early_product/pallas_call | solution.py:195
  119.5 0.9 copy-done.5
  120.4 4.2 %last_product.2 = (bf16[256,512]{1,0:T(8,128)(2,1)S(1)}, bf16[256,512]{1,0:T(8,128)(2,1)S(1)}) custom-call(s32[3,9]{1,0:T(4,128)S(1)} %get-tuple-element.43.where_ref, bf16[1024,2048]{1,0:T(8,128)(2,1)} %refs_0_.5, bf16[1024,2048]{1,0:T(8,128)(2,1)} %get-tuple-element.18.refs_1_, bf16[1024,2048]{1,0:T(8,128)(2,1)} %get-tuple-element.19.refs_2_, ...), custom_call_target="tpu_custom_call" | custom-call | tf_op jit(solution)/shard_map/last_product/pallas_call | solution.py:195
  124.7 1.3 collective-permute-start.14
  126.0 1.3 collective-permute-start.15
  127.3 4.2 %last_product.3.refs_2_ = bf16[512,512]{1,0:T(8,128)(2,1)S(1)} custom-call(s32[3,9]{1,0:T(4,128)S(1)} %get-tuple-element.43.where_ref, bf16[1024,2048]{1,0:T(8,128)(2,1)} %refs_0_.5, bf16[1024,2048]{1,0:T(8,128)(2,1)} %get-tuple-element.18.refs_1_, bf16[1024,2048]{1,0:T(8,128)(2,1)} %get-tuple-element.19.refs_2_, ...), custom_call_target="tpu_custom_call" | custom-call | tf_op jit(solution)/shard_map/last_product/pallas_call | solution.py:195
  131.5 5.7 %collective-permute-done.14.refs_0_ = bf16[256,512]{1,0:T(8,128)(2,1)S(1)} collective-permute-done((bf16[256,512]{1,0:T(8,128)(2,1)S(1)}, bf16[256,512]{1,0:T(8,128)(2,1)S(1)}, u32[]{:S(2)}, u32[]{:S(2)}) %collective-permute-start.14) | collective-permute-done | bytes 262176 | tf_op jit(solution)/shard_map/ppermute | solution.py:233
  137.2 2.0 %blend_stats.1 = f32[3,512]{1,0:T(4,128)S(1)} custom-call(s32[8,3]{1,0:T(8,128)S(1)} %subtract_clamp_fusion.ids_ref, s32[8]{0:T(128)S(1)} %copy-done.3, bf16[8,3,128,128]{3,2,1,0:T(8,128)(2,1)S(1)} %copy-done.2, bf16[256,512]{1,0:T(8,128)(2,1)S(1)} %collective-permute-done.14.refs_0_, bf16[256,512]{1,0:T(8,128)(2,1)S(1)} %get-tuple-element.23.refs_1_, ...), custom_call_target="tpu_custom_call" | custom-call | flops 402653184 | bytes 1572864 | tf_op jit(solution)/shard_map/blend_stats/pallas_call | solution.py:111
  139.2 4.3 %collective-permute-start.16 = (f32[3,512]{1,0:T(4,128)S(1)}, f32[3,512]{1,0:T(4,128)S(1)}, u32[]{:S(2)}, u32[]{:S(2)}) collective-permute-start(f32[3,512]{1,0:T(4,128)S(1)} %blend_stats.1), channel_id=1, source_target_pairs={{0,12},{4,8},{8,4},{12,0},{16,28},{20,24},{24,20},{28,16},{1,13},{... | collective-permute-start | bytes 18440 | tf_op jit(solution)/shard_map/ppermute | solution.py:243
  143.5 1.2 collective-permute-start.18
  145.2 2.0 %collective-permute-done.17 = f32[3,512]{1,0:T(4,128)S(1)} collective-permute-done((f32[3,512]{1,0:T(4,128)S(1)}, f32[3,512]{1,0:T(4,128)S(1)}, u32[]{:S(2)}, u32[]{:S(2)}) %collective-permute-start.17) | collective-permute-done | bytes 6176 | tf_op jit(solution)/shard_map/ppermute | solution.py:243
  147.3 2.9 %collective-permute-start.19 = (f32[3,512]{1,0:T(4,128)S(1)}, f32[3,512]{1,0:T(4,128)S(1)}, u32[]{:S(2)}, u32[]{:S(2)}) collective-permute-start(f32[3,512]{1,0:T(4,128)S(1)} %pad_maximum_fusion), channel_id=1, source_target_pairs={{0,16},{4,20},{8,24},{12,28},{16,0},{20,4},{24,8},{28,12},{1,17},{... | collective-permute-start | bytes 18440 | tf_op jit(solution)/shard_map/ppermute | solution.py:243
  150.2 1.7 %collective-permute-done.19 = f32[3,512]{1,0:T(4,128)S(1)} collective-permute-done((f32[3,512]{1,0:T(4,128)S(1)}, f32[3,512]{1,0:T(4,128)S(1)}, u32[]{:S(2)}, u32[]{:S(2)}) %collective-permute-start.19) | collective-permute-done | bytes 6176 | tf_op jit(solution)/shard_map/ppermute | solution.py:243
  (52 shorter events, 4.1 us)
Async XLA Ops:
  0.6 30.0 %collective-permute-start.2 = (bf16[1024,2048]{1,0:T(8,128)(2,1)}, bf16[1024,2048]{1,0:T(8,128)(2,1)}, u32[]{:S(2)}, u32[]{:S(2)}) collective-permute-start(bf16[1024,2048]{1,0:T(8,128)(2,1)} %refs_0_.5), channel_id=1, source_target_pairs={{0,1},{1,0},{2,3},{3,2},{4,5},{5,4},{6,7},{7,6},{8,9},{9,8},{10,11... | collective-permute-start | bytes 12582920 | tf_op jit(solution)/shard_map/ppermute | solution.py:281
  1.1 94.1 %collective-permute-start.10 = (bf16[1024,2048]{1,0:T(8,128)(2,1)}, bf16[1024,2048]{1,0:T(8,128)(2,1)}, u32[]{:S(2)}, u32[]{:S(2)}) collective-permute-start(bf16[1024,2048]{1,0:T(8,128)(2,1)} %refs_0_.5), channel_id=1, source_target_pairs={{0,2},{1,3},{2,0},{3,1},{4,6},{5,7},{6,4},{7,5},{8,10},{9,11},{10,... | collective-permute-start | bytes 12582920 | tf_op jit(solution)/shard_map/ppermute | solution.py:276
  3.7 25.4 %collective-permute-start = (bf16[512,1024]{1,0:T(8,128)(2,1)}, bf16[512,1024]{1,0:T(8,128)(2,1)S(1)}, u32[]{:S(2)}, u32[]{:S(2)}) collective-permute-start(bf16[512,1024]{1,0:T(8,128)(2,1)} %refs_4_.3), channel_id=1, source_target_pairs={{0,8},{8,16},{16,24},{24,28},{28,20},{20,12},{12,4},{4,0},{1,9},{9... | collective-permute-start | bytes 3145736 | tf_op jit(solution)/shard_map/ppermute | solution.py:313
  5.3 25.3 %collective-permute-start.1 = (bf16[512,1024]{1,0:T(8,128)(2,1)}, bf16[512,1024]{1,0:T(8,128)(2,1)}, u32[]{:S(2)}, u32[]{:S(2)}) collective-permute-start(bf16[512,1024]{1,0:T(8,128)(2,1)} %refs_4_.3), channel_id=1, source_target_pairs={{8,0},{16,8},{24,16},{28,24},{20,28},{12,20},{4,12},{0,4},{9,1},{1... | collective-permute-start | bytes 3145736 | tf_op jit(solution)/shard_map/ppermute | solution.py:313
  8.4 24.3 %collective-permute-start.7 = (bf16[256,2048]{1,0:T(8,128)(2,1)}, bf16[256,2048]{1,0:T(8,128)(2,1)S(1)}, u32[]{:S(2)}, u32[]{:S(2)}) collective-permute-start(bf16[256,2048]{1,0:T(8,128)(2,1)} %broadcast_select_fusion.1), channel_id=1, source_target_pairs={{8,12},{12,8},{16,20},{20,16},{9,13},{13,9},{17,21},{21,17},{10,14... | collective-permute-start | bytes 3145736 | tf_op jit(solution)/shard_map/ppermute | solution.py:233
  29.2 1.4 copy-start.4
  30.6 29.7 %copy-start.6 = (s32[8,3]{0,1:T(4,128)S(1)}, s32[8,3]{0,1:T(4,128)}, u32[]{:S(2)}) copy-start(s32[8,3]{0,1:T(4,128)} %param.10) | copy-start | bytes 292
  30.6 49.0 %copy-start.2 = (bf16[8,3,128,128]{3,2,1,0:T(8,128)(2,1)S(1)}, bf16[8,3,128,128]{3,2,1,0:T(8,128)(2,1)}, u32[]{:S(2)}) copy-start(bf16[8,3,128,128]{3,2,1,0:T(8,128)(2,1)} %weights_ref.3) | copy-start | bytes 2359300
  30.6 49.0 %copy-start.3 = (s32[8]{0:T(128)S(1)}, s32[8]{0:T(128)}, u32[]{:S(2)}) copy-start(s32[8]{0:T(128)} %counts_ref.3) | copy-start | bytes 100
  30.6 26.5 %collective-permute-start.3 = (bf16[512,1024]{1,0:T(8,128)(2,1)}, bf16[512,1024]{1,0:T(8,128)(2,1)}, u32[]{:S(2)}, u32[]{:S(2)}) collective-permute-start(bf16[512,1024]{1,0:T(8,128)(2,1)} %get-tuple-element.13.refs_4_.refs_5_), channel_id=1, source_target_pairs={{0,8},{8,16},{16,24},{24,28},{28,20},{20,12},{12,4},{4,0},{1,9},{9... | collective-permute-start | bytes 3145736 | tf_op jit(solution)/shard_map/ppermute | solution.py:318
  32.3 24.8 %collective-permute-start.4 = (bf16[512,1024]{1,0:T(8,128)(2,1)}, bf16[512,1024]{1,0:T(8,128)(2,1)}, u32[]{:S(2)}, u32[]{:S(2)}) collective-permute-start(bf16[512,1024]{1,0:T(8,128)(2,1)} %get-tuple-element.14.refs_5_.refs_6_), channel_id=1, source_target_pairs={{8,0},{16,8},{24,16},{28,24},{20,28},{12,20},{4,12},{0,4},{9,1},{1... | collective-permute-start | bytes 3145736 | tf_op jit(solution)/shard_map/ppermute | solution.py:318
  35.9 43.2 %collective-permute-start.8 = (bf16[256,2048]{1,0:T(8,128)(2,1)}, bf16[256,2048]{1,0:T(8,128)(2,1)S(1)}, u32[]{:S(2)}, u32[]{:S(2)}) collective-permute-start(bf16[256,2048]{1,0:T(8,128)(2,1)} %get-tuple-element.29), channel_id=1, source_target_pairs={{0,4},{4,8},{8,12},{12,16},{16,24},{24,28},{1,5},{5,9},{9,13},{13,... | collective-permute-start | bytes 3145736 | tf_op jit(solution)/shard_map/ppermute | solution.py:233
  38.8 40.7 %collective-permute-start.9 = (bf16[256,2048]{1,0:T(8,128)(2,1)}, bf16[256,2048]{1,0:T(8,128)(2,1)}, u32[]{:S(2)}, u32[]{:S(2)}) collective-permute-start(bf16[256,2048]{1,0:T(8,128)(2,1)} %get-tuple-element.28), channel_id=1, source_target_pairs={{4,0},{12,4},{16,12},{20,16},{24,20},{28,24},{5,1},{13,5},{17,13},... | collective-permute-start | bytes 3145736 | tf_op jit(solution)/shard_map/ppermute | solution.py:233
  57.1 42.9 %collective-permute-start.5 = (bf16[512,1024]{1,0:T(8,128)(2,1)}, bf16[512,1024]{1,0:T(8,128)(2,1)}, u32[]{:S(2)}, u32[]{:S(2)}) collective-permute-start(bf16[512,1024]{1,0:T(8,128)(2,1)} %get-tuple-element.15.refs_6_.refs_7_), channel_id=1, source_target_pairs={{0,8},{8,16},{16,24},{24,28},{28,20},{20,12},{12,4},{4,0},{1,9},{9... | collective-permute-start | bytes 3145736 | tf_op jit(solution)/shard_map/ppermute | solution.py:322
  60.2 39.8 %collective-permute-start.6 = (bf16[512,1024]{1,0:T(8,128)(2,1)}, bf16[512,1024]{1,0:T(8,128)(2,1)}, u32[]{:S(2)}, u32[]{:S(2)}) collective-permute-start(bf16[512,1024]{1,0:T(8,128)(2,1)} %get-tuple-element.16.refs_7_.refs_8_), channel_id=1, source_target_pairs={{8,0},{16,8},{24,16},{28,24},{20,28},{12,20},{4,12},{0,4},{9,1},{1... | collective-permute-start | bytes 3145736 | tf_op jit(solution)/shard_map/ppermute | solution.py:322
  79.6 2.2 %copy-start = (bf16[1024,2048]{1,0:T(8,128)(2,1)S(1)}, bf16[1024,2048]{1,0:T(8,128)(2,1)}, u32[]{:S(2)}) copy-start(bf16[1024,2048]{1,0:T(8,128)(2,1)} %own_ref.1) | copy-start | bytes 12582916
  100.0 19.5 %collective-permute-start.11 = (bf16[1024,2048]{1,0:T(8,128)(2,1)}, bf16[1024,2048]{1,0:T(8,128)(2,1)}, u32[]{:S(2)}, u32[]{:S(2)}) collective-permute-start(bf16[1024,2048]{1,0:T(8,128)(2,1)} %get-tuple-element.19.refs_2_), channel_id=1, source_target_pairs={{0,1},{1,0},{2,3},{3,2},{4,5},{5,4},{6,7},{7,6},{8,9},{9,8},{10,11... | collective-permute-start | bytes 12582920 | tf_op jit(solution)/shard_map/ppermute | solution.py:281
  100.0 19.4 %collective-permute-start.12 = (bf16[512,1024]{1,0:T(8,128)(2,1)}, bf16[512,1024]{1,0:T(8,128)(2,1)S(1)}, u32[]{:S(2)}, u32[]{:S(2)}) collective-permute-start(bf16[512,1024]{1,0:T(8,128)(2,1)} %get-tuple-element.20.refs_8_.refs_9_), channel_id=1, source_target_pairs={{0,8},{8,16},{16,24},{24,28},{28,20},{20,12},{12,4},{4,0},{2,10},{... | collective-permute-start | bytes 3145736 | tf_op jit(solution)/shard_map/ppermute | solution.py:331
  104.8 14.6 %collective-permute-start.13 = (bf16[512,1024]{1,0:T(8,128)(2,1)}, bf16[512,1024]{1,0:T(8,128)(2,1)}, u32[]{:S(2)}, u32[]{:S(2)}) collective-permute-start(bf16[512,1024]{1,0:T(8,128)(2,1)} %get-tuple-element.21.refs_9_.refs_10_), channel_id=1, source_target_pairs={{9,1},{17,9},{25,17},{29,25},{21,29},{13,21},{5,13},{1,5},{11,3},{... | collective-permute-start | bytes 3145736 | tf_op jit(solution)/shard_map/ppermute | solution.py:332
  107.4 13.0 %copy-start.1 = (bf16[512,1024]{1,0:T(8,128)(2,1)S(1)}, bf16[512,1024]{1,0:T(8,128)(2,1)}, u32[]{:S(2)}) copy-start(bf16[512,1024]{1,0:T(8,128)(2,1)} %refs_4_.3) | copy-start | bytes 3145732
  119.5 1.0 copy-start.5
  120.4 6.9 %copy-start.8 = (s32[512]{0:T(512)S(1)}, s32[512]{0:T(512)}, u32[]{:S(2)}) copy-start(s32[512]{0:T(512)} %param.14) | copy-start | bytes 6148
  124.7 12.5 %collective-permute-start.14 = (bf16[256,512]{1,0:T(8,128)(2,1)S(1)}, bf16[256,512]{1,0:T(8,128)(2,1)S(1)}, u32[]{:S(2)}, u32[]{:S(2)}) collective-permute-start(bf16[256,512]{1,0:T(8,128)(2,1)S(1)} %get-tuple-element.22.refs_3_), channel_id=1, source_target_pairs={{0,4},{4,8},{8,12},{12,16},{16,20},{20,24},{24,28},{1,5},{5,9},{9,... | collective-permute-start | bytes 786440 | tf_op jit(solution)/shard_map/ppermute | solution.py:233
  126.0 11.2 %collective-permute-start.15 = (bf16[256,512]{1,0:T(8,128)(2,1)S(1)}, bf16[256,512]{1,0:T(8,128)(2,1)S(1)}, u32[]{:S(2)}, u32[]{:S(2)}) collective-permute-start(bf16[256,512]{1,0:T(8,128)(2,1)S(1)} %get-tuple-element.23.refs_1_), channel_id=1, source_target_pairs={{4,0},{8,4},{12,8},{16,12},{20,16},{24,20},{28,24},{5,1},{9,5},{13... | collective-permute-start | bytes 786440 | tf_op jit(solution)/shard_map/ppermute | solution.py:233
  127.3 24.6 %copy-start.7 = (s32[512]{0:T(512)S(1)}, s32[512]{0:T(512)}, u32[]{:S(2)}) copy-start(s32[512]{0:T(512)} %param.15) | copy-start | bytes 6148
  139.2 6.0 %collective-permute-start.16 = (f32[3,512]{1,0:T(4,128)S(1)}, f32[3,512]{1,0:T(4,128)S(1)}, u32[]{:S(2)}, u32[]{:S(2)}) collective-permute-start(f32[3,512]{1,0:T(4,128)S(1)} %blend_stats.1), channel_id=1, source_target_pairs={{0,12},{4,8},{8,4},{12,0},{16,28},{20,24},{24,20},{28,16},{1,13},{... | collective-permute-start | bytes 18440 | tf_op jit(solution)/shard_map/ppermute | solution.py:243
  143.5 3.7 %collective-permute-start.17 = (f32[3,512]{1,0:T(4,128)S(1)}, f32[3,512]{1,0:T(4,128)S(1)}, u32[]{:S(2)}, u32[]{:S(2)}) collective-permute-start(f32[3,512]{1,0:T(4,128)S(1)} %blend_stats.1), channel_id=1, source_target_pairs={{0,8},{4,12},{8,0},{12,4},{16,24},{20,28},{24,16},{28,20},{1,9},{5... | collective-permute-start | bytes 18440 | tf_op jit(solution)/shard_map/ppermute | solution.py:243
  143.5 3.7 %collective-permute-start.18 = (f32[3,512]{1,0:T(4,128)S(1)}, f32[3,512]{1,0:T(4,128)S(1)}, u32[]{:S(2)}, u32[]{:S(2)}) collective-permute-start(f32[3,512]{1,0:T(4,128)S(1)} %blend_stats.1), channel_id=1, source_target_pairs={{0,4},{4,0},{8,12},{12,8},{16,20},{20,16},{24,28},{28,24},{1,5},{5... | collective-permute-start | bytes 18440 | tf_op jit(solution)/shard_map/ppermute | solution.py:243
  147.3 4.6 %collective-permute-start.19 = (f32[3,512]{1,0:T(4,128)S(1)}, f32[3,512]{1,0:T(4,128)S(1)}, u32[]{:S(2)}, u32[]{:S(2)}) collective-permute-start(f32[3,512]{1,0:T(4,128)S(1)} %pad_maximum_fusion), channel_id=1, source_target_pairs={{0,16},{4,20},{8,24},{12,28},{16,0},{20,4},{24,8},{28,12},{1,17},{... | collective-permute-start | bytes 18440 | tf_op jit(solution)/shard_map/ppermute | solution.py:243

commit v5 on v4

--- a/solution.py
+++ b/solution.py
@@ -310,39 +310,44 @@
         up_pairs = [(0, 1), (1, 2), (2, 3), (3, 4), (4, 6), (6, 7)]
         down_pairs = [(1, 0), (3, 1), (4, 3), (5, 4), (6, 5), (7, 6)]
         side = jnp.where(vocab_index == 5, 1, jnp.where(vocab_index == 2, 2, 0))
-        a1, b1 = lax.ppermute(hidden, "vocab", ahead), lax.ppermute(hidden, "vocab", behind)
+        def by_parity(even_pairs, odd_pairs):
+            return [
+                (i * tok_count + t, j * tok_count + t)
+                for t in range(tok_count)
+                for i, j in (odd_pairs if t % 2 else even_pairs)
+            ]
+
+        send_a = lambda value: lax.ppermute(value, ("vocab", "tok"), by_parity(ahead, behind))
+        send_b = lambda value: lax.ppermute(value, ("vocab", "tok"), by_parity(behind, ahead))
+        way = 1 - 2 * (tok_index % 2)
+        a1, b1 = send_a(hidden), send_b(hidden)
         far_head = to_far(src_head)
         aside = shifted(jnp.where(vocab_index < 4, top_edge, bottom_edge), aside_pairs)
         near_head = spread({0: src_head})[1]
         a1, b1, near_head = fence(a1, b1, near_head)
-        a2, b2 = lax.ppermute(a1, "vocab", ahead), lax.ppermute(b1, "vocab", behind)
+        a2, b2 = send_a(a1), send_b(b1)
         table_before = shifted(jnp.where(vocab_index == 4, aside, bottom_edge), up_pairs)
         table_after = shifted(jnp.where(vocab_index == 3, aside, top_edge), down_pairs)
         a2, b2 = fence(a2, b2)
-        a3, b3 = lax.ppermute(a2, "vocab", ahead), lax.ppermute(b2, "vocab", behind)
+        a3, b3 = send_a(a2), send_b(b2)
         new_embed = blend_table(
             local_ids, slot_counts, slot_weights, src_embed, table_before, table_after, aside, side.reshape(1)
         )
         a3, b3, new_embed, far_head = fence(a3, b3, new_embed, far_head)
-        def some(pairs, parity):
-            return [(i * tok_count + t, j * tok_count + t) for t in range(parity, tok_count, 2) for i, j in pairs]
-
-        even = (tok_index % 2 == 0).astype(jnp.int32)
-        a4 = lax.ppermute(a3, ("vocab", "tok"), some(ahead, 0))
-        b4 = lax.ppermute(b3, ("vocab", "tok"), some(behind, 1))
+        a4 = send_a(a3)
         far_near_head = spread({far: far_head})[far | 1]
         pieces = [src_head, near_head, far_head, far_near_head]
         per = count // tok_count
-        offsets = [0, -1, 1, -2, 2, -3, 3, 4, 4]
-        origins = jnp.stack([origin(offset) for offset in offsets]).astype(jnp.int32)
+        offsets = [0, -1, 1, -2, 2, -3, 3, 4]
+        origins = jnp.stack([origin(way * offset) for offset in offsets]).astype(jnp.int32)
         piece_of = (origins // per) ^ tok_index
         late_piece = (piece_of == 3).astype(jnp.int32)
-        wanted = jnp.concatenate([late_piece[:7], jnp.stack([even, 1 - even])])
+        wanted = jnp.concatenate([late_piece[:7], jnp.ones((1,), jnp.int32)])
         early_where = jnp.stack([piece_of, origins % per, 1 - late_piece])[:, :7]
         late_where = jnp.stack([piece_of, origins % per, wanted])
         blocks = [hidden, a1, b1, a2, b2, a3, b3]
         (early,) = add_products(early_where, pieces[:3], blocks, [(0, rows)])
-        late = lambda bands: add_products(late_where, pieces, blocks + [a4, b4], bands, early)
+        late = lambda bands: add_products(late_where, pieces, blocks + [a4], bands, early)
         top_logits, bottom_logits = late([(0, halo), (rows - halo, halo)])
         (middle_logits,) = late([(halo, rows - 2 * halo)])
         source_logits = [top_logits, middle_logits, bottom_logits]

time: 153 us -> 153 us (level)
  starting transfers between devices: 32.8 us -> 25.6 us
  waiting for transfers between devices: 79 us -> 84.8 us
    ppermute x8 -> x7, starting transfers between devices: 13.7 us -> 7 us  [the longest x4 5.78 us: body(): lax.ppermute(value, ('vocab', 'tok'), by_parity(ahead, behind))]
    ppermute x4, starting transfers between devices: 8.45 us -> 5.46 us  [merge_stats(): lax.ppermute(stats, axis, xor_perm(count, low * mask))]
    ppermute x4, waiting for transfers between devices: 4.15 us -> 6.81 us  [merge_stats(): lax.ppermute(stats, axis, xor_perm(count, low * mask))]
    ppermute x5, starting transfers between devices: 7.55 us -> 10.1 us  [shifted(): return lax.ppermute(value, 'vocab', pairs)]
    ppermute x8 -> x7, waiting for transfers between devices: 43.2 us -> 45.5 us  [the longest x4 45.5 us: body(): lax.ppermute(value, ('vocab', 'tok'), by_parity(ahead, behind))]
  transfers between devices with their start and end apart: 20 -> 19, of which waited for: 11 -> 12; matrix products, arithmetic and copies ran while one was open for 4% -> 4% of each run, Pallas kernels for 15% -> 15%
where the time goes in v5:
time: 153 us; the launch traced here: 152 us
  waiting for transfers between devices  84.8 us (55%)
  Pallas kernels  29.1 us (19%)
  starting transfers between devices  25.6 us (17%)
  other arithmetic  7.17 us (5%)
  local copies, waits for them, and re-layouts  4.43 us (3%)
    ppermute x4, waiting for transfers between devices, body(): lax.ppermute(value, ('vocab', 'tok'), by_parity(ahead, behind))  45.5 us
    ppermute x5, waiting for transfers between devices, shifted(): return lax.ppermute(value, 'vocab', pairs)  25.6 us
    pallas_call x3, Pallas kernels, add_products(): pl.pallas_call(functools.partial(product_kernel, pieces=len(pieces), chun...  20.4 us
    ppermute x5, starting transfers between devices, shifted(): return lax.ppermute(value, 'vocab', pairs)  10.1 us
    ppermute x1, waiting for transfers between devices, to_far(): return lax.ppermute(value, 'tok', xor_perm(tok_count, far))  6.84 us
    ppermute x4, waiting for transfers between devices, merge_stats(): lax.ppermute(stats, axis, xor_perm(count, low * mask))  6.81 us
    pallas_call x1, Pallas kernels, blend_table(): pl.pallas_call(table_kernel, grid=(columns // tile,), out_shape=jax.Shape...  6.7 us
    ppermute x4, starting transfers between devices, body(): lax.ppermute(value, ('vocab', 'tok'), by_parity(ahead, behind))  5.78 us
  transfers between devices with their start and end apart: 19, of which 12 were waited for; matrix products, arithmetic and copies ran while one was open for 4% of the time, Pallas kernels for 15%

profile of v5, /device:TPU:0, one launch (start us, length us, event | category | flops | bytes accessed | tf_op | source)
XLA Modules:
  0.0 152.1 jit_solution(7420724655986863611)
XLA Ops:
  1.1 2.6 %collective-permute-start.10 = (bf16[1024,2048]{1,0:T(8,128)(2,1)}, bf16[1024,2048]{1,0:T(8,128)(2,1)}, u32[]{:S(2)}, u32[]{:S(2)}) collective-permute-start(bf16[1024,2048]{1,0:T(8,128)(2,1)} %refs_0_.5), channel_id=1, source_target_pairs={{0,2},{1,3},{2,0},{3,1},{4,6},{5,7},{6,4},{7,5},{8,10},{9,11},{10,... | collective-permute-start | bytes 12582920 | tf_op jit(solution)/shard_map/ppermute | solution.py:276
  3.7 1.6 %collective-permute-start = (bf16[512,1024]{1,0:T(8,128)(2,1)}, bf16[512,1024]{1,0:T(8,128)(2,1)S(1)}, u32[]{:S(2)}, u32[]{:S(2)}) collective-permute-start(bf16[512,1024]{1,0:T(8,128)(2,1)} %refs_4_.3), channel_id=1, source_target_pairs={{0,8},{8,16},{16,24},{24,28},{28,20},{20,12},{12,4},{4,0},{9,1},{1... | collective-permute-start | bytes 3145736 | tf_op jit(solution)/shard_map/ppermute | solution.py:320
  5.8 2.6 %broadcast_select_fusion.1 = bf16[256,2048]{1,0:T(8,128)(2,1)} fusion(pred[]{:T(512)S(6)} %lt.85, bf16[1024,2048]{1,0:T(8,128)(2,1)} %own_ref.1), kind=kLoop, calls=%fused_computation.1 | loop fusion | flops 524288 | bytes 3145729 | tf_op jit(solution)/shard_map/jit(_where)/select_n | solution.py:325
  9.1 20.6 %collective-permute-done.refs_0_ = bf16[512,1024]{1,0:T(8,128)(2,1)S(1)} collective-permute-done((bf16[512,1024]{1,0:T(8,128)(2,1)}, bf16[512,1024]{1,0:T(8,128)(2,1)S(1)}, u32[]{:S(2)}, u32[]{:S(2)}) %collective-permute-start) | collective-permute-done | bytes 1048608 | tf_op jit(solution)/shard_map/ppermute | solution.py:320
  29.7 1.0 copy-done.4
  30.7 1.3 collective-permute-start.3
  31.9 0.8 collective-permute-start.4
  32.7 3.2 %broadcast_select_fusion = (bf16[256,2048]{1,0:T(8,128)(2,1)}, bf16[256,2048]{1,0:T(8,128)(2,1)}) fusion(bf16[256,2048]{1,0:T(8,128)(2,1)S(1)} %collective-permute-done.7.relayed_ref, pred[]{:T(512)S(6)} %eq.88, bf16[1024,2048]{1,0:T(8,128)(2,1)} %own_ref.1, pred[]{:T(512)S(6)} %eq.87), kind=kLoop, calls=%fused_computation | loop fusion | flops 1048576 | bytes 5242882 | tf_op jit(solution)/shard_map/jit(_where)/select_n | solution.py:330
  35.9 3.3 %collective-permute-start.8 = (bf16[256,2048]{1,0:T(8,128)(2,1)}, bf16[256,2048]{1,0:T(8,128)(2,1)S(1)}, u32[]{:S(2)}, u32[]{:S(2)}) collective-permute-start(bf16[256,2048]{1,0:T(8,128)(2,1)} %get-tuple-element.29), channel_id=1, source_target_pairs={{0,4},{4,8},{8,12},{12,16},{16,24},{24,28},{1,5},{5,9},{9,13},{13,... | collective-permute-start | bytes 3145736 | tf_op jit(solution)/shard_map/ppermute | solution.py:233
  39.2 1.3 collective-permute-start.9
  40.5 16.5 %collective-permute-done.3.refs_0_ = bf16[512,1024]{1,0:T(8,128)(2,1)} collective-permute-done((bf16[512,1024]{1,0:T(8,128)(2,1)}, bf16[512,1024]{1,0:T(8,128)(2,1)}, u32[]{:S(2)}, u32[]{:S(2)}) %collective-permute-start.3) | collective-permute-done | bytes 1048608 | tf_op jit(solution)/shard_map/ppermute | solution.py:320
  57.0 2.9 %collective-permute-start.5 = (bf16[512,1024]{1,0:T(8,128)(2,1)}, bf16[512,1024]{1,0:T(8,128)(2,1)}, u32[]{:S(2)}, u32[]{:S(2)}) collective-permute-start(bf16[512,1024]{1,0:T(8,128)(2,1)} %get-tuple-element.15.refs_6_.refs_7_), channel_id=1, source_target_pairs={{0,8},{8,16},{16,24},{24,28},{28,20},{20,12},{12,4},{4,0},{9,1},{1... | collective-permute-start | bytes 3145736 | tf_op jit(solution)/shard_map/ppermute | solution.py:320
  60.0 19.1 %collective-permute-done.8.before_ref = bf16[256,2048]{1,0:T(8,128)(2,1)S(1)} collective-permute-done((bf16[256,2048]{1,0:T(8,128)(2,1)}, bf16[256,2048]{1,0:T(8,128)(2,1)S(1)}, u32[]{:S(2)}, u32[]{:S(2)}) %collective-permute-start.8) | collective-permute-done | bytes 1048608 | tf_op jit(solution)/shard_map/ppermute | solution.py:233
  79.5 2.2 %copy-done = bf16[1024,2048]{1,0:T(8,128)(2,1)S(1)} copy-done((bf16[1024,2048]{1,0:T(8,128)(2,1)S(1)}, bf16[1024,2048]{1,0:T(8,128)(2,1)}, u32[]{:S(2)}) %copy-start) | copy-done | bytes 4194328
  81.7 6.7 %blend_table.1.refs_2_ = bf16[1024,2048]{1,0:T(8,128)(2,1)} custom-call(s32[8,3]{1,0:T(8,128)S(1)} %subtract_clamp_fusion.ids_ref, s32[8]{0:T(128)S(1)} %copy-done.3, s32[1]{0:T(128)} %bitcast.side_ref, bf16[8,3,128,128]{3,2,1,0:T(8,128)(2,1)S(1)} %copy-done.2, bf16[1024,2048]{1,0:T(8,128)(2,1)S(1)} %copy-done, ...), custom_call_target="tpu_custom_call" | custom-call | tf_op jit(solution)/shard_map/blend_table/pallas_call | solution.py:64
  88.4 6.8 %collective-permute-done.10.refs_3_ = bf16[1024,2048]{1,0:T(8,128)(2,1)} collective-permute-done((bf16[1024,2048]{1,0:T(8,128)(2,1)}, bf16[1024,2048]{1,0:T(8,128)(2,1)}, u32[]{:S(2)}, u32[]{:S(2)}) %collective-permute-start.10) | collective-permute-done | bytes 4194336 | tf_op jit(solution)/shard_map/ppermute | solution.py:276
  95.2 6.6 %collective-permute-done.5.refs_0_ = bf16[512,1024]{1,0:T(8,128)(2,1)} collective-permute-done((bf16[512,1024]{1,0:T(8,128)(2,1)}, bf16[512,1024]{1,0:T(8,128)(2,1)}, u32[]{:S(2)}, u32[]{:S(2)}) %collective-permute-start.5) | collective-permute-done | bytes 1048608 | tf_op jit(solution)/shard_map/ppermute | solution.py:320
  103.0 12.1 %early_product.1.refs_12_ = f32[1024,512]{1,0:T(8,128)} custom-call(s32[3,7]{1,0:T(4,128)} %bitcast.28, bf16[1024,2048]{1,0:T(8,128)(2,1)} %refs_0_.5, bf16[1024,2048]{1,0:T(8,128)(2,1)} %get-tuple-element.18.refs_1_, bf16[1024,2048]{1,0:T(8,128)(2,1)} %get-tuple-element.19.refs_2_, bf16[512,1024]{1,0:T(8,128)(2,1)} %refs_4_.3, ...), custom_call_target="tpu_custom_call" | custom-call | tf_op jit(solution)/shard_map/early_product/pallas_call | solution.py:195
  115.1 1.8 %collective-permute-done.12.refs_11_ = bf16[512,1024]{1,0:T(8,128)(2,1)S(1)} collective-permute-done((bf16[512,1024]{1,0:T(8,128)(2,1)}, bf16[512,1024]{1,0:T(8,128)(2,1)S(1)}, u32[]{:S(2)}, u32[]{:S(2)}) %collective-permute-start.12) | collective-permute-done | bytes 1048608 | tf_op jit(solution)/shard_map/ppermute | solution.py:320
  116.9 1.0 copy-done.5
  117.9 4.2 %last_product.2 = (bf16[256,512]{1,0:T(8,128)(2,1)S(1)}, bf16[256,512]{1,0:T(8,128)(2,1)S(1)}) custom-call(s32[3,8]{1,0:T(4,128)S(1)} %get-tuple-element.43.where_ref, bf16[1024,2048]{1,0:T(8,128)(2,1)} %refs_0_.5, bf16[1024,2048]{1,0:T(8,128)(2,1)} %get-tuple-element.18.refs_1_, bf16[1024,2048]{1,0:T(8,128)(2,1)} %get-tuple-element.19.refs_2_, ...), custom_call_target="tpu_custom_call" | custom-call | tf_op jit(solution)/shard_map/last_product/pallas_call | solution.py:195
  122.1 3.4 %collective-permute-start.13 = (bf16[256,512]{1,0:T(8,128)(2,1)S(1)}, bf16[256,512]{1,0:T(8,128)(2,1)S(1)}, u32[]{:S(2)}, u32[]{:S(2)}) collective-permute-start(bf16[256,512]{1,0:T(8,128)(2,1)S(1)} %get-tuple-element.22.refs_3_), channel_id=1, source_target_pairs={{0,4},{4,8},{8,12},{12,16},{16,20},{20,24},{24,28},{1,5},{5,9},{9,... | collective-permute-start | bytes 786440 | tf_op jit(solution)/shard_map/ppermute | solution.py:233
  125.5 1.3 collective-permute-start.14
  126.8 4.2 %last_product.3.refs_2_ = bf16[512,512]{1,0:T(8,128)(2,1)S(1)} custom-call(s32[3,8]{1,0:T(4,128)S(1)} %get-tuple-element.43.where_ref, bf16[1024,2048]{1,0:T(8,128)(2,1)} %refs_0_.5, bf16[1024,2048]{1,0:T(8,128)(2,1)} %get-tuple-element.18.refs_1_, bf16[1024,2048]{1,0:T(8,128)(2,1)} %get-tuple-element.19.refs_2_, ...), custom_call_target="tpu_custom_call" | custom-call | tf_op jit(solution)/shard_map/last_product/pallas_call | solution.py:195
  131.0 6.1 %collective-permute-done.13.refs_0_ = bf16[256,512]{1,0:T(8,128)(2,1)S(1)} collective-permute-done((bf16[256,512]{1,0:T(8,128)(2,1)S(1)}, bf16[256,512]{1,0:T(8,128)(2,1)S(1)}, u32[]{:S(2)}, u32[]{:S(2)}) %collective-permute-start.13) | collective-permute-done | bytes 262176 | tf_op jit(solution)/shard_map/ppermute | solution.py:233
  137.1 2.0 %blend_stats.1 = f32[3,512]{1,0:T(4,128)S(1)} custom-call(s32[8,3]{1,0:T(8,128)S(1)} %subtract_clamp_fusion.ids_ref, s32[8]{0:T(128)S(1)} %copy-done.3, bf16[8,3,128,128]{3,2,1,0:T(8,128)(2,1)S(1)} %copy-done.2, bf16[256,512]{1,0:T(8,128)(2,1)S(1)} %collective-permute-done.13.refs_0_, bf16[256,512]{1,0:T(8,128)(2,1)S(1)} %get-tuple-element.23.refs_1_, ...), custom_call_target="tpu_custom_call" | custom-call | flops 402653184 | bytes 1572864 | tf_op jit(solution)/shard_map/blend_stats/pallas_call | solution.py:111
  139.1 1.8 %collective-permute-start.15 = (f32[3,512]{1,0:T(4,128)S(1)}, f32[3,512]{1,0:T(4,128)S(1)}, u32[]{:S(2)}, u32[]{:S(2)}) collective-permute-start(f32[3,512]{1,0:T(4,128)S(1)} %blend_stats.1), channel_id=1, source_target_pairs={{0,12},{4,8},{8,4},{12,0},{16,28},{20,24},{24,20},{28,16},{1,13},{... | collective-permute-start | bytes 18440 | tf_op jit(solution)/shard_map/ppermute | solution.py:243
  141.0 2.2 %collective-permute-start.16 = (f32[3,512]{1,0:T(4,128)S(1)}, f32[3,512]{1,0:T(4,128)S(1)}, u32[]{:S(2)}, u32[]{:S(2)}) collective-permute-start(f32[3,512]{1,0:T(4,128)S(1)} %blend_stats.1), channel_id=1, source_target_pairs={{0,8},{4,12},{8,0},{12,4},{16,24},{20,28},{24,16},{28,20},{1,9},{5... | collective-permute-start | bytes 18440 | tf_op jit(solution)/shard_map/ppermute | solution.py:243
  143.8 1.1 collective-permute-done.16
  144.9 1.9 %collective-permute-done.17 = f32[3,512]{1,0:T(4,128)S(1)} collective-permute-done((f32[3,512]{1,0:T(4,128)S(1)}, f32[3,512]{1,0:T(4,128)S(1)}, u32[]{:S(2)}, u32[]{:S(2)}) %collective-permute-start.17) | collective-permute-done | bytes 6176 | tf_op jit(solution)/shard_map/ppermute | solution.py:243
  146.9 1.5 collective-permute-start.18
  148.3 3.2 %collective-permute-done.18 = f32[3,512]{1,0:T(4,128)S(1)} collective-permute-done((f32[3,512]{1,0:T(4,128)S(1)}, f32[3,512]{1,0:T(4,128)S(1)}, u32[]{:S(2)}, u32[]{:S(2)}) %collective-permute-start.18) | collective-permute-done | bytes 6176 | tf_op jit(solution)/shard_map/ppermute | solution.py:243
  (49 shorter events, 4.4 us)
Async XLA Ops:
  0.6 29.0 %collective-permute-start.2 = (bf16[1024,2048]{1,0:T(8,128)(2,1)}, bf16[1024,2048]{1,0:T(8,128)(2,1)}, u32[]{:S(2)}, u32[]{:S(2)}) collective-permute-start(bf16[1024,2048]{1,0:T(8,128)(2,1)} %refs_0_.5), channel_id=1, source_target_pairs={{0,1},{1,0},{2,3},{3,2},{4,5},{5,4},{6,7},{7,6},{8,9},{9,8},{10,11... | collective-permute-start | bytes 12582920 | tf_op jit(solution)/shard_map/ppermute | solution.py:281
  1.1 94.1 %collective-permute-start.10 = (bf16[1024,2048]{1,0:T(8,128)(2,1)}, bf16[1024,2048]{1,0:T(8,128)(2,1)}, u32[]{:S(2)}, u32[]{:S(2)}) collective-permute-start(bf16[1024,2048]{1,0:T(8,128)(2,1)} %refs_0_.5), channel_id=1, source_target_pairs={{0,2},{1,3},{2,0},{3,1},{4,6},{5,7},{6,4},{7,5},{8,10},{9,11},{10,... | collective-permute-start | bytes 12582920 | tf_op jit(solution)/shard_map/ppermute | solution.py:276
  3.7 25.9 %collective-permute-start = (bf16[512,1024]{1,0:T(8,128)(2,1)}, bf16[512,1024]{1,0:T(8,128)(2,1)S(1)}, u32[]{:S(2)}, u32[]{:S(2)}) collective-permute-start(bf16[512,1024]{1,0:T(8,128)(2,1)} %refs_4_.3), channel_id=1, source_target_pairs={{0,8},{8,16},{16,24},{24,28},{28,20},{20,12},{12,4},{4,0},{9,1},{1... | collective-permute-start | bytes 3145736 | tf_op jit(solution)/shard_map/ppermute | solution.py:320
  5.3 24.4 %collective-permute-start.1 = (bf16[512,1024]{1,0:T(8,128)(2,1)}, bf16[512,1024]{1,0:T(8,128)(2,1)}, u32[]{:S(2)}, u32[]{:S(2)}) collective-permute-start(bf16[512,1024]{1,0:T(8,128)(2,1)} %refs_4_.3), channel_id=1, source_target_pairs={{8,0},{16,8},{24,16},{28,24},{20,28},{12,20},{4,12},{0,4},{1,9},{9... | collective-permute-start | bytes 3145736 | tf_op jit(solution)/shard_map/ppermute | solution.py:321
  8.4 24.3 %collective-permute-start.7 = (bf16[256,2048]{1,0:T(8,128)(2,1)}, bf16[256,2048]{1,0:T(8,128)(2,1)S(1)}, u32[]{:S(2)}, u32[]{:S(2)}) collective-permute-start(bf16[256,2048]{1,0:T(8,128)(2,1)} %broadcast_select_fusion.1), channel_id=1, source_target_pairs={{8,12},{12,8},{16,20},{20,16},{9,13},{13,9},{17,21},{21,17},{10,14... | collective-permute-start | bytes 3145736 | tf_op jit(solution)/shard_map/ppermute | solution.py:233
  29.7 1.0 copy-start.4
  30.6 29.3 %copy-start.6 = (s32[8,3]{0,1:T(4,128)S(1)}, s32[8,3]{0,1:T(4,128)}, u32[]{:S(2)}) copy-start(s32[8,3]{0,1:T(4,128)} %param.10) | copy-start | bytes 292
  30.7 48.8 %copy-start.2 = (bf16[8,3,128,128]{3,2,1,0:T(8,128)(2,1)S(1)}, bf16[8,3,128,128]{3,2,1,0:T(8,128)(2,1)}, u32[]{:S(2)}) copy-start(bf16[8,3,128,128]{3,2,1,0:T(8,128)(2,1)} %weights_ref.3) | copy-start | bytes 2359300
  30.7 48.8 %copy-start.3 = (s32[8]{0:T(128)S(1)}, s32[8]{0:T(128)}, u32[]{:S(2)}) copy-start(s32[8]{0:T(128)} %counts_ref.3) | copy-start | bytes 100
  30.7 26.4 %collective-permute-start.3 = (bf16[512,1024]{1,0:T(8,128)(2,1)}, bf16[512,1024]{1,0:T(8,128)(2,1)}, u32[]{:S(2)}, u32[]{:S(2)}) collective-permute-start(bf16[512,1024]{1,0:T(8,128)(2,1)} %get-tuple-element.13.refs_4_.refs_5_), channel_id=1, source_target_pairs={{0,8},{8,16},{16,24},{24,28},{28,20},{20,12},{12,4},{4,0},{9,1},{1... | collective-permute-start | bytes 3145736 | tf_op jit(solution)/shard_map/ppermute | solution.py:320
  31.9 25.1 %collective-permute-start.4 = (bf16[512,1024]{1,0:T(8,128)(2,1)}, bf16[512,1024]{1,0:T(8,128)(2,1)}, u32[]{:S(2)}, u32[]{:S(2)}) collective-permute-start(bf16[512,1024]{1,0:T(8,128)(2,1)} %get-tuple-element.14.refs_5_.refs_6_), channel_id=1, source_target_pairs={{8,0},{16,8},{24,16},{28,24},{20,28},{12,20},{4,12},{0,4},{1,9},{9... | collective-permute-start | bytes 3145736 | tf_op jit(solution)/shard_map/ppermute | solution.py:321
  35.9 43.2 %collective-permute-start.8 = (bf16[256,2048]{1,0:T(8,128)(2,1)}, bf16[256,2048]{1,0:T(8,128)(2,1)S(1)}, u32[]{:S(2)}, u32[]{:S(2)}) collective-permute-start(bf16[256,2048]{1,0:T(8,128)(2,1)} %get-tuple-element.29), channel_id=1, source_target_pairs={{0,4},{4,8},{8,12},{12,16},{16,24},{24,28},{1,5},{5,9},{9,13},{13,... | collective-permute-start | bytes 3145736 | tf_op jit(solution)/shard_map/ppermute | solution.py:233
  39.2 40.3 %collective-permute-start.9 = (bf16[256,2048]{1,0:T(8,128)(2,1)}, bf16[256,2048]{1,0:T(8,128)(2,1)}, u32[]{:S(2)}, u32[]{:S(2)}) collective-permute-start(bf16[256,2048]{1,0:T(8,128)(2,1)} %get-tuple-element.28), channel_id=1, source_target_pairs={{4,0},{12,4},{16,12},{20,16},{24,20},{28,24},{5,1},{13,5},{17,13},... | collective-permute-start | bytes 3145736 | tf_op jit(solution)/shard_map/ppermute | solution.py:233
  57.0 44.8 %collective-permute-start.5 = (bf16[512,1024]{1,0:T(8,128)(2,1)}, bf16[512,1024]{1,0:T(8,128)(2,1)}, u32[]{:S(2)}, u32[]{:S(2)}) collective-permute-start(bf16[512,1024]{1,0:T(8,128)(2,1)} %get-tuple-element.15.refs_6_.refs_7_), channel_id=1, source_target_pairs={{0,8},{8,16},{16,24},{24,28},{28,20},{20,12},{12,4},{4,0},{9,1},{1... | collective-permute-start | bytes 3145736 | tf_op jit(solution)/shard_map/ppermute | solution.py:320
  59.9 41.9 %collective-permute-start.6 = (bf16[512,1024]{1,0:T(8,128)(2,1)}, bf16[512,1024]{1,0:T(8,128)(2,1)}, u32[]{:S(2)}, u32[]{:S(2)}) collective-permute-start(bf16[512,1024]{1,0:T(8,128)(2,1)} %get-tuple-element.16.refs_7_.refs_8_), channel_id=1, source_target_pairs={{8,0},{16,8},{24,16},{28,24},{20,28},{12,20},{4,12},{0,4},{1,9},{9... | collective-permute-start | bytes 3145736 | tf_op jit(solution)/shard_map/ppermute | solution.py:321
  79.5 2.2 %copy-start = (bf16[1024,2048]{1,0:T(8,128)(2,1)S(1)}, bf16[1024,2048]{1,0:T(8,128)(2,1)}, u32[]{:S(2)}) copy-start(bf16[1024,2048]{1,0:T(8,128)(2,1)} %own_ref.1) | copy-start | bytes 12582916
  101.8 15.1 %collective-permute-start.11 = (bf16[1024,2048]{1,0:T(8,128)(2,1)}, bf16[1024,2048]{1,0:T(8,128)(2,1)}, u32[]{:S(2)}, u32[]{:S(2)}) collective-permute-start(bf16[1024,2048]{1,0:T(8,128)(2,1)} %get-tuple-element.19.refs_2_), channel_id=1, source_target_pairs={{0,1},{1,0},{2,3},{3,2},{4,5},{5,4},{6,7},{7,6},{8,9},{9,8},{10,11... | collective-permute-start | bytes 12582920 | tf_op jit(solution)/shard_map/ppermute | solution.py:281
  101.8 15.1 %collective-permute-start.12 = (bf16[512,1024]{1,0:T(8,128)(2,1)}, bf16[512,1024]{1,0:T(8,128)(2,1)S(1)}, u32[]{:S(2)}, u32[]{:S(2)}) collective-permute-start(bf16[512,1024]{1,0:T(8,128)(2,1)} %get-tuple-element.20.refs_8_.refs_9_), channel_id=1, source_target_pairs={{0,8},{8,16},{16,24},{24,28},{28,20},{20,12},{12,4},{4,0},{9,1},{1... | collective-permute-start | bytes 3145736 | tf_op jit(solution)/shard_map/ppermute | solution.py:320
  103.0 14.9 %copy-start.1 = (bf16[512,1024]{1,0:T(8,128)(2,1)S(1)}, bf16[512,1024]{1,0:T(8,128)(2,1)}, u32[]{:S(2)}) copy-start(bf16[512,1024]{1,0:T(8,128)(2,1)} %refs_4_.3) | copy-start | bytes 3145732
  116.9 1.0 copy-start.5
  117.9 8.9 %copy-start.8 = (s32[512]{0:T(512)S(1)}, s32[512]{0:T(512)}, u32[]{:S(2)}) copy-start(s32[512]{0:T(512)} %param.14) | copy-start | bytes 6148
  122.1 15.0 %collective-permute-start.13 = (bf16[256,512]{1,0:T(8,128)(2,1)S(1)}, bf16[256,512]{1,0:T(8,128)(2,1)S(1)}, u32[]{:S(2)}, u32[]{:S(2)}) collective-permute-start(bf16[256,512]{1,0:T(8,128)(2,1)S(1)} %get-tuple-element.22.refs_3_), channel_id=1, source_target_pairs={{0,4},{4,8},{8,12},{12,16},{16,20},{20,24},{24,28},{1,5},{5,9},{9,... | collective-permute-start | bytes 786440 | tf_op jit(solution)/shard_map/ppermute | solution.py:233
  125.5 11.6 %collective-permute-start.14 = (bf16[256,512]{1,0:T(8,128)(2,1)S(1)}, bf16[256,512]{1,0:T(8,128)(2,1)S(1)}, u32[]{:S(2)}, u32[]{:S(2)}) collective-permute-start(bf16[256,512]{1,0:T(8,128)(2,1)S(1)} %get-tuple-element.23.refs_1_), channel_id=1, source_target_pairs={{4,0},{8,4},{12,8},{16,12},{20,16},{24,20},{28,24},{5,1},{9,5},{13... | collective-permute-start | bytes 786440 | tf_op jit(solution)/shard_map/ppermute | solution.py:233
  126.8 24.7 %copy-start.7 = (s32[512]{0:T(512)S(1)}, s32[512]{0:T(512)}, u32[]{:S(2)}) copy-start(s32[512]{0:T(512)} %param.15) | copy-start | bytes 6148
  139.1 4.6 %collective-permute-start.15 = (f32[3,512]{1,0:T(4,128)S(1)}, f32[3,512]{1,0:T(4,128)S(1)}, u32[]{:S(2)}, u32[]{:S(2)}) collective-permute-start(f32[3,512]{1,0:T(4,128)S(1)} %blend_stats.1), channel_id=1, source_target_pairs={{0,12},{4,8},{8,4},{12,0},{16,28},{20,24},{24,20},{28,16},{1,13},{... | collective-permute-start | bytes 18440 | tf_op jit(solution)/shard_map/ppermute | solution.py:243
  141.0 3.9 %collective-permute-start.16 = (f32[3,512]{1,0:T(4,128)S(1)}, f32[3,512]{1,0:T(4,128)S(1)}, u32[]{:S(2)}, u32[]{:S(2)}) collective-permute-start(f32[3,512]{1,0:T(4,128)S(1)} %blend_stats.1), channel_id=1, source_target_pairs={{0,8},{4,12},{8,0},{12,4},{16,24},{20,28},{24,16},{28,20},{1,9},{5... | collective-permute-start | bytes 18440 | tf_op jit(solution)/shard_map/ppermute | solution.py:243
  143.2 3.7 %collective-permute-start.17 = (f32[3,512]{1,0:T(4,128)S(1)}, f32[3,512]{1,0:T(4,128)S(1)}, u32[]{:S(2)}, u32[]{:S(2)}) collective-permute-start(f32[3,512]{1,0:T(4,128)S(1)} %blend_stats.1), channel_id=1, source_target_pairs={{0,4},{4,0},{8,12},{12,8},{16,20},{20,16},{24,28},{28,24},{1,5},{5... | collective-permute-start | bytes 18440 | tf_op jit(solution)/shard_map/ppermute | solution.py:243
  146.9 4.6 %collective-permute-start.18 = (f32[3,512]{1,0:T(4,128)S(1)}, f32[3,512]{1,0:T(4,128)S(1)}, u32[]{:S(2)}, u32[]{:S(2)}) collective-permute-start(f32[3,512]{1,0:T(4,128)S(1)} %pad_maximum_fusion), channel_id=1, source_target_pairs={{0,16},{4,20},{8,24},{12,28},{16,0},{20,4},{24,8},{28,12},{1,17},{... | collective-permute-start | bytes 18440 | tf_op jit(solution)/shard_map/ppermute | solution.py:243
